TPU v7x, 128 devices: a whole 4x4x4 slice. The times are simulated.
128 devices in a mesh: vessel: 8 (over z, core), tissue: 16 (over y, x).
Axes of the slice: x: 4, y: 4, z: 4, core: 2. Of those that a mesh axis runs over, the one named last changes fastest.
Arguments:
- tissue_start: float32 [3, 32, 128, 128], P(None, 'vessel', 'tissue'), may hold values from 0 to 1
- consumption: float32 [3, 32, 128, 128], P(None, 'vessel', 'tissue'), may hold values from 0.002 to 0.05
- inlet: float32 [3, 512], P(None, ('vessel', 'tissue')), may hold values from 0.5 to 2
- flow: float32 [512, 256], P(('vessel', 'tissue')), may hold values from 0.3 to 30
- permeability: float32 [3], replicated, may hold values from 0.3 to 3
- intersection_count: int32 [512, 16], P(('vessel', 'tissue')), may hold values from 64 to 128, as said below
- intersection_segment: int32 [512, 16, 128], P(('vessel', 'tissue')), may hold values from 0 to 255
- intersection_voxel: int32 [512, 16, 128], P(('vessel', 'tissue')), may hold values from 0 to 4095
- intersection_weight: float32 [512, 16, 128], P(('vessel', 'tissue')), may hold values from 0.1 to 1
- upstream: int32 [512], P(('vessel', 'tissue')), may hold values from 0 to 511
Outputs:
- tissue_field: float32 [3, 32, 128, 128], P(None, 'vessel', 'tissue')
- vessel_field: float32 [3, 512, 256], P(None, ('vessel', 'tissue'))
Inputs may be any that keep to these rules, and one draw needn't show every extreme that they name: `intersection_count`: every block has all 128 slots live toward at least one tissue brick of its vessel part, at most 128 toward any, and at least 64 toward every other.
All inputs are finite; a program needn't handle non-finite values.
Results may differ from a plain program's by a relative error of at most 0.0001.
Values sent between devices are 32-bit elements; how exact they have to be, the bound alone decides.
No kernel may reach another device: no remote copies, remote signals or barrier semaphores. Data moves between devices by JAX's collectives and lax.ppermute only.
A program may use at most 128 MiB of HBM per device.

v0:
```python
import jax
import jax.numpy as jnp
from jax import lax
from jax.sharding import PartitionSpec as P

SEG = 256
OUTER = 2
SWEEPS = 4


DIFFUSION = (1.0, 0.7, 0.7)


def with_halo(value, sides, width):
    for axis, dim in sides:
        size, length = (lax.axis_size(axis), value.shape[dim])
        up = [(i, (i + 1) % size) for i in range(size - 1)]
        down = [(j, i) for i, j in up]
        last = lax.slice_in_dim(value, length - width, length, axis=dim)
        first = lax.slice_in_dim(value, 0, width, axis=dim)
        before = lax.ppermute(last, axis, up)
        after = lax.ppermute(first, axis, down)
        value = jnp.concatenate([before, value, after], axis=dim)
    return value


def combine(earlier, later):
    return (earlier[0] * later[0], later[0] * earlier[1] + later[1])


def relax_sweep(tissue, source, consumption):
    padded = with_halo(tissue, (("vessel", 1), ("tissue", 2)), 1)
    padded = jnp.pad(padded, ((0, 0), (0, 0), (0, 0), (1, 1)))
    neighbours = padded[:, 2:, 1:-1, 1:-1] + padded[:, :-2, 1:-1, 1:-1]
    neighbours = neighbours + padded[:, 1:-1, 2:, 1:-1] + padded[:, 1:-1, :-2, 1:-1]
    neighbours = neighbours + padded[:, 1:-1, 1:-1, 2:] + padded[:, 1:-1, 1:-1, :-2]
    rates = jnp.array(DIFFUSION, jnp.float32)[:, None, None, None]
    produced = jnp.zeros_like(tissue).at[2].set(2.0 * consumption[1] * tissue[1])
    return (source + produced + rates * neighbours) / (6.0 * rates + consumption)


def solve_blocks(arranged, flat_weight, flat_segment, flow, inflow_rows, permeability):

    def solve_block(block_items):
        slot_values, weight, segment, speed, inflow_row = block_items
        onehot = (segment[:, None] == jnp.arange(SEG)[None, :]).astype(jnp.float32)
        weight_sum = jnp.dot(weight, onehot, precision=lax.Precision.HIGHEST)
        gathered = jnp.dot(slot_values * weight[None, :], onehot, precision=lax.Precision.HIGHEST)
        denominator = speed[None, :] + permeability[:, None] * weight_sum[None, :]
        decay_rate = speed[None, :] / denominator
        drive_term = permeability[:, None] * gathered / denominator
        drive_term = drive_term.at[:, 0].add(decay_rate[:, 0] * inflow_row)
        _, vessel = lax.associative_scan(combine, (decay_rate, drive_term), axis=1)
        at_slot = jnp.dot(vessel, onehot.T, precision=lax.Precision.HIGHEST)
        slot_flux = permeability[:, None] * weight[None, :] * (at_slot - slot_values)
        return (vessel, slot_flux)

    return lax.map(solve_block, (arranged, flat_weight, flat_segment, flow, inflow_rows))


def shards(
    tissue_start,
    consumption,
    inlet,
    flow,
    permeability,
    intersection_count,
    intersection_segment,
    intersection_voxel,
    intersection_weight,
    upstream,
):
    blocks_here, columns, slots = intersection_voxel.shape
    species, depth, rows_here, width = tissue_start.shape
    voxels = depth * rows_here * width
    live_slot = jnp.arange(slots)[None, None, :] < intersection_count[:, :, None]
    weight = jnp.where(live_slot, intersection_weight, 0.0)
    flat_weight = weight.reshape(blocks_here, -1)
    flat_segment = intersection_segment.reshape(blocks_here, -1)
    full_rows = rows_here * columns
    column = jnp.arange(columns)[None, :, None]
    region_index = (
        intersection_voxel // (rows_here * width) * full_rows
        + column * rows_here
        + intersection_voxel // width % rows_here
    ) * width + intersection_voxel % width
    region_index = region_index.reshape(-1)
    tissue = tissue_start
    inflow_rows = inlet.T
    vessel = jnp.zeros((blocks_here, species, SEG), jnp.float32)
    for outer_step in range(OUTER):
        region = lax.all_gather(tissue, "tissue", axis=2, tiled=True).reshape(species, -1)
        slot_values = region[:, region_index].reshape(species, blocks_here, columns, slots)
        arranged = jnp.swapaxes(slot_values, 0, 1).reshape(blocks_here, species, -1)
        vessel, slot_flux = solve_blocks(
            arranged, flat_weight, flat_segment, flow, inflow_rows, permeability
        )
        gathered_ends = lax.all_gather(
            vessel[:, :, SEG - 1], ("vessel", "tissue"), axis=0, tiled=True
        )
        inflow_rows = 0.5 * (inlet.T + gathered_ends[upstream])
        flux_grid = jnp.swapaxes(slot_flux.reshape(blocks_here, species, columns, slots), 0, 1)
        partial_source = jax.vmap(
            lambda species_row: jax.ops.segment_sum(species_row, region_index, voxels * columns)
        )(flux_grid.reshape(species, -1))
        source = lax.psum_scatter(
            partial_source.reshape(species, depth, full_rows, width),
            "tissue",
            scatter_dimension=2,
            tiled=True,
        )
        for sweep_step in range(SWEEPS):
            tissue = relax_sweep(tissue, source, consumption)
    return (tissue, jnp.swapaxes(vessel, 0, 1))


def solution(mesh):
    return jax.shard_map(
        shards,
        mesh=mesh,
        in_specs=(
            P(None, "vessel", "tissue", None),
            P(None, "vessel", "tissue", None),
            P(None, ("vessel", "tissue")),
            P(("vessel", "tissue"), None),
            P(),
            P(("vessel", "tissue"), None),
            P(("vessel", "tissue"), None, None),
            P(("vessel", "tissue"), None, None),
            P(("vessel", "tissue"), None, None),
            P(("vessel", "tissue")),
        ),
        out_specs=(P(None, "vessel", "tissue", None), P(None, ("vessel", "tissue"), None)),
        check_vma=False,
    )
```

profile of v0, /device:TPU:1, one launch (start us, length us, event | category | flops | bytes accessed | tf_op | source)
XLA Modules:
  0.0 745.9 jit_solution(14316864906050526464)
XLA Ops:
  7.2 21.8 %all_gather.9 = f32[3,4,128,128]{3,2,1,0:T(8,128)S(1)} all-gather(f32[3,4,8,128]{3,2,1,0:T(8,128)} %param.42), channel_id=1, replica_groups=mesh['vessel'=8,'tissue'=16] {'tissue'}, dimensions={2}, use_global_device_ids=true | all-gather | bytes 835584 | tf_op jit(solution)/shard_map/all_gather | solution.py:92
  29.1 16.6 %copy.52 = f32[3,4,128,128]{0,3,2,1:T(8,128)} copy(f32[3,4,128,128]{3,2,1,0:T(8,128)S(1)} %all_gather.9) | data formatting | bytes 1572864 | tf_op jit(solution)/shard_map/all_gather | solution.py:92
  45.9 38.3 %gather_fusion = f32[8192,3]{1,0:T(8,128)} fusion(f32[3,65536]{0,1:T(8,128)} %bitcast.162, s32[8192]{0:T(1024)S(1)} %broadcast_clamp_fusion), kind=kCustom, calls=%fused_computation | custom fusion | bytes 229376 | tf_op jit(solution)/shard_map/gather | solution.py:93
  84.1 2.8 copy.53
  87.3 48.8 %while.38 = (s32[]{:T(128)}, f32[4,3,256]{2,1,0:T(4,128)S(1)}, f32[4,3,2048]{2,1,0:T(4,128)S(1)}, f32[3]{0:T(128)S(1)}, f32[4,3,2048]{2,0,1:T(4,128)S(1)}, /*ind...) while((s32[]{:T(128)}, f32[4,3,256]{2,1,0:T(4,128)S(1)}, ...), condition=%wide.region_2.3_spmd, body=%wide.region_0.2_spmd.sunk | while | flops 45649856 | bytes 347579 | solution.py:58
  136.3 2.7 copy.68
  139.0 57.5 %scatter_custom_fusion = f32[3,65536]{0,1:T(8,128)} fusion(s32[8192]{0:T(1024)S(1)} %bitcast.196, f32[8192,3]{1,0:T(8,128)} %bitcast.167, f32[]{:T(128)} %constant.353.clone.1), kind=kCustom, calls=%fused_computation.111 | custom fusion | flops 24576 | bytes 786944 | tf_op jit(solution)/shard_map/vmap()/scatter-add | solution.py:104
  196.5 20.3 %copy.58 = f32[3,4,128,128]{3,2,1,0:T(8,128)} copy(f32[3,4,128,128]{0,3,2,1:T(8,128)} %bitcast.161) | data formatting | bytes 1572864 | tf_op jit(solution)/shard_map/reshape | solution.py:107
  216.9 9.3 %collective-permute-start.1 = (f32[3,1,8,128]{3,2,1,0:T(8,128)S(1)}, f32[3,1,8,128]{3,2,1,0:T(8,128)S(1)}, u32[]{:S(2)}, u32[]{:S(2)}) collective-permute-start(f32[3,1,8,128]{3,2,1,0:T(8,128)S(1)} %get-tuple-element.493), channel_id=1, source_target_pairs={{0,16},{16,32},{32,48},{48,64},{64,80},{80,96},{96,112},{1,17},{17... | collective-permute-start | bytes 36872 | tf_op jit(solution)/shard_map/ppermute | solution.py:21
  226.2 1.9 collective-permute-start
  228.2 3.0 collective-permute-done
  231.2 1.3 collective-permute-start.2
  232.5 4.0 collective-permute-start.3
  237.5 55.3 %reduce-scatter.3.cloned.1.call-done = f32[3,4,8,128]{3,2,1,0:T(8,128)} async-done(((f32[3,4,128,128]{3,2,1,0:T(8,128)}), f32[3,4,8,128]{3,2,1,0:T(8,128)}) %reduce-scatter.3.cloned.1.call-update) | async-done | bytes 49168 | tf_op jit(solution)/shard_map/reduce_scatter | solution.py:106
  295.2 1.3 add_dynamic-update-slice_fusion
  297.4 4.2 collective-permute-start.4
  301.7 3.1 collective-permute-start.5
  306.9 4.0 collective-permute-start.7
  312.0 2.4 collective-permute-start.8
  314.4 4.9 collective-permute-start.9
  319.5 61.1 %all-gather = f32[512,3,1]{1,2,0:T(1,128)S(1)} all-gather(f32[4,3,1]{1,2,0:T(1,128)S(1)} %slice.1438), channel_id=2, replica_groups=mesh['vessel'=8,'tissue'=16] {'vessel','tissue'}, dimensions={0}, use_global_device_ids=true | all-gather | bytes 6192 | tf_op jit(solution)/shard_map/all_gather | solution.py:98
  382.6 4.0 collective-permute-start.11
  387.7 5.0 collective-permute-start.12
  392.7 1.9 collective-permute-start.13
  397.0 4.5 collective-permute-start.15
  402.7 24.9 %all_gather.10 = f32[3,4,128,128]{3,2,1,0:T(8,128)S(1)} all-gather(f32[3,4,8,128]{3,2,1,0:T(8,128)S(1)} %fusion.65), channel_id=1, replica_groups=mesh['vessel'=8,'tissue'=16] {'tissue'}, dimensions={2}, use_global_device_ids=true | all-gather | bytes 835584 | tf_op jit(solution)/shard_map/all_gather | solution.py:92
  427.6 16.6 %copy.59 = f32[3,4,128,128]{0,3,2,1:T(8,128)} copy(f32[3,4,128,128]{3,2,1,0:T(8,128)S(1)} %all_gather.10) | data formatting | bytes 1572864 | tf_op jit(solution)/shard_map/all_gather | solution.py:92
  444.2 38.3 %gather_fusion.1 = f32[8192,3]{1,0:T(8,128)} fusion(f32[3,65536]{0,1:T(8,128)} %bitcast.163, s32[8192]{0:T(1024)S(1)} %broadcast_clamp_fusion), kind=kCustom, calls=%fused_computation.1 | custom fusion | bytes 229376 | tf_op jit(solution)/shard_map/gather | solution.py:93
  482.4 2.8 copy.60
  485.4 49.1 %while.39 = (s32[]{:T(128)}, f32[4,3,256]{2,0,1:T(4,128)S(1)}, f32[4,3,2048]{2,1,0:T(4,128)S(1)}, f32[3]{0:T(128)S(1)}, f32[4,3,2048]{2,0,1:T(4,128)S(1)}, /*ind...) while((s32[]{:T(128)}, f32[4,3,256]{2,0,1:T(4,128)S(1)}, ...), condition=%wide.region_7.8_spmd, body=%wide.region_5.7_spmd.sunk | while | flops 45649856 | bytes 356795 | solution.py:58
  534.6 2.7 copy.70
  537.3 57.5 %scatter_custom_fusion.1 = f32[3,65536]{0,1:T(8,128)} fusion(s32[8192]{0:T(1024)S(1)} %bitcast.197, f32[8192,3]{1,0:T(8,128)} %bitcast.166, f32[]{:T(128)} %constant.353.clone.1), kind=kCustom, calls=%fused_computation.109 | custom fusion | flops 24576 | bytes 786944 | tf_op jit(solution)/shard_map/vmap()/scatter-add | solution.py:104
  594.8 20.2 %copy.65 = f32[3,4,128,128]{3,2,1,0:T(8,128)} copy(f32[3,4,128,128]{0,3,2,1:T(8,128)} %bitcast.160) | data formatting | bytes 1572864 | tf_op jit(solution)/shard_map/reshape | solution.py:107
  615.0 8.9 %collective-permute-start.16 = (f32[3,1,8,128]{3,2,1,0:T(8,128)S(1)}, f32[3,1,8,128]{3,2,1,0:T(8,128)S(1)}, u32[]{:S(2)}, u32[]{:S(2)}) collective-permute-start(f32[3,1,8,128]{3,2,1,0:T(8,128)S(1)} %get-tuple-element.485), channel_id=1, source_target_pairs={{16,0},{32,16},{48,32},{64,48},{80,64},{96,80},{112,96},{17,1},{33... | collective-permute-start | bytes 36872 | tf_op jit(solution)/shard_map/ppermute | solution.py:22
  624.0 3.0 collective-permute-start.17
  629.1 4.0 collective-permute-start.19
  634.1 55.3 %reduce-scatter.5.cloned.1.call-done = f32[3,4,8,128]{3,2,1,0:T(8,128)} async-done(((f32[3,4,128,128]{3,2,1,0:T(8,128)}), f32[3,4,8,128]{3,2,1,0:T(8,128)}) %reduce-scatter.5.cloned.1.call-update) | async-done | bytes 49168 | tf_op jit(solution)/shard_map/reduce_scatter | solution.py:106
  691.9 1.3 fusion.103
  694.1 4.2 collective-permute-start.20
  698.3 3.1 collective-permute-start.21
  703.5 4.0 collective-permute-start.23
  708.6 2.4 collective-permute-start.24
  711.0 4.9 collective-permute-start.25
  716.7 1.3 collective-permute-start.26
  718.0 4.5 collective-permute-start.27
  723.7 1.9 collective-permute-start.28
  725.6 5.1 collective-permute-start.29
  732.8 4.5 collective-permute-start.31
  (920 shorter events, 126.3 us)
Async XLA Ops:
  7.2 285.6 %reduce-scatter.3.cloned.1.call-start = ((), (), s32[]{:S(2)}) async-start(), calls=%async_computation.2 | async-start | bytes 835584 | tf_op jit(solution)/shard_map/reduce_scatter | solution.py:106
  29.1 16.6 %copy-start.5 = (s32[4,16,128]{2,1,0:T(8,128)S(1)}, s32[4,16,128]{2,1,0:T(8,128)}, u32[]{:S(2)}) copy-start(s32[4,16,128]{2,1,0:T(8,128)} %param.49) | copy-start | bytes 98308
  45.7 41.3 %copy-start.6 = (f32[4,16,128]{2,1,0:T(8,128)S(1)}, f32[4,16,128]{2,1,0:T(8,128)}, u32[]{:S(2)}) copy-start(f32[4,16,128]{2,1,0:T(8,128)} %param.50) | copy-start | bytes 98308
  45.7 41.3 %copy-start.9 = (s32[4,16]{1,0:T(4,128)S(1)}, s32[4,16]{1,0:T(4,128)}, u32[]{:S(2)}) copy-start(s32[4,16]{1,0:T(4,128)} %param.47) | copy-start | bytes 772
  45.7 41.5 %copy-start.7 = (s32[4,16,128]{2,1,0:T(8,128)S(1)}, s32[4,16,128]{2,1,0:T(8,128)}, u32[]{:S(2)}) copy-start(s32[4,16,128]{2,1,0:T(8,128)} %param.48) | copy-start | bytes 98308
  45.7 41.5 %copy-start.10 = (f32[3,4]{1,0:T(4,128)S(1)}, f32[3,4]{1,0:T(4,128)}, u32[]{:S(2)}) copy-start(f32[3,4]{1,0:T(4,128)} %param.44) | copy-start | bytes 148
  45.7 41.6 %copy-start.2 = (f32[3]{0:T(128)S(1)}, f32[3]{0:T(128)}, u32[]{:S(2)}) copy-start(f32[3]{0:T(128)} %param.46) | copy-start | bytes 40
  45.7 41.6 %copy-start.8 = (f32[4,256]{1,0:T(4,128)S(1)}, f32[4,256]{1,0:T(4,128)}, u32[]{:S(2)}) copy-start(f32[4,256]{1,0:T(4,128)} %param.45) | copy-start | bytes 12292
  196.5 20.4 %copy-start.1 = (f32[3,4,8,128]{3,2,1,0:T(8,128)S(1)}, f32[3,4,8,128]{3,2,1,0:T(8,128)}, u32[]{:S(2)}) copy-start(f32[3,4,8,128]{3,2,1,0:T(8,128)} %param.42) | copy-start | bytes 147460
  196.5 98.7 %copy-start = (f32[3,4,8,128]{3,2,1,0:T(8,128)S(1)}, f32[3,4,8,128]{3,2,1,0:T(8,128)}, u32[]{:S(2)}) copy-start(f32[3,4,8,128]{3,2,1,0:T(8,128)} %param.43) | copy-start | bytes 147460
  196.5 100.1 %copy-start.3 = (f32[3]{0:T(128)S(1)}, f32[3]{0:T(128)}, u32[]{:S(2)}) copy-start(f32[3]{0:T(128)} %constant.459) | copy-start | bytes 40
  196.5 100.1 %copy-start.4 = (f32[3]{0:T(128)S(1)}, f32[3]{0:T(128)}, u32[]{:S(2)}) copy-start(f32[3]{0:T(128)} %constant.369.clone) | copy-start | bytes 40
  196.5 108.3 %copy-start.12 = (s32[4]{0:T(128)S(1)}, s32[4]{0:T(128)}, u32[]{:S(2)}) copy-start(s32[4]{0:T(128)} %param.51) | copy-start | bytes 52
  216.8 472.7 %reduce-scatter.5.cloned.1.call-start = ((), (), s32[]{:S(2)}) async-start(), calls=%async_computation.3 | async-start | bytes 835584 | tf_op jit(solution)/shard_map/reduce_scatter | solution.py:106
  216.9 11.3 %collective-permute-start.1 = (f32[3,1,8,128]{3,2,1,0:T(8,128)S(1)}, f32[3,1,8,128]{3,2,1,0:T(8,128)S(1)}, u32[]{:S(2)}, u32[]{:S(2)}) collective-permute-start(f32[3,1,8,128]{3,2,1,0:T(8,128)S(1)} %get-tuple-element.493), channel_id=1, source_target_pairs={{0,16},{16,32},{32,48},{48,64},{64,80},{80,96},{96,112},{1,17},{17... | collective-permute-start | bytes 36872 | tf_op jit(solution)/shard_map/ppermute | solution.py:21
  226.2 5.0 collective-permute-start
  231.2 5.3 collective-permute-start.2
  232.5 4.8 collective-permute-start.3
  297.4 7.3 collective-permute-start.4
  301.7 3.9 collective-permute-start.5
  305.6 5.3 collective-permute-start.6
  306.9 4.8 collective-permute-start.7
  312.0 69.2 %collective-permute-start.8 = (f32[3,1,8,128]{3,2,1,0:T(8,128)S(1)}, f32[3,1,8,128]{3,2,1,0:T(8,128)S(1)}, u32[]{:S(2)}, u32[]{:S(2)}) collective-permute-start(f32[3,1,8,128]{3,2,1,0:T(8,128)S(1)} %get-tuple-element.489), channel_id=1, source_target_pairs={{16,0},{32,16},{48,32},{64,48},{80,64},{96,80},{112,96},{17,1},{33... | collective-permute-start | bytes 36872 | tf_op jit(solution)/shard_map/ppermute | solution.py:22
  314.4 66.8 %collective-permute-start.9 = (f32[3,1,8,128]{3,2,1,0:T(8,128)S(1)}, f32[3,1,8,128]{3,2,1,0:T(8,128)S(1)}, u32[]{:S(2)}, u32[]{:S(2)}) collective-permute-start(f32[3,1,8,128]{3,2,1,0:T(8,128)S(1)} %get-tuple-element.488), channel_id=1, source_target_pairs={{0,16},{16,32},{32,48},{48,64},{64,80},{80,96},{96,112},{1,17},{17... | collective-permute-start | bytes 36872 | tf_op jit(solution)/shard_map/ppermute | solution.py:21
  381.3 5.3 collective-permute-start.10
  382.6 4.8 collective-permute-start.11
  387.7 6.9 collective-permute-start.12
  392.7 3.1 collective-permute-start.13
  395.7 5.9 collective-permute-start.14
  397.0 5.3 collective-permute-start.15
  534.5 60.3 %copy-start.11 = (f32[4,3,256]{2,0,1:T(4,128)}, f32[4,3,256]{2,0,1:T(4,128)S(1)}, u32[]{:S(2)}) copy-start(f32[4,3,256]{2,0,1:T(4,128)S(1)} %get-tuple-element.353) | copy-start | bytes 36868
  615.0 12.0 %collective-permute-start.16 = (f32[3,1,8,128]{3,2,1,0:T(8,128)S(1)}, f32[3,1,8,128]{3,2,1,0:T(8,128)S(1)}, u32[]{:S(2)}, u32[]{:S(2)}) collective-permute-start(f32[3,1,8,128]{3,2,1,0:T(8,128)S(1)} %get-tuple-element.485), channel_id=1, source_target_pairs={{16,0},{32,16},{48,32},{64,48},{80,64},{96,80},{112,96},{17,1},{33... | collective-permute-start | bytes 36872 | tf_op jit(solution)/shard_map/ppermute | solution.py:22
  624.0 3.8 collective-permute-start.17
  627.8 5.3 collective-permute-start.18
  629.1 4.8 collective-permute-start.19
  694.1 7.3 collective-permute-start.20
  698.3 3.9 collective-permute-start.21
  702.2 5.3 collective-permute-start.22
  703.5 4.8 collective-permute-start.23
  708.6 7.3 collective-permute-start.24
  711.0 5.7 collective-permute-start.25
  716.7 5.9 collective-permute-start.26
  718.0 5.3 collective-permute-start.27
  723.7 7.0 collective-permute-start.28
  725.6 5.9 collective-permute-start.29
  731.5 5.9 collective-permute-start.30
  732.8 5.3 collective-permute-start.31
Sparse Core Ops, SparseCore 0:
  216.9 75.8 reduce-scatter.2
  615.1 74.2 reduce-scatter.4
where the time goes:
time: 757 us; the launch traced here: 746 us
  local copies, waits for them, and re-layouts  224 us (30%)
  other arithmetic  141 us (19%)
  waiting for transfers between devices  125 us (17%)
  starting transfers between devices  110 us (15%)
  blocking collectives  108 us (14%)
  matrix products  21.3 us (3%)
  between operations  14.9 us (2%)
    scatter-add x2, other arithmetic, shards(): jax.ops.segment_sum(species_row, region_index, voxels * columns)  115 us
    reduce_scatter x2, waiting for transfers between devices, shards(): lax.psum_scatter(partial_source.reshape(species, depth, full_rows, width)...  111 us
    gather x2, local copies, waits for them, and re-layouts, shards(): region[:, region_index].reshape(species, blocks_here, columns, slots)  76.5 us
    ppermute x16, starting transfers between devices, with_halo(): before = lax.ppermute(last, axis, up)  68.8 us
    all_gather x1, blocking collectives, shards(): lax.all_gather(vessel[:, :, SEG - 1], ('vessel', 'tissue'), axis=0, tiled...  61.1 us
    all_gather x2, blocking collectives, shards(): lax.all_gather(tissue, 'tissue', axis=2, tiled=True).reshape(species, -1)  46.7 us
    slice x320, local copies, waits for them, and re-layouts, solve_block(): _, vessel = lax.associative_scan(combine, (decay_rate, drive_term), axis=1)  41.6 us
    ppermute x16, starting transfers between devices, with_halo(): after = lax.ppermute(first, axis, down)  41.3 us
  transfers between devices with their start and end apart: 34, of which 17 were waited for; matrix products, arithmetic and copies ran while one was open for 0% of the time, Pallas kernels for 0%

commit v1 on v0

v1 whole, which is shorter than its diff:
```python
import jax
import jax.numpy as jnp
from jax import lax
from jax.experimental import pallas as pl
from jax.experimental.pallas import tpu as pltpu
from jax.sharding import PartitionSpec as P


SEG = 256
SWEEPS = 4
DIFFUSION = (1.0, 0.7, 0.7)
BRICKS = 16
PARTS = 8
F32 = jnp.float32
BF16 = jnp.bfloat16
VMEM_LIMIT = 48 * 1024 * 1024


def rows_of(shape):
    return lax.broadcasted_iota(jnp.int32, shape, 0)


def lanes_of(shape):
    return lax.broadcasted_iota(jnp.int32, shape, 1)


def matmul(lhs, rhs):
    return lax.dot_general(lhs, rhs, (((1,), (0,)), ((), ())), preferred_element_type=F32)


def matmul_nt(lhs, rhs):
    return lax.dot_general(lhs, rhs, (((1,), (1,)), ((), ())), preferred_element_type=F32)


def split(value):
    high = value.astype(BF16).astype(F32)
    return high, value - high


def onehot(index, size):
    return jnp.where(rows_of((size, 128)) == index, 1.0, 0.0).astype(BF16)


def split_brick(brick):
    high, low = split(brick)
    return jnp.concatenate([high, low], axis=1).astype(BF16)


def gather_slots(brick_split, cells):
    hot = jnp.concatenate([onehot(cell & 127, 128) for cell in cells], axis=1)
    found = matmul(brick_split, jnp.concatenate([hot, hot], axis=0))
    values = []
    for i, cell in enumerate(cells):
        here = rows_of((32, 128)) == (cell >> 7)
        part = found[:, i * 128 : (i + 1) * 128]
        values.append(
            [
                jnp.sum(jnp.where(here, part[32 * k : 32 * k + 32], 0.0), axis=0, keepdims=True)
                for k in range(3)
            ]
        )
    return values


def pair_tile(rows):
    row = rows_of((8, 128))
    tile = jnp.broadcast_to(rows[7], (8, 128))
    for i in range(7):
        tile = jnp.where(row == i, rows[i], tile)
    return tile


def species_scale(perm_ref, shape):
    species = rows_of(shape) & 3
    return jnp.where(species == 0, perm_ref[0], jnp.where(species == 1, perm_ref[1], perm_ref[2]))


def prepare_slots(t, segment_ref, weight_ref, count_ref, weights, halves, hots):
    row = rows_of((8, 128))
    lane = lanes_of((1, 128))
    for pair in range(2):
        both = []
        for block in (2 * pair, 2 * pair + 1):
            weight = weight_ref[block, pl.ds(t, 1), :]
            both.append(jnp.where(lane < count_ref[block, t], weight, 0.0))
            segment = segment_ref[block, pl.ds(t, 1), :]
            halves[block, t] = jnp.broadcast_to(segment >> 7, (8, 128))
            hots[block, t] = onehot(segment & 127, 128)
        weights[pair, t] = jnp.where(row < 4, both[0], both[1])


def scan_segments(decay, drive):
    lane = lanes_of(decay.shape)
    step = 1
    while step < SEG:
        inside = lane >= step
        earlier_decay = jnp.where(inside, pltpu.roll(decay, step, 1), 1.0)
        earlier_drive = jnp.where(inside, pltpu.roll(drive, step, 1), 0.0)
        drive = decay * earlier_drive + drive
        decay = decay * earlier_decay
        step *= 2
    return drive


def solve_blocks(inflow, values, weights, halves, hots, voxel_ref, flow_ref, perm_ref, send_ref):
    row = rows_of((8, SEG))
    scale = species_scale(perm_ref, (8, SEG))
    wide = lambda ref, i: jnp.concatenate([ref[i, t] for t in range(BRICKS)], axis=1)
    decays, drives = [], []
    for pair in range(2):
        high, low = split(wide(values, pair) * wide(weights, pair))
        sums = []
        for block in (2 * pair, 2 * pair + 1):
            upper = wide(halves, block) == 1
            lhs = jnp.concatenate(
                [
                    jnp.where(upper, 0.0, high),
                    jnp.where(upper, 0.0, low),
                    jnp.where(upper, high, 0.0),
                    jnp.where(upper, low, 0.0),
                ],
                axis=0,
            ).astype(BF16)
            part = matmul_nt(lhs, wide(hots, block))
            sums.append(
                jnp.concatenate([part[0:8] + part[8:16], part[16:24] + part[24:32]], axis=1)
            )
        gathered = jnp.where(row < 4, sums[0], sums[1])
        weight_sum = jnp.where(row < 4, gathered[3:4], gathered[7:8])
        speed = jnp.where(row < 4, flow_ref[2 * pair : 2 * pair + 1], flow_ref[2 * pair + 1 : 2 * pair + 2])
        inverse = 1.0 / (speed + scale * weight_sum)
        decays.append(speed * inverse)
        drives.append(scale * gathered * inverse)
    decay = jnp.concatenate(decays, axis=0)
    drive = jnp.concatenate(drives, axis=0)
    drive = drive + jnp.where(lanes_of((16, SEG)) == 0, decay * inflow, 0.0)
    vessel = scan_segments(decay, drive)

    send_ref[0, 32:48] = jnp.zeros((16, 128), F32)
    send_ref[BRICKS - 1, 16:32] = jnp.zeros((16, 128), F32)
    tile_row = rows_of((8, 128))
    scale = species_scale(perm_ref, (8, 128))
    for pair in range(2):
        high, low = split(vessel[8 * pair : 8 * pair + 8])
        lhs = jnp.concatenate(
            [high[:, :128], low[:, :128], high[:, 128:], low[:, 128:]], axis=0
        ).astype(BF16)
        found = [matmul(lhs, wide(hots, block)) for block in (2 * pair, 2 * pair + 1)]
        for t in range(BRICKS):
            at_slot = []
            for i in range(2):
                part = found[i][:, t * 128 : (t + 1) * 128]
                at_slot.append(
                    jnp.where(
                        halves[2 * pair + i, t] == 1,
                        part[16:24] + part[24:32],
                        part[0:8] + part[8:16],
                    )
                )
            vessel_value = jnp.where(tile_row < 4, at_slot[0], at_slot[1])
            flux = scale * weights[pair, t] * (vessel_value - values[pair, t])
            cell = jnp.where(
                tile_row < 4, voxel_ref[2 * pair, t : t + 1, :], voxel_ref[2 * pair + 1, t : t + 1, :]
            )
            cell_row = (tile_row & 3) == 3
            cell_value = cell.astype(F32)
            first = ((cell >> 7) & 7) < 4
            here = slice(8 * pair, 8 * pair + 8)
            send_ref[t, here] = jnp.where(cell_row, cell_value, flux)
            if t > 0:
                send_ref[t - 1, 16 + 8 * pair : 24 + 8 * pair] = jnp.where(
                    cell_row, cell_value, jnp.where(first, flux, 0.0)
                )
            if t < BRICKS - 1:
                send_ref[t + 1, 32 + 8 * pair : 40 + 8 * pair] = jnp.where(
                    cell_row, cell_value, jnp.where(first, 0.0, flux)
                )
    return vessel


def inlet_column(inlet_ref):
    row = rows_of((16, 1))
    column = jnp.zeros((16, 1), F32)
    for block in range(4):
        for k in range(3):
            column = jnp.where(row == 4 * block + k, inlet_ref[k, block], column)
    return column


def first_solve_kernel(
    place_ref, count_ref, perm_ref, inlet_ref, region_ref, voxel_ref, segment_ref, weight_ref, flow_ref,
    send_ref, ends_ref, around_ref, values, weights, halves, hots,
):
    def brick(t, carry):
        prepare_slots(t, segment_ref, weight_ref, count_ref, weights, halves, hots)
        found = gather_slots(
            split_brick(region_ref[t]), [voxel_ref[block, pl.ds(t, 1), :] for block in range(4)]
        )
        for pair in range(2):
            values[pair, t] = pair_tile([*found[2 * pair], 1.0, *found[2 * pair + 1], 1.0])
        return carry

    lax.fori_loop(0, BRICKS, brick, 0)
    vessel = solve_blocks(
        inlet_column(inlet_ref), values, weights, halves, hots, voxel_ref, flow_ref, perm_ref, send_ref
    )
    part, t = place_ref[0], place_ref[1]
    last = vessel[:, SEG - 1 : SEG]
    spot = lanes_of((16, 128)) == part * 16 + rows_of((16, 128))
    ends = jnp.sum(jnp.where(spot, last, 0.0), axis=0, keepdims=True)
    ends_ref[...] = jnp.broadcast_to(ends[None], (PARTS, 8, 128))
    after = jnp.where(t < BRICKS - 1, region_ref[jnp.minimum(t + 1, BRICKS - 1)], 0.0)
    before = jnp.where(t > 0, region_ref[jnp.maximum(t - 1, 0)], 0.0)
    around_ref[...] = jnp.where((rows_of((96, 128)) & 7) < 4, after, before)


def second_solve_kernel(
    upstream_ref, count_ref, perm_ref, inlet_ref, values_ref, voxel_ref, segment_ref, weight_ref, flow_ref,
    send_ref, vessel_ref, values, weights, halves, hots,
):
    def brick(t, carry):
        prepare_slots(t, segment_ref, weight_ref, count_ref, weights, halves, hots)
        spare = (rows_of((8, 128)) & 3) == 3
        for pair in range(2):
            values[pair, t] = jnp.where(spare, 1.0, values_ref[t, 8 * pair : 8 * pair + 8])
        return carry

    lax.fori_loop(0, BRICKS, brick, 0)
    row, lane = rows_of((16, 128)), lanes_of((16, 128))
    picked = jnp.zeros((16, 128), F32)
    for block in range(4):
        feeder = upstream_ref[block]
        device = feeder >> 2
        ends = values_ref[device & 15, 3:4, :]
        spot = (device >> 4) * 16 + (feeder & 3) * 4
        picked = jnp.where(((row >> 2) == block) & (lane == spot + (row & 3)), ends, picked)
    inflow = 0.5 * (inlet_column(inlet_ref) + jnp.sum(picked, axis=1, keepdims=True))
    vessel = solve_blocks(
        inflow, values, weights, halves, hots, voxel_ref, flow_ref, perm_ref, send_ref
    )
    for block in range(4):
        for k in range(3):
            vessel_ref[k, block : block + 1, :] = vessel[4 * block + k : 4 * block + k + 1]


def scatter_slots(recv_ref, source, first_tile, tiles):
    source[...] = jnp.zeros((192, 128), F32)

    def sender(s, carry):
        hots, parts = [], []
        for i in range(tiles):
            start = first_tile + 8 * i
            for base in (0, 4):
                cell = recv_ref[s, start + base + 3 : start + base + 4, :].astype(jnp.int32)
                hots.append(onehot(cell & 127, 128))
                here = rows_of((32, 128)) == (cell >> 7)
                highs, lows = [], []
                for k in range(3):
                    high, low = split(recv_ref[s, start + base + k : start + base + k + 1, :])
                    highs.append(jnp.where(here, high, 0.0))
                    lows.append(jnp.where(here, low, 0.0))
                parts.append(jnp.concatenate(highs + lows, axis=0).astype(BF16))
        source[...] += matmul_nt(jnp.concatenate(parts, axis=1), jnp.concatenate(hots, axis=1))
        return carry

    lax.fori_loop(0, BRICKS, sender, 0)
    return source[0:96] + source[96:192]


def planes(value):
    return value.reshape(3, 4, 8, 128)


def first_scatter_kernel(
    place_ref, recv_ref, tissue_ref, around_ref, rate_ref, rate_after_ref, rate_before_ref,
    up_ref, down_ref, own_ref, side_ref, rate_side_ref, scratch,
):
    side_rows = (rows_of((96, 128)) & 7) < 4
    rate_side = jnp.where(side_rows, rate_after_ref[...], rate_before_ref[...])
    rate_side_ref[...] = rate_side
    rates = (planes(rate_ref[...]), planes(rate_side))
    for i, value in enumerate(rates):
        here = slice(8 * i, 8 * i + 8)
        up_ref[:, 7:10, here] = value[:, 1:4]
        down_ref[:, 7:10, here] = value[:, 0:3]
    write_messages(recv_ref, planes(tissue_ref[...]), planes(around_ref[...]), up_ref, down_ref, own_ref, side_ref, scratch)


def write_messages(recv_ref, tissue, around, up_ref, down_ref, own_ref, side_ref, scratch):
    own = scatter_slots(recv_ref, scratch, 0, 2)
    side = scatter_slots(recv_ref, scratch, 16, 4)
    own_ref[...] = own
    side_ref[...] = side
    for i, (value, source) in enumerate(((tissue, planes(own)), (around, planes(side)))):
        here = slice(8 * i, 8 * i + 8)
        up_ref[:, 0:4, here] = value
        down_ref[:, 0:4, here] = value
        up_ref[:, 4:7, here] = source[:, 1:4]
        down_ref[:, 4:7, here] = source[:, 0:3]


def unpack_edges(values_ref, t):
    after = values_ref[jnp.minimum(t + 1, BRICKS - 1), 16:64, :]
    before = values_ref[jnp.maximum(t - 1, 0), 16:64, :]
    after = jnp.where(t < BRICKS - 1, after, 0.0).reshape(6, 8, 128)
    before = jnp.where(t > 0, before, 0.0).reshape(6, 8, 128)
    low = lax.broadcasted_iota(jnp.int32, (6, 8, 128), 1) < 4
    even = jnp.where(low, after, pltpu.roll(before, 4, 1))
    odd = jnp.where(low, pltpu.roll(after, 4, 1), before)
    both = [value for i in range(6) for value in (even[i], odd[i])]
    return jnp.concatenate(both, axis=0).reshape(3, 4, 8, 128)


def second_scatter_kernel(
    place_ref, recv_ref, tissue_ref, values_ref, up_ref, down_ref, own_ref, side_ref, around_ref, scratch
):
    around = unpack_edges(values_ref, place_ref[1])
    around_ref[...] = around.reshape(96, 128)
    write_messages(recv_ref, planes(tissue_ref[...]), around, up_ref, down_ref, own_ref, side_ref, scratch)


def run_sweeps(place_ref, below, above, tissue_ref, around_ref, source_ref, side_ref, rate_own, rate_side, rate_below, rate_above, now, later, source, inverse, produced):
    part, t = place_ref[0], place_ref[1]
    row = rows_of((16, 128))
    row_inside = ((row < 8) | ((row >= 12) & (t > 0)) | ((row < 12) & (t < BRICKS - 1))) & (
        (row < 8) | (row >= 12) | (t < BRICKS - 1)
    )
    inside = jnp.where(row_inside, 1.0, 0.0)
    lower = jnp.where(part > 0, inside, 0.0)
    upper = jnp.where(part < PARTS - 1, inside, 0.0)
    for k in range(3):
        now[k, 0:4] = below[k, 0:4]
        now[k, 8:12] = above[k, 0:4]
        now[k, 4:8, 0:8] = planes(tissue_ref[...])[k]
        now[k, 4:8, 8:16] = planes(around_ref[...])[k]
        source[k, 1:4] = below[k, 4:7]
        source[k, 8:11] = above[k, 4:7]
        source[k, 4:8, 0:8] = planes(source_ref[...])[k]
        source[k, 4:8, 8:16] = planes(side_ref[...])[k]
        own, side = planes(rate_own[...])[k], planes(rate_side[...])[k]
        for z in range(1, 11):
            if z < 4:
                rate, valid = rate_below[k, z + 6], lower
            elif z < 8:
                rate, valid = jnp.concatenate([own[z - 4], side[z - 4]], axis=0), inside
            else:
                rate, valid = rate_above[k, z - 1], upper
            inverse[k, z] = valid / (6.0 * DIFFUSION[k] + rate)
            if k == 1:
                produced[z] = 2.0 * rate
    lane = lanes_of((16, 128))
    old, new = now, later
    for sweep in range(1, SWEEPS + 1):
        for k in range(3):
            for z in range(sweep, 12 - sweep):
                middle = old[k, z]
                total = old[k, z - 1] + old[k, z + 1]
                total = total + pltpu.roll(middle, 1, 0) + pltpu.roll(middle, 15, 0)
                total = total + jnp.where(lane > 0, pltpu.roll(middle, 1, 1), 0.0)
                total = total + jnp.where(lane < 127, pltpu.roll(middle, 127, 1), 0.0)
                total = source[k, z] + DIFFUSION[k] * total
                if k == 2:
                    total = total + produced[z] * old[1, z]
                new[k, z] = total * inverse[k, z]
        old, new = new, old
    return old


def first_sweeps_kernel(
    place_ref, below, above, tissue_ref, around_ref, source_ref, side_ref, rate_own, rate_side, recv_ref, ends_ref,
    out_ref, send_ref, now, later, source, inverse, produced,
):
    final = run_sweeps(
        place_ref, below, above, tissue_ref, around_ref, source_ref, side_ref, rate_own, rate_side, below, above,
        now, later, source, inverse, produced,
    )
    t = place_ref[1]
    brick = final[:, 4:8, 0:8].reshape(96, 128)
    out_ref[...] = brick
    brick_split = split_brick(brick)
    tiles = brick.reshape(6, 2, 8, 128)
    low = lax.broadcasted_iota(jnp.int32, (6, 8, 128), 1) < 4
    even, odd = tiles[:, 0], tiles[:, 1]
    first_rows = jnp.where(low, even, pltpu.roll(odd, 4, 1)).reshape(48, 128)
    last_rows = jnp.where(low, pltpu.roll(even, 4, 1), odd).reshape(48, 128)
    ends = ends_ref[0, 0:1]
    for part in range(1, PARTS):
        ends = ends + ends_ref[part, 0:1]

    def receiver(s, carry):
        cells = [recv_ref[s, 4 * b + 3 : 4 * b + 4, :].astype(jnp.int32) for b in range(4)]
        found = gather_slots(brick_split, cells)
        for pair in range(2):
            send_ref[s, 8 * pair : 8 * pair + 8] = pair_tile(
                [*found[2 * pair], ends, *found[2 * pair + 1], ends]
            )
        send_ref[s, 16:64] = jnp.where(s < t, first_rows, last_rows)
        return carry

    lax.fori_loop(0, BRICKS, receiver, 0)


def second_sweeps_kernel(
    place_ref, below, above, tissue_ref, around_ref, source_ref, side_ref, rate_own, rate_side, rate_below, rate_above,
    out_ref, now, later, source, inverse, produced,
):
    final = run_sweeps(
        place_ref, below, above, tissue_ref, around_ref, source_ref, side_ref, rate_own, rate_side, rate_below, rate_above,
        now, later, source, inverse, produced,
    )
    out_ref[...] = final[:, 4:8, 0:8]


def call(kernel, name, outs, args, scalars, scratch):
    whole = pl.BlockSpec(memory_space=pltpu.VMEM)
    scalar = pl.BlockSpec(memory_space=pltpu.SMEM)
    return pl.pallas_call(
        kernel,
        out_shape=[jax.ShapeDtypeStruct(shape, F32) for shape in outs],
        in_specs=[scalar] * scalars + [whole] * (len(args) - scalars),
        out_specs=[whole] * len(outs),
        scratch_shapes=scratch,
        compiler_params=pltpu.CompilerParams(vmem_limit_bytes=VMEM_LIMIT),
        name=name,
    )(*args)


def shards(
    tissue_start,
    consumption,
    inlet,
    flow,
    permeability,
    intersection_count,
    intersection_segment,
    intersection_voxel,
    intersection_weight,
    upstream,
):
    place = jnp.stack([lax.axis_index("vessel"), lax.axis_index("tissue")]).astype(jnp.int32)
    tissue = tissue_start.reshape(96, 128)
    rate = consumption.reshape(96, 128)

    def exchange(value, axis):
        return lax.all_to_all(value, axis, 0, 0, tiled=True)

    def shift(value, axis, step):
        size = lax.axis_size(axis)
        pairs = [(i, i + step) for i in range(size) if 0 <= i + step < size]
        return lax.ppermute(value, axis, pairs)

    solve_scratch = [
        pltpu.VMEM((2, BRICKS, 8, 128), F32),
        pltpu.VMEM((2, BRICKS, 8, 128), F32),
        pltpu.VMEM((4, BRICKS, 8, 128), jnp.int32),
        pltpu.VMEM((4, BRICKS, 128, 128), BF16),
    ]
    sweep_scratch = [
        pltpu.VMEM((3, 12, 16, 128), F32),
        pltpu.VMEM((3, 12, 16, 128), F32),
        pltpu.VMEM((3, 12, 16, 128), F32),
        pltpu.VMEM((3, 12, 16, 128), F32),
        pltpu.VMEM((12, 16, 128), F32),
    ]
    scatter_scratch = [pltpu.VMEM((192, 128), F32)]
    slots = (intersection_voxel, intersection_segment, intersection_weight, flow)

    rate_after = shift(rate, "tissue", -1)
    rate_before = shift(rate, "tissue", 1)
    region = exchange(jnp.broadcast_to(tissue[None], (BRICKS, 96, 128)), "tissue")
    send, ends, around = call(
        first_solve_kernel,
        "first_solve",
        [(BRICKS, 48, 128), (PARTS, 8, 128), (96, 128)],
        [place, intersection_count, permeability, inlet, region, *slots],
        4,
        solve_scratch,
    )
    received = exchange(send, "tissue")
    ends = exchange(ends, "vessel")
    up, down, source, side, rate_side = call(
        first_scatter_kernel,
        "first_scatter",
        [(3, 10, 16, 128), (3, 10, 16, 128), (96, 128), (96, 128), (96, 128)],
        [place, received, tissue, around, rate, rate_after, rate_before],
        1,
        scatter_scratch,
    )
    rate_below = below = shift(up, "vessel", 1)
    rate_above = above = shift(down, "vessel", -1)
    tissue, send = call(
        first_sweeps_kernel,
        "first_sweeps",
        [(96, 128), (BRICKS, 64, 128)],
        [place, below, above, tissue, around, source, side, rate, rate_side, received, ends],
        1,
        sweep_scratch,
    )
    values = exchange(send, "tissue")
    send, vessel = call(
        second_solve_kernel,
        "second_solve",
        [(BRICKS, 48, 128), (3, 4, SEG)],
        [upstream, intersection_count, permeability, inlet, values, *slots],
        4,
        solve_scratch,
    )
    received = exchange(send, "tissue")
    up, down, source, side, around = call(
        second_scatter_kernel,
        "second_scatter",
        [(3, 7, 16, 128), (3, 7, 16, 128), (96, 128), (96, 128), (96, 128)],
        [place, received, tissue, values],
        1,
        scatter_scratch,
    )
    below = shift(up, "vessel", 1)
    above = shift(down, "vessel", -1)
    (tissue,) = call(
        second_sweeps_kernel,
        "second_sweeps",
        [(3, 4, 8, 128)],
        [place, below, above, tissue, around, source, side, rate, rate_side, rate_below, rate_above],
        1,
        sweep_scratch,
    )
    return tissue, vessel


def solution(mesh):
    return jax.shard_map(
        shards,
        mesh=mesh,
        in_specs=(
            P(None, "vessel", "tissue", None),
            P(None, "vessel", "tissue", None),
            P(None, ("vessel", "tissue")),
            P(("vessel", "tissue"), None),
            P(),
            P(("vessel", "tissue"), None),
            P(("vessel", "tissue"), None, None),
            P(("vessel", "tissue"), None, None),
            P(("vessel", "tissue"), None, None),
            P(("vessel", "tissue")),
        ),
        out_specs=(P(None, "vessel", "tissue", None), P(None, ("vessel", "tissue"), None)),
        check_vma=False,
    )
```

time: 757 us -> 129 us (0.17); the launches traced: 746 us -> 128 us
  local copies, waits for them, and re-layouts: 224 us -> 1.8 us
  other arithmetic: 141 us -> 0.08 us
  waiting for transfers between devices: 125 us -> 21.7 us
  starting transfers between devices: 110 us -> 32.1 us
  blocking collectives: 108 us -> 39.6 us
  Pallas kernels: 0 us -> 32.3 us
  matrix products: 21.3 us -> 0 us
  between operations: 14.9 us -> 0.81 us
    scatter-add x2 -> x0, other arithmetic: 115 us -> none  [shards(): jax.ops.segment_sum(species_row, region_index, voxels * columns)]
    reduce_scatter x2 -> x0, waiting for transfers between devices: 111 us -> none  [shards(): lax.psum_scatter(partial_source.reshape(species, depth, full_rows, width)...]
    all_gather x3 -> x0, blocking collectives: 108 us -> none  [the longest x1 61.1 us: shards(): lax.all_gather(vessel[:, :, SEG - 1], ('vessel', 'tissue'), axis=0, tiled...]
    ppermute x32 -> x6, starting transfers between devices: 110 us -> 20.4 us  [shift(): return lax.ppermute(value, axis, pairs)]
    gather x3 -> x0, local copies, waits for them, and re-layouts: 77.1 us -> none  [the longest x2 76.5 us: shards(): region[:, region_index].reshape(species, blocks_here, columns, slots)]
    reshape x10 -> x0, local copies, waits for them, and re-layouts: 51.8 us -> none  [the longest x2 40.5 us: shards(): partial_source.reshape(species, depth, full_rows, width)]
    slice x330 -> x0, local copies, waits for them, and re-layouts: 41.6 us -> none  [the longest x320 41.6 us: solve_block(): _, vessel = lax.associative_scan(combine, (decay_rate, drive_term), axis=1)]
    all_to_all x0 -> x3, blocking collectives: none -> 39.6 us  [exchange(): return lax.all_to_all(value, axis, 0, 0, tiled=True)]
  transfers between devices with their start and end apart: 34 -> 8, of which waited for: 17 -> 5; matrix products, arithmetic and copies ran while one was open for 0% -> 0% of each run, Pallas kernels for 0% -> 0%
where the time goes in v1:
time: 129 us; the launch traced here: 128 us
  blocking collectives  39.6 us (31%)
  Pallas kernels  32.3 us (25%)
  starting transfers between devices  32.1 us (25%)
  waiting for transfers between devices  21.7 us (17%)
  local copies, waits for them, and re-layouts  1.8 us (1%)
    all_to_all x3, blocking collectives, exchange(): return lax.all_to_all(value, axis, 0, 0, tiled=True)  39.6 us
    pallas_call x6, Pallas kernels, call(): pl.pallas_call(kernel, out_shape=[jax.ShapeDtypeStruct(shape, F32) for sh...  32.3 us
    ppermute x6, starting transfers between devices, shift(): return lax.ppermute(value, axis, pairs)  20.4 us
    all_to_all x2, waiting for transfers between devices, exchange(): return lax.all_to_all(value, axis, 0, 0, tiled=True)  13.1 us
    all_to_all x2, starting transfers between devices, exchange(): return lax.all_to_all(value, axis, 0, 0, tiled=True)  11.7 us
    ppermute x6, waiting for transfers between devices, shift(): return lax.ppermute(value, axis, pairs)  8.63 us
  transfers between devices with their start and end apart: 8, of which 5 were waited for; matrix products, arithmetic and copies ran while one was open for 0% of the time, Pallas kernels for 0%

profile of v1, /device:TPU:1, one launch (start us, length us, event | category | flops | bytes accessed | tf_op | source)
XLA Modules:
  0.0 128.3 jit_solution(14612496976294900210)
XLA Ops:
  0.6 1.8 %broadcast_in_dim.8 = f32[16,96,128]{2,1,0:T(8,128)} broadcast(f32[96,128]{1,0:T(8,128)} %bitcast.9), dimensions={1,2} | broadcast | bytes 835584 | tf_op jit(solution)/shard_map/broadcast_in_dim | solution.py:470
  2.4 0.0 copy-start.2
  2.4 0.0 copy-start.3
  2.4 0.0 copy-start.4
  2.4 0.0 copy-start.7
  2.4 7.7 %all-to-all-start = ((f32[16,96,128]{2,1,0:T(8,128)}), f32[16,96,128]{2,1,0:T(8,128)S(1)}, u32[]{:S(2)}, u32[]{:S(2)}) async-start(f32[16,96,128]{2,1,0:T(8,128)} %broadcast_in_dim.8), calls=%async_computation | async-start | bytes 1572864 | tf_op jit(solution)/shard_map/all_to_all | solution.py:445
  10.1 0.0 copy-start.5
  10.1 0.0 copy-start.6
  10.2 0.0 copy-start.8
  10.2 0.1 pad_add_fusion.place_ref
  10.2 13.1 %all-to-all-done.region_ref = f32[16,96,128]{2,1,0:T(8,128)S(1)} async-done(((f32[16,96,128]{2,1,0:T(8,128)}), f32[16,96,128]{2,1,0:T(8,128)S(1)}, u32[]{:S(2)}, u32[]{:S(2)}) %all-to-all-start) | async-done | bytes 786464 | tf_op jit(solution)/shard_map/all_to_all | solution.py:445
  23.3 0.0 copy-done.2
  23.3 0.0 copy-done.3
  23.3 0.0 copy-done.4
  23.3 0.0 copy-done.7
  23.3 0.0 copy-done.5
  23.3 0.0 copy-done.6
  23.4 0.0 copy-done.8
  23.4 6.2 %first_solve.1 = (f32[16,48,128]{2,1,0:T(8,128)}, f32[8,8,128]{2,1,0:T(8,128)S(1)}, f32[96,128]{1,0:T(8,128)S(1)}) custom-call(s32[2]{0:T(128)S(1)} %pad_add_fusion.place_ref, s32[4,16]{1,0:T(4,128)S(1)} %copy-done.6, f32[3]{0:T(128)S(1)} %copy-done.8, f32[3,4]{1,0:T(4,128)S(1)} %copy-done.7, f32[16,96,128]{2,1,0:T(8,128)S(1)} %all-to-all-done.region_ref, ...), custom_call_target="tpu_custom_call" | custom-call | tf_op jit(solution)/shard_map/first_solve/pallas_call | solution.py:417
  29.5 0.0 copy-start
  29.6 0.0 copy-start.1
  29.6 3.9 %all-to-all-start.1 = ((f32[16,48,128]{2,1,0:T(8,128)}), f32[16,48,128]{2,1,0:T(8,128)S(1)}, u32[]{:S(2)}, u32[]{:S(2)}) async-start(f32[16,48,128]{2,1,0:T(8,128)} %get-tuple-element.19), calls=%async_computation.1 | async-start | bytes 786432 | tf_op jit(solution)/shard_map/all_to_all | solution.py:445
  33.5 0.0 copy-done
  33.5 3.3 %collective-permute-start.1 = (f32[96,128]{1,0:T(8,128)S(1)}, f32[96,128]{1,0:T(8,128)S(1)}, u32[]{:S(2)}, u32[]{:S(2)}) collective-permute-start(f32[96,128]{1,0:T(8,128)S(1)} %bitcast.4), channel_id=1, source_target_pairs={{0,1},{1,2},{2,3},{3,4},{4,5},{5,6},{6,7},{7,8},{8,9},{9,10},{10,1... | collective-permute-start | bytes 147464 | tf_op jit(solution)/shard_map/ppermute | solution.py:450
  36.8 1.3 %collective-permute-start = (f32[96,128]{1,0:T(8,128)S(1)}, f32[96,128]{1,0:T(8,128)S(1)}, u32[]{:S(2)}, u32[]{:S(2)}) collective-permute-start(f32[96,128]{1,0:T(8,128)S(1)} %bitcast.5), channel_id=1, source_target_pairs={{1,0},{2,1},{3,2},{4,3},{5,4},{6,5},{7,6},{8,7},{9,8},{10,9},{11,1... | collective-permute-start | bytes 147464 | tf_op jit(solution)/shard_map/ppermute | solution.py:450
  38.1 0.2 collective-permute-done.1.rate_before_ref
  38.3 3.6 %collective-permute-done.rate_after_ref = f32[96,128]{1,0:T(8,128)S(1)} collective-permute-done((f32[96,128]{1,0:T(8,128)S(1)}, f32[96,128]{1,0:T(8,128)S(1)}, u32[]{:S(2)}, u32[]{:S(2)}) %collective-permute-start) | collective-permute-done | bytes 49184 | tf_op jit(solution)/shard_map/ppermute | solution.py:450
  41.9 0.0 all-to-all-done.1.recv_ref
  41.9 0.0 copy-done.1
  41.9 8.6 %first_scatter.1 = (f32[3,10,16,128]{3,2,1,0:T(8,128)S(1)}, f32[3,10,16,128]{3,2,1,0:T(8,128)S(1)}, f32[96,128]{1,0:T(8,128)S(1)}, f32[96,128]{1,0:T(8,128)S(1)}, f32[96,128]{1,0:T(8,128)S(1)}) custom-call(s32[2]{0:T(128)S(1)} %pad_add_fusion.place_ref, f32[16,48,128]{2,1,0:T(8,128)S(1)} %all-to-all-done.1.recv_ref, f32[96,128]{1,0:T(8,128)S(1)} %bitcast.10, ...), custom_call_target="tpu_custom_call" | custom-call | tf_op jit(solution)/shard_map/first_scatter/pallas_call | solution.py:417
  50.6 6.9 %collective-permute-start.2 = (f32[3,10,16,128]{3,2,1,0:T(8,128)S(1)}, f32[3,10,16,128]{3,2,1,0:T(8,128)S(1)}, u32[]{:S(2)}, u32[]{:S(2)}) collective-permute-start(f32[3,10,16,128]{3,2,1,0:T(8,128)S(1)} %get-tuple-element.21), channel_id=1, source_target_pairs={{0,16},{16,32},{32,48},{48,64},{64,80},{80,96},{96,112},{1,17},{17... | collective-permute-start | bytes 737288 | tf_op jit(solution)/shard_map/ppermute | solution.py:450
  57.5 1.9 %collective-permute-start.3 = (f32[3,10,16,128]{3,2,1,0:T(8,128)S(1)}, f32[3,10,16,128]{3,2,1,0:T(8,128)S(1)}, u32[]{:S(2)}, u32[]{:S(2)}) collective-permute-start(f32[3,10,16,128]{3,2,1,0:T(8,128)S(1)} %get-tuple-element.22), channel_id=1, source_target_pairs={{16,0},{32,16},{48,32},{64,48},{80,64},{96,80},{112,96},{17,1},{33... | collective-permute-start | bytes 737288 | tf_op jit(solution)/shard_map/ppermute | solution.py:450
  59.4 10.0 %all_to_all.25.ends_ref = f32[8,8,128]{2,1,0:T(8,128)S(1)} all-to-all(f32[8,8,128]{2,1,0:T(8,128)S(1)} %get-tuple-element.26), channel_id=1, replica_groups=mesh['vessel'=8,'tissue'=16] {'vessel'}, dimensions={0} | all-to-all | bytes 65536 | tf_op jit(solution)/shard_map/all_to_all | solution.py:445
  69.5 0.0 collective-permute-done.2.below.rate_below
  69.5 0.0 collective-permute-done.3.above.rate_above
  69.5 4.2 %first_sweeps.1 = (f32[96,128]{1,0:T(8,128)S(1)}, f32[16,64,128]{2,1,0:T(8,128)S(1)}) custom-call(s32[2]{0:T(128)S(1)} %pad_add_fusion.place_ref, f32[3,10,16,128]{3,2,1,0:T(8,128)S(1)} %collective-permute-done.2.below.rate_below, f32[3,10,16,128]{3,2,1,0:T(8,128)S(1)} %collective-permute-done.3.above.rate_above, f32[96,128]{1,0:T(8,128)S(1)} %bitcast.11, ...), custom_call_target="tpu_custom_call" | custom-call | tf_op jit(solution)/shard_map/first_sweeps/pallas_call | solution.py:417
  73.7 0.0 copy-start.9
  73.7 18.3 %all_to_all.26.values_ref = f32[16,64,128]{2,1,0:T(8,128)S(1)} all-to-all(f32[16,64,128]{2,1,0:T(8,128)S(1)} %get-tuple-element.27), channel_id=1, replica_groups=mesh['vessel'=8,'tissue'=16] {'tissue'}, dimensions={0} | all-to-all | bytes 1048576 | tf_op jit(solution)/shard_map/all_to_all | solution.py:445
  92.0 0.0 copy-done.9
  92.0 3.1 %second_solve.1 = (f32[16,48,128]{2,1,0:T(8,128)S(1)}, f32[3,4,256]{2,1,0:T(4,128)}) custom-call(s32[4]{0:T(128)S(1)} %copy-done.9, s32[4,16]{1,0:T(4,128)S(1)} %copy-done.6, f32[3]{0:T(128)S(1)} %copy-done.8, f32[3,4]{1,0:T(4,128)S(1)} %copy-done.7, f32[16,64,128]{2,1,0:T(8,128)S(1)} %all_to_all.26.values_ref, s32[4,16,128]{2,1,0:T(8,128)S(1)} %copy-done.2, ...), custom_call_target="tpu_custom_call" | custom-call | tf_op jit(solution)/shard_map/second_solve/pallas_call | solution.py:417
  95.1 11.2 %all_to_all.27.recv_ref = f32[16,48,128]{2,1,0:T(8,128)S(1)} all-to-all(f32[16,48,128]{2,1,0:T(8,128)S(1)} %get-tuple-element.28), channel_id=1, replica_groups=mesh['vessel'=8,'tissue'=16] {'tissue'}, dimensions={0} | all-to-all | bytes 786432 | tf_op jit(solution)/shard_map/all_to_all | solution.py:445
  106.3 8.6 %second_scatter.1 = (f32[3,7,16,128]{3,2,1,0:T(8,128)S(1)}, f32[3,7,16,128]{3,2,1,0:T(8,128)S(1)}, f32[96,128]{1,0:T(8,128)S(1)}, f32[96,128]{1,0:T(8,128)S(1)}, f32[96,128]{1,0:T(8,128)S(1)}) custom-call(s32[2]{0:T(128)S(1)} %pad_add_fusion.place_ref, f32[16,48,128]{2,1,0:T(8,128)S(1)} %all_to_all.27.recv_ref, f32[96,128]{1,0:T(8,128)S(1)} %get-tuple-element.29.tissue_ref, ...), custom_call_target="tpu_custom_call" | custom-call | tf_op jit(solution)/shard_map/second_scatter/pallas_call | solution.py:417
  114.9 5.1 %collective-permute-start.4 = (f32[3,7,16,128]{3,2,1,0:T(8,128)S(1)}, f32[3,7,16,128]{3,2,1,0:T(8,128)S(1)}, u32[]{:S(2)}, u32[]{:S(2)}) collective-permute-start(f32[3,7,16,128]{3,2,1,0:T(8,128)S(1)} %get-tuple-element.30), channel_id=1, source_target_pairs={{0,16},{16,32},{32,48},{48,64},{64,80},{80,96},{96,112},{1,17},{17... | collective-permute-start | bytes 516104 | tf_op jit(solution)/shard_map/ppermute | solution.py:450
  120.0 1.9 %collective-permute-start.5 = (f32[3,7,16,128]{3,2,1,0:T(8,128)S(1)}, f32[3,7,16,128]{3,2,1,0:T(8,128)S(1)}, u32[]{:S(2)}, u32[]{:S(2)}) collective-permute-start(f32[3,7,16,128]{3,2,1,0:T(8,128)S(1)} %get-tuple-element.31), channel_id=1, source_target_pairs={{16,0},{32,16},{48,32},{64,48},{80,64},{96,80},{112,96},{17,1},{33... | collective-permute-start | bytes 516104 | tf_op jit(solution)/shard_map/ppermute | solution.py:450
  121.9 0.4 collective-permute-done.4.below
  122.3 4.4 %collective-permute-done.5.above = f32[3,7,16,128]{3,2,1,0:T(8,128)S(1)} collective-permute-done((f32[3,7,16,128]{3,2,1,0:T(8,128)S(1)}, f32[3,7,16,128]{3,2,1,0:T(8,128)S(1)}, u32[]{:S(2)}, u32[]{:S(2)}) %collective-permute-start.5) | collective-permute-done | bytes 172064 | tf_op jit(solution)/shard_map/ppermute | solution.py:450
  126.7 1.6 %second_sweeps.1 = f32[3,4,8,128]{3,2,1,0:T(8,128)} custom-call(s32[2]{0:T(128)S(1)} %pad_add_fusion.place_ref, f32[3,7,16,128]{3,2,1,0:T(8,128)S(1)} %collective-permute-done.4.below, f32[3,7,16,128]{3,2,1,0:T(8,128)S(1)} %collective-permute-done.5.above, f32[96,128]{1,0:T(8,128)S(1)} %get-tuple-element.29.tissue_ref, ...), custom_call_target="tpu_custom_call" | custom-call | tf_op jit(solution)/shard_map/second_sweeps/pallas_call | solution.py:417
Async XLA Ops:
  2.4 20.9 %copy-start.2 = (s32[4,16,128]{2,1,0:T(8,128)S(1)}, s32[4,16,128]{2,1,0:T(8,128)}, u32[]{:S(2)}) copy-start(s32[4,16,128]{2,1,0:T(8,128)} %voxel_ref.3) | copy-start | bytes 98308
  2.4 20.9 %copy-start.3 = (s32[4,16,128]{2,1,0:T(8,128)S(1)}, s32[4,16,128]{2,1,0:T(8,128)}, u32[]{:S(2)}) copy-start(s32[4,16,128]{2,1,0:T(8,128)} %segment_ref.3) | copy-start | bytes 98308
  2.4 20.9 %copy-start.4 = (f32[4,16,128]{2,1,0:T(8,128)S(1)}, f32[4,16,128]{2,1,0:T(8,128)}, u32[]{:S(2)}) copy-start(f32[4,16,128]{2,1,0:T(8,128)} %weight_ref.3) | copy-start | bytes 98308
  2.4 20.9 %copy-start.7 = (f32[3,4]{1,0:T(4,128)S(1)}, f32[3,4]{1,0:T(4,128)}, u32[]{:S(2)}) copy-start(f32[3,4]{1,0:T(4,128)} %inlet_ref.3) | copy-start | bytes 148
  2.4 20.9 %all-to-all-start = ((f32[16,96,128]{2,1,0:T(8,128)}), f32[16,96,128]{2,1,0:T(8,128)S(1)}, u32[]{:S(2)}, u32[]{:S(2)}) async-start(f32[16,96,128]{2,1,0:T(8,128)} %broadcast_in_dim.8), calls=%async_computation | async-start | bytes 1572864 | tf_op jit(solution)/shard_map/all_to_all | solution.py:445
  10.1 13.2 %copy-start.5 = (f32[4,256]{1,0:T(4,128)S(1)}, f32[4,256]{1,0:T(4,128)}, u32[]{:S(2)}) copy-start(f32[4,256]{1,0:T(4,128)} %flow_ref.3) | copy-start | bytes 12292
  10.1 13.2 %copy-start.6 = (s32[4,16]{1,0:T(4,128)S(1)}, s32[4,16]{1,0:T(4,128)}, u32[]{:S(2)}) copy-start(s32[4,16]{1,0:T(4,128)} %count_ref.3) | copy-start | bytes 772
  10.2 13.2 %copy-start.8 = (f32[3]{0:T(128)S(1)}, f32[3]{0:T(128)}, u32[]{:S(2)}) copy-start(f32[3]{0:T(128)} %perm_ref.3) | copy-start | bytes 40
  29.5 4.0 %copy-start = (f32[3,4,8,128]{3,2,1,0:T(8,128)S(1)}, f32[3,4,8,128]{3,2,1,0:T(8,128)}, u32[]{:S(2)}) copy-start(f32[3,4,8,128]{3,2,1,0:T(8,128)} %param.11) | copy-start | bytes 147460
  29.6 12.4 %copy-start.1 = (f32[3,4,8,128]{3,2,1,0:T(8,128)S(1)}, f32[3,4,8,128]{3,2,1,0:T(8,128)}, u32[]{:S(2)}) copy-start(f32[3,4,8,128]{3,2,1,0:T(8,128)} %param.10) | copy-start | bytes 147460
  29.6 12.4 %all-to-all-start.1 = ((f32[16,48,128]{2,1,0:T(8,128)}), f32[16,48,128]{2,1,0:T(8,128)S(1)}, u32[]{:S(2)}, u32[]{:S(2)}) async-start(f32[16,48,128]{2,1,0:T(8,128)} %get-tuple-element.19), calls=%async_computation.1 | async-start | bytes 786432 | tf_op jit(solution)/shard_map/all_to_all | solution.py:445
  33.5 4.8 %collective-permute-start.1 = (f32[96,128]{1,0:T(8,128)S(1)}, f32[96,128]{1,0:T(8,128)S(1)}, u32[]{:S(2)}, u32[]{:S(2)}) collective-permute-start(f32[96,128]{1,0:T(8,128)S(1)} %bitcast.4), channel_id=1, source_target_pairs={{0,1},{1,2},{2,3},{3,4},{4,5},{5,6},{6,7},{7,8},{8,9},{9,10},{10,1... | collective-permute-start | bytes 147464 | tf_op jit(solution)/shard_map/ppermute | solution.py:450
  36.8 5.1 %collective-permute-start = (f32[96,128]{1,0:T(8,128)S(1)}, f32[96,128]{1,0:T(8,128)S(1)}, u32[]{:S(2)}, u32[]{:S(2)}) collective-permute-start(f32[96,128]{1,0:T(8,128)S(1)} %bitcast.5), channel_id=1, source_target_pairs={{1,0},{2,1},{3,2},{4,3},{5,4},{6,5},{7,6},{8,7},{9,8},{10,9},{11,1... | collective-permute-start | bytes 147464 | tf_op jit(solution)/shard_map/ppermute | solution.py:450
  50.6 18.9 %collective-permute-start.2 = (f32[3,10,16,128]{3,2,1,0:T(8,128)S(1)}, f32[3,10,16,128]{3,2,1,0:T(8,128)S(1)}, u32[]{:S(2)}, u32[]{:S(2)}) collective-permute-start(f32[3,10,16,128]{3,2,1,0:T(8,128)S(1)} %get-tuple-element.21), channel_id=1, source_target_pairs={{0,16},{16,32},{32,48},{48,64},{64,80},{80,96},{96,112},{1,17},{17... | collective-permute-start | bytes 737288 | tf_op jit(solution)/shard_map/ppermute | solution.py:450
  57.5 12.0 %collective-permute-start.3 = (f32[3,10,16,128]{3,2,1,0:T(8,128)S(1)}, f32[3,10,16,128]{3,2,1,0:T(8,128)S(1)}, u32[]{:S(2)}, u32[]{:S(2)}) collective-permute-start(f32[3,10,16,128]{3,2,1,0:T(8,128)S(1)} %get-tuple-element.22), channel_id=1, source_target_pairs={{16,0},{32,16},{48,32},{64,48},{80,64},{96,80},{112,96},{17,1},{33... | collective-permute-start | bytes 737288 | tf_op jit(solution)/shard_map/ppermute | solution.py:450
  73.7 18.3 %copy-start.9 = (s32[4]{0:T(128)S(1)}, s32[4]{0:T(128)}, u32[]{:S(2)}) copy-start(s32[4]{0:T(128)} %upstream_ref.1) | copy-start | bytes 52
  114.9 7.4 %collective-permute-start.4 = (f32[3,7,16,128]{3,2,1,0:T(8,128)S(1)}, f32[3,7,16,128]{3,2,1,0:T(8,128)S(1)}, u32[]{:S(2)}, u32[]{:S(2)}) collective-permute-start(f32[3,7,16,128]{3,2,1,0:T(8,128)S(1)} %get-tuple-element.30), channel_id=1, source_target_pairs={{0,16},{16,32},{32,48},{48,64},{64,80},{80,96},{96,112},{1,17},{17... | collective-permute-start | bytes 516104 | tf_op jit(solution)/shard_map/ppermute | solution.py:450
  120.0 6.7 %collective-permute-start.5 = (f32[3,7,16,128]{3,2,1,0:T(8,128)S(1)}, f32[3,7,16,128]{3,2,1,0:T(8,128)S(1)}, u32[]{:S(2)}, u32[]{:S(2)}) collective-permute-start(f32[3,7,16,128]{3,2,1,0:T(8,128)S(1)} %get-tuple-element.31), channel_id=1, source_target_pairs={{16,0},{32,16},{48,32},{64,48},{80,64},{96,80},{112,96},{17,1},{33... | collective-permute-start | bytes 516104 | tf_op jit(solution)/shard_map/ppermute | solution.py:450

commit v2 on v1

v2 whole, which is shorter than its diff:
```python
import jax
import jax.numpy as jnp
from jax import lax
from jax.experimental import pallas as pl
from jax.experimental.pallas import tpu as pltpu
from jax.sharding import PartitionSpec as P


SEG = 256
SWEEPS = 4
DIFFUSION = (1.0, 0.7, 0.7)
BRICKS = 16
PARTS = 8
F32 = jnp.float32
BF16 = jnp.bfloat16
VMEM_LIMIT = 32 * 1024 * 1024
SENDERS = 4


def rows_of(shape):
    return lax.broadcasted_iota(jnp.int32, shape, 0)


def lanes_of(shape):
    return lax.broadcasted_iota(jnp.int32, shape, 1)


def matmul(lhs, rhs):
    return lax.dot_general(lhs, rhs, (((1,), (0,)), ((), ())), preferred_element_type=F32)


def matmul_nt(lhs, rhs):
    return lax.dot_general(lhs, rhs, (((1,), (1,)), ((), ())), preferred_element_type=F32)


def split(value):
    high = value.astype(BF16).astype(F32)
    return high, value - high


def packed(row):
    return jnp.broadcast_to(row, (16, 128)).astype(F32).astype(BF16)


def matches(index, size):
    row = rows_of((16, 128)).astype(F32).astype(BF16)
    wanted = packed(index)
    return [row + BF16(i) == wanted for i in range(0, size, 16)]


def onehot(index, size):
    one, zero = jnp.ones((16, 128), BF16), jnp.zeros((16, 128), BF16)
    return jnp.concatenate([jnp.where(hit, one, zero) for hit in matches(index, size)], axis=0)


def split_brick(brick):
    high, low = split(brick)
    return jnp.concatenate([high, low], axis=1).astype(BF16)


def gather_slots(brick_split, cells):
    hot = jnp.concatenate([onehot(cell & 127, 128) for cell in cells], axis=1)
    found = matmul(brick_split, jnp.concatenate([hot, hot], axis=0))
    values = []
    for i, cell in enumerate(cells):
        here = rows_of((32, 128)) == (cell >> 7)
        part = found[:, i * 128 : (i + 1) * 128]
        values.append(
            [
                jnp.sum(jnp.where(here, part[32 * k : 32 * k + 32], 0.0), axis=0, keepdims=True)
                for k in range(3)
            ]
        )
    return values


def pair_tile(rows):
    row = rows_of((8, 128))
    tile = jnp.broadcast_to(rows[7], (8, 128))
    for i in range(7):
        tile = jnp.where(row == i, rows[i], tile)
    return tile


def species_scale(perm_ref, shape):
    species = rows_of(shape) & 3
    return jnp.where(species == 0, perm_ref[0], jnp.where(species == 1, perm_ref[1], perm_ref[2]))


def prepare_slots(t, segment_ref, weight_ref, count_ref, weights, halves, hots):
    row = rows_of((8, 128))
    lane = lanes_of((1, 128))
    for pair in range(2):
        both = []
        for block in (2 * pair, 2 * pair + 1):
            weight = weight_ref[block, pl.ds(t, 1), :]
            both.append(jnp.where(lane < count_ref[block, t], weight, 0.0))
            segment = segment_ref[block, pl.ds(t, 1), :]
            halves[block, t] = jnp.broadcast_to(segment >> 7, (8, 128))
            hots[block, t] = onehot(segment & 127, 128)
        weights[pair, t] = jnp.where(row < 4, both[0], both[1])


def scan_segments(decay, drive):
    lane = lanes_of(decay.shape)
    step = 1
    while step < SEG:
        inside = lane >= step
        earlier_decay = jnp.where(inside, pltpu.roll(decay, step, 1), 1.0)
        earlier_drive = jnp.where(inside, pltpu.roll(drive, step, 1), 0.0)
        drive = decay * earlier_drive + drive
        decay = decay * earlier_decay
        step *= 2
    return drive


def solve_blocks(inflow, values, weights, halves, hots, voxel_ref, flow_ref, perm_ref, send_ref, narrow):
    row = rows_of((8, SEG))
    scale = species_scale(perm_ref, (8, SEG))
    wide = lambda ref, i: jnp.concatenate([ref[i, t] for t in range(BRICKS)], axis=1)
    decays, drives = [], []
    for pair in range(2):
        high, low = split(wide(values, pair) * wide(weights, pair))
        sums = []
        for block in (2 * pair, 2 * pair + 1):
            upper = wide(halves, block) == 1
            lhs = jnp.concatenate(
                [
                    jnp.where(upper, 0.0, high),
                    jnp.where(upper, 0.0, low),
                    jnp.where(upper, high, 0.0),
                    jnp.where(upper, low, 0.0),
                ],
                axis=0,
            ).astype(BF16)
            part = matmul_nt(lhs, wide(hots, block))
            sums.append(
                jnp.concatenate([part[0:8] + part[8:16], part[16:24] + part[24:32]], axis=1)
            )
        gathered = jnp.where(row < 4, sums[0], sums[1])
        weight_sum = jnp.where(row < 4, gathered[3:4], gathered[7:8])
        speed = jnp.where(row < 4, flow_ref[2 * pair : 2 * pair + 1], flow_ref[2 * pair + 1 : 2 * pair + 2])
        inverse = 1.0 / (speed + scale * weight_sum)
        decays.append(speed * inverse)
        drives.append(scale * gathered * inverse)
    decay = jnp.concatenate(decays, axis=0)
    drive = jnp.concatenate(drives, axis=0)
    drive = drive + jnp.where(lanes_of((16, SEG)) == 0, decay * inflow, 0.0)
    vessel = scan_segments(decay, drive)

    send_ref[0, 32:48] = jnp.zeros((16, 128), F32)
    send_ref[BRICKS - 1, 16:32] = jnp.zeros((16, 128), F32)
    tile_row = rows_of((8, 128))
    scale = species_scale(perm_ref, (8, 128))
    for pair in range(2):
        high, low = split(vessel[8 * pair : 8 * pair + 8])
        lhs = jnp.concatenate(
            [high[:, :128], low[:, :128], high[:, 128:], low[:, 128:]], axis=0
        ).astype(BF16)
        found = [matmul(lhs, wide(hots, block)) for block in (2 * pair, 2 * pair + 1)]
        for t in range(BRICKS):
            at_slot = []
            for i in range(2):
                part = found[i][:, t * 128 : (t + 1) * 128]
                at_slot.append(
                    jnp.where(
                        halves[2 * pair + i, t] == 1,
                        part[16:24] + part[24:32],
                        part[0:8] + part[8:16],
                    )
                )
            vessel_value = jnp.where(tile_row < 4, at_slot[0], at_slot[1])
            flux = scale * weights[pair, t] * (vessel_value - values[pair, t])
            cell = jnp.where(
                tile_row < 4, voxel_ref[2 * pair, t : t + 1, :], voxel_ref[2 * pair + 1, t : t + 1, :]
            )
            cell_row = (tile_row & 3) == 3
            cell_value = cell.astype(F32)
            here = slice(8 * pair, 8 * pair + 8)
            own = jnp.where(cell_row, cell_value, flux)
            first = last = own
            if narrow:
                is_first = ((cell >> 7) & 7) < 4
                first = jnp.where(cell_row | is_first, own, 0.0)
                last = jnp.where(is_first & ~cell_row, 0.0, own)
            send_ref[t, here] = own
            if t > 0:
                send_ref[t - 1, 16 + 8 * pair : 24 + 8 * pair] = first
            if t < BRICKS - 1:
                send_ref[t + 1, 32 + 8 * pair : 40 + 8 * pair] = last
    return vessel


def inlet_column(inlet_ref):
    row = rows_of((16, 1))
    column = jnp.zeros((16, 1), F32)
    for block in range(4):
        for k in range(3):
            column = jnp.where(row == 4 * block + k, inlet_ref[k, block], column)
    return column


def first_solve_kernel(
    place_ref, count_ref, perm_ref, inlet_ref, region_ref, voxel_ref, segment_ref, weight_ref, flow_ref,
    rate_after_ref, rate_before_ref,
    send_ref, ends_ref, around_ref, values, weights, halves, hots,
):
    def brick(t, carry):
        prepare_slots(t, segment_ref, weight_ref, count_ref, weights, halves, hots)
        found = gather_slots(
            split_brick(region_ref[t]), [voxel_ref[block, pl.ds(t, 1), :] for block in range(4)]
        )
        for pair in range(2):
            values[pair, t] = pair_tile([*found[2 * pair], 1.0, *found[2 * pair + 1], 1.0])
        return carry

    lax.fori_loop(0, BRICKS, brick, 0, unroll=4)
    vessel = solve_blocks(
        inlet_column(inlet_ref), values, weights, halves, hots, voxel_ref, flow_ref, perm_ref, send_ref, False
    )
    part, t = place_ref[0], place_ref[1]
    last = vessel[:, SEG - 1 : SEG]
    spot = lanes_of((16, 128)) == part * 16 + rows_of((16, 128))
    ends = jnp.sum(jnp.where(spot, last, 0.0), axis=0, keepdims=True)
    ends_ref[...] = jnp.broadcast_to(ends[None], (PARTS, 8, 128))
    around_ref[0] = jnp.where(t < BRICKS - 1, region_ref[jnp.minimum(t + 1, BRICKS - 1)], 0.0)
    around_ref[1] = jnp.where(t > 0, region_ref[jnp.maximum(t - 1, 0)], 0.0)


def second_solve_kernel(
    upstream_ref, count_ref, perm_ref, inlet_ref, values_ref, voxel_ref, segment_ref, weight_ref, flow_ref,
    send_ref, vessel_ref, values, weights, halves, hots,
):
    def brick(t, carry):
        prepare_slots(t, segment_ref, weight_ref, count_ref, weights, halves, hots)
        spare = (rows_of((8, 128)) & 3) == 3
        for pair in range(2):
            values[pair, t] = jnp.where(spare, 1.0, values_ref[t, 8 * pair : 8 * pair + 8])
        return carry

    lax.fori_loop(0, BRICKS, brick, 0, unroll=4)
    row, lane = rows_of((16, 128)), lanes_of((16, 128))
    picked = jnp.zeros((16, 128), F32)
    for block in range(4):
        feeder = upstream_ref[block]
        device = feeder >> 2
        ends = values_ref[device & 15, 3:4, :]
        spot = (device >> 4) * 16 + (feeder & 3) * 4
        picked = jnp.where(((row >> 2) == block) & (lane == spot + (row & 3)), ends, picked)
    inflow = 0.5 * (inlet_column(inlet_ref) + jnp.sum(picked, axis=1, keepdims=True))
    vessel = solve_blocks(
        inflow, values, weights, halves, hots, voxel_ref, flow_ref, perm_ref, send_ref, True
    )
    for block in range(4):
        for k in range(3):
            vessel_ref[k, block : block + 1, :] = vessel[4 * block + k : 4 * block + k + 1]


def scatter_slots(recv_ref, source, groups):
    source[...] = jnp.zeros((len(groups), 192, 128), F32)
    zero = jnp.zeros((16, 128), BF16)

    def senders(i, carry):
        for j, tiles in enumerate(groups):
            hots, parts = [], []
            for q in range(SENDERS):
                s = i * SENDERS + q
                for start in tiles:
                    for base in (start, start + 4):
                        cell = recv_ref[s, base + 3 : base + 4, :].astype(jnp.int32)
                        hots.append(onehot(cell & 127, 128))
                        here = matches(cell >> 7, 32)
                        highs, lows = [], []
                        for k in range(3):
                            flux = jnp.broadcast_to(recv_ref[s, base + k : base + k + 1, :], (16, 128))
                            high = flux.astype(BF16)
                            low = (flux - high.astype(F32)).astype(BF16)
                            highs += [jnp.where(hit, high, zero) for hit in here]
                            lows += [jnp.where(hit, low, zero) for hit in here]
                        parts.append(jnp.concatenate(highs + lows, axis=0))
            source[j] += matmul_nt(jnp.concatenate(parts, axis=1), jnp.concatenate(hots, axis=1))
        return carry

    lax.fori_loop(0, BRICKS // SENDERS, senders, 0, unroll=2)
    return [source[j, 0:96] + source[j, 96:192] for j in range(len(groups))]


def planes(value):
    return value.reshape(3, 4, 8, 128)


def write_messages(tissues, sources, up_ref, down_ref):
    for i, (value, source) in enumerate(zip(tissues, sources)):
        here = slice(8 * i, 8 * i + 8)
        value, source = planes(value), planes(source)
        up_ref[:, 0:4, here] = value
        down_ref[:, 0:4, here] = value
        up_ref[:, 4:7, here] = source[:, 1:4]
        down_ref[:, 4:7, here] = source[:, 0:3]


def first_scatter_kernel(
    recv_ref, tissue_ref, around_ref, rate_ref, rate_after_ref, rate_before_ref, ends_ref,
    up_ref, down_ref, sources_ref, ends_row_ref, scratch,
):
    sources = scatter_slots(recv_ref, scratch, ((0, 8), (16, 24), (32, 40)))
    for i in range(3):
        sources_ref[i] = sources[i]
    write_messages((tissue_ref[...], around_ref[0], around_ref[1]), sources, up_ref, down_ref)
    for i, ref in enumerate((rate_ref, rate_after_ref, rate_before_ref)):
        here = slice(8 * i, 8 * i + 8)
        value = planes(ref[...])
        up_ref[:, 7:10, here] = value[:, 1:4]
        down_ref[:, 7:10, here] = value[:, 0:3]
    ends = ends_ref[0]
    for part in range(1, PARTS):
        ends = ends + ends_ref[part]
    ends_row_ref[...] = ends


def second_scatter_kernel(recv_ref, tissue_ref, around_ref, up_ref, down_ref, sources_ref, scratch):
    sources = scatter_slots(recv_ref, scratch, ((0, 8), (16, 24, 32, 40)))
    for i in range(2):
        sources_ref[i] = sources[i]
    write_messages((tissue_ref[...], around_ref[...]), sources, up_ref, down_ref)


def fill(now, source, below, above, tissues, sources):
    for k in range(3):
        now[k, 0:4] = below[k, 0:4]
        now[k, 8:12] = above[k, 0:4]
        source[k, 1:4] = below[k, 4:7]
        source[k, 8:11] = above[k, 4:7]
        for i in range(len(tissues)):
            now[k, 4:8, 8 * i : 8 * i + 8] = planes(tissues[i])[k]
            source[k, 4:8, 8 * i : 8 * i + 8] = planes(sources[i])[k]


def run_sweeps(now, later, source, inverse, produced):
    count = now.shape[2]
    lane = lanes_of((count, 128))
    old, new = now, later
    for sweep in range(1, SWEEPS + 1):
        for k in range(3):
            for z in range(sweep, 12 - sweep):
                middle = old[k, z]
                total = old[k, z - 1] + old[k, z + 1]
                total = total + pltpu.roll(middle, 1, 0) + pltpu.roll(middle, count - 1, 0)
                total = total + jnp.where(lane > 0, pltpu.roll(middle, 1, 1), 0.0)
                total = total + jnp.where(lane < 127, pltpu.roll(middle, 127, 1), 0.0)
                total = source[k, z] + DIFFUSION[k] * total
                if k == 2:
                    total = total + produced[z] * old[1, z]
                new[k, z] = total * inverse[k, z]
        old, new = new, old
    return old


def beside(after, before):
    low = lax.broadcasted_iota(jnp.int32, after.shape, after.ndim - 2) < 4
    return jnp.where(low, after, before)


def first_sweeps_kernel(
    place_ref, below, above, tissue_ref, around_ref, sources_ref, rate_own, rate_after, rate_before, recv_ref, ends_ref,
    out_ref, side_ref, inverse_ref, produced_ref, send_ref, now, later, source, inverse, produced,
):
    part, t = place_ref[0], place_ref[1]
    row = rows_of((24, 128))
    row_inside = (row < 8) | ((row < 16) & (t < BRICKS - 1)) | ((row >= 16) & (t > 0))
    inside = jnp.where(row_inside, 1.0, 0.0)
    lower = jnp.where(part > 0, inside, 0.0)
    upper = jnp.where(part < PARTS - 1, inside, 0.0)
    fill(now, source, below, above, [tissue_ref[...], around_ref[0], around_ref[1]], [sources_ref[i] for i in range(3)])
    for k in range(3):
        rates = [planes(ref[...])[k] for ref in (rate_own, rate_after, rate_before)]
        for z in range(1, 11):
            if z < 4:
                rate, valid = below[k, z + 6], lower
            elif z < 8:
                rate, valid = jnp.concatenate([value[z - 4] for value in rates], axis=0), inside
            else:
                rate, valid = above[k, z - 1], upper
            value = valid / (6.0 * DIFFUSION[k] + rate)
            inverse[k, z] = value
            inverse_ref[k, z, 0:8] = value[0:8]
            inverse_ref[k, z, 8:16] = beside(value[8:16], value[16:24])
            if k == 1:
                rate = 2.0 * rate
                produced[z] = rate
                produced_ref[z, 0:8] = rate[0:8]
                produced_ref[z, 8:16] = beside(rate[8:16], rate[16:24])
    final = run_sweeps(now, later, source, inverse, produced)
    brick = final[:, 4:8, 0:8].reshape(96, 128)
    out_ref[...] = brick
    side_ref[...] = beside(final[:, 4:8, 8:16], final[:, 4:8, 16:24]).reshape(96, 128)
    brick_split = split_brick(brick)
    ends = ends_ref[0:1]

    def receiver(s, carry):
        cells = [recv_ref[s, 4 * b + 3 : 4 * b + 4, :].astype(jnp.int32) for b in range(4)]
        found = gather_slots(brick_split, cells)
        for pair in range(2):
            send_ref[s, 8 * pair : 8 * pair + 8] = pair_tile(
                [*found[2 * pair], ends, *found[2 * pair + 1], ends]
            )
        return carry

    lax.fori_loop(0, BRICKS, receiver, 0, unroll=4)


def second_sweeps_kernel(
    below, above, tissue_ref, side_ref, sources_ref, inverse, produced, out_ref, now, later, source
):
    fill(now, source, below, above, [tissue_ref[...], side_ref[...]], [sources_ref[i] for i in range(2)])
    final = run_sweeps(now, later, source, inverse, produced)
    out_ref[...] = final[:, 4:8, 0:8]


def call(kernel, name, outs, args, scalars, scratch):
    whole = pl.BlockSpec(memory_space=pltpu.VMEM)
    scalar = pl.BlockSpec(memory_space=pltpu.SMEM)
    return pl.pallas_call(
        kernel,
        out_shape=[jax.ShapeDtypeStruct(shape, F32) for shape in outs],
        in_specs=[scalar] * scalars + [whole] * (len(args) - scalars),
        out_specs=[whole] * len(outs),
        scratch_shapes=scratch,
        compiler_params=pltpu.CompilerParams(vmem_limit_bytes=VMEM_LIMIT),
        name=name,
    )(*args)


def shards(
    tissue_start,
    consumption,
    inlet,
    flow,
    permeability,
    intersection_count,
    intersection_segment,
    intersection_voxel,
    intersection_weight,
    upstream,
):
    place = jnp.stack([lax.axis_index("vessel"), lax.axis_index("tissue")]).astype(jnp.int32)
    tissue = tissue_start.reshape(96, 128)
    rate = consumption.reshape(96, 128)

    def exchange(value, axis):
        return lax.all_to_all(value, axis, 0, 0, tiled=True)

    def shift(value, axis, step):
        size = lax.axis_size(axis)
        pairs = [(i, i + step) for i in range(size) if 0 <= i + step < size]
        return lax.ppermute(value, axis, pairs)

    solve_scratch = [
        pltpu.VMEM((2, BRICKS, 8, 128), F32),
        pltpu.VMEM((2, BRICKS, 8, 128), F32),
        pltpu.VMEM((4, BRICKS, 8, 128), jnp.int32),
        pltpu.VMEM((4, BRICKS, 128, 128), BF16),
    ]
    wide, ring = (3, 12, 24, 128), (3, 12, 16, 128)
    slots = (intersection_voxel, intersection_segment, intersection_weight, flow)

    bricks = jnp.broadcast_to(tissue[None], (BRICKS, 96, 128))
    rate_after = shift(rate, "tissue", -1)
    rate_before = shift(rate, "tissue", 1)
    region = exchange(bricks, "tissue")
    send, ends, around = call(
        first_solve_kernel,
        "first_solve",
        [(BRICKS, 48, 128), (PARTS, 8, 128), (2, 96, 128)],
        [place, intersection_count, permeability, inlet, region, *slots, rate_after, rate_before],
        4,
        solve_scratch,
    )
    received = exchange(send, "tissue")
    ends = exchange(ends, "vessel")
    up, down, sources, ends_row = call(
        first_scatter_kernel,
        "first_scatter",
        [(3, 10, 24, 128), (3, 10, 24, 128), (3, 96, 128), (8, 128)],
        [received, tissue, around, rate, rate_after, rate_before, ends],
        0,
        [pltpu.VMEM((3, 192, 128), F32)],
    )
    below = shift(up, "vessel", 1)
    above = shift(down, "vessel", -1)
    tissue, side, inverse, produced, send = call(
        first_sweeps_kernel,
        "first_sweeps",
        [(96, 128), (96, 128), ring, ring[1:], (BRICKS, 16, 128)],
        [place, below, above, tissue, around, sources, rate, rate_after, rate_before, received, ends_row],
        1,
        [pltpu.VMEM(wide, F32)] * 4 + [pltpu.VMEM(wide[1:], F32)],
    )
    values = exchange(send, "tissue")
    send, vessel = call(
        second_solve_kernel,
        "second_solve",
        [(BRICKS, 48, 128), (3, 4, SEG)],
        [upstream, intersection_count, permeability, inlet, values, *slots],
        4,
        solve_scratch,
    )
    received = exchange(send, "tissue")
    up, down, sources = call(
        second_scatter_kernel,
        "second_scatter",
        [(3, 7, 16, 128), (3, 7, 16, 128), (2, 96, 128)],
        [received, tissue, side],
        0,
        [pltpu.VMEM((2, 192, 128), F32)],
    )
    below = shift(up, "vessel", 1)
    above = shift(down, "vessel", -1)
    (tissue,) = call(
        second_sweeps_kernel,
        "second_sweeps",
        [(3, 4, 8, 128)],
        [below, above, tissue, side, sources, inverse, produced],
        0,
        [pltpu.VMEM(ring, F32)] * 3,
    )
    return tissue, vessel


def solution(mesh):
    return jax.shard_map(
        shards,
        mesh=mesh,
        in_specs=(
            P(None, "vessel", "tissue", None),
            P(None, "vessel", "tissue", None),
            P(None, ("vessel", "tissue")),
            P(("vessel", "tissue"), None),
            P(),
            P(("vessel", "tissue"), None),
            P(("vessel", "tissue"), None, None),
            P(("vessel", "tissue"), None, None),
            P(("vessel", "tissue"), None, None),
            P(("vessel", "tissue")),
        ),
        out_specs=(P(None, "vessel", "tissue", None), P(None, ("vessel", "tissue"), None)),
        check_vma=False,
    )
```

time: 129 us -> 110 us (0.85)
  Pallas kernels: 32.3 us -> 15.9 us
  starting transfers between devices: 32.1 us -> 25.3 us
  blocking collectives: 39.6 us -> 45.5 us
  waiting for transfers between devices: 21.7 us -> 20.2 us
    pallas_call x6, Pallas kernels: 32.3 us -> 15.9 us  [call(): pl.pallas_call(kernel, out_shape=[jax.ShapeDtypeStruct(shape, F32) for sh...]
    all_to_all x2 -> x1, waiting for transfers between devices: 13.1 us -> 2.26 us  [exchange(): return lax.all_to_all(value, axis, 0, 0, tiled=True)]
    ppermute x6, waiting for transfers between devices: 8.63 us -> 17.9 us  [shift(): return lax.ppermute(value, axis, pairs)]
    all_to_all x3 -> x4, blocking collectives: 39.6 us -> 45.5 us  [exchange(): return lax.all_to_all(value, axis, 0, 0, tiled=True)]
    all_to_all x2 -> x1, starting transfers between devices: 11.7 us -> 7.73 us  [exchange(): return lax.all_to_all(value, axis, 0, 0, tiled=True)]
    ppermute x6, starting transfers between devices: 20.4 us -> 17.6 us  [shift(): return lax.ppermute(value, axis, pairs)]
  transfers between devices with their start and end apart: 8 -> 7, of which waited for: 5 -> 7; matrix products, arithmetic and copies ran while one was open for 0% -> 0% of each run, Pallas kernels for 0% -> 0%
where the time goes in v2:
time: 110 us
  blocking collectives  45.5 us (41%)
  starting transfers between devices  25.3 us (23%)
  waiting for transfers between devices  20.2 us (18%)
  Pallas kernels  15.9 us (14%)
  local copies, waits for them, and re-layouts  1.82 us (2%)
    all_to_all x4, blocking collectives, exchange(): return lax.all_to_all(value, axis, 0, 0, tiled=True)  45.5 us
    ppermute x6, waiting for transfers between devices, shift(): return lax.ppermute(value, axis, pairs)  17.9 us
    ppermute x6, starting transfers between devices, shift(): return lax.ppermute(value, axis, pairs)  17.6 us
    pallas_call x6, Pallas kernels, call(): pl.pallas_call(kernel, out_shape=[jax.ShapeDtypeStruct(shape, F32) for sh...  15.9 us
    all_to_all x1, starting transfers between devices, exchange(): return lax.all_to_all(value, axis, 0, 0, tiled=True)  7.73 us
    all_to_all x1, waiting for transfers between devices, exchange(): return lax.all_to_all(value, axis, 0, 0, tiled=True)  2.26 us
  transfers between devices with their start and end apart: 7, of which 7 were waited for; matrix products, arithmetic and copies ran while one was open for 0% of the time, Pallas kernels for 0%

profile of v2, /device:TPU:1, one launch (start us, length us, event | category | flops | bytes accessed | tf_op | source)
XLA Modules:
  0.0 109.6 jit_solution(5813628389767468509)
XLA Ops:
  0.6 1.8 %broadcast_in_dim.8 = f32[16,96,128]{2,1,0:T(8,128)} broadcast(f32[96,128]{1,0:T(8,128)} %bitcast.4), dimensions={1,2} | broadcast | bytes 835584 | tf_op jit(solution)/shard_map/broadcast_in_dim | solution.py:467
  2.4 0.0 copy-start.1
  2.4 0.0 copy-start.2
  2.4 0.0 copy-start.3
  2.4 0.0 copy-start.4
  2.4 0.0 copy-start.7
  2.4 7.7 %all-to-all-start = ((f32[16,96,128]{2,1,0:T(8,128)}), f32[16,96,128]{2,1,0:T(8,128)S(1)}, u32[]{:S(2)}, u32[]{:S(2)}) async-start(f32[16,96,128]{2,1,0:T(8,128)} %broadcast_in_dim.8), calls=%async_computation | async-start | bytes 1572864 | tf_op jit(solution)/shard_map/all_to_all | solution.py:451
  10.2 0.0 copy-done.1
  10.2 3.3 %collective-permute-start.1 = (f32[96,128]{1,0:T(8,128)S(1)}, f32[96,128]{1,0:T(8,128)S(1)}, u32[]{:S(2)}, u32[]{:S(2)}) collective-permute-start(f32[96,128]{1,0:T(8,128)S(1)} %bitcast.7), channel_id=1, source_target_pairs={{0,1},{1,2},{2,3},{3,4},{4,5},{5,6},{6,7},{7,8},{8,9},{9,10},{10,1... | collective-permute-start | bytes 147464 | tf_op jit(solution)/shard_map/ppermute | solution.py:456
  13.4 1.3 %collective-permute-start = (f32[96,128]{1,0:T(8,128)S(1)}, f32[96,128]{1,0:T(8,128)S(1)}, u32[]{:S(2)}, u32[]{:S(2)}) collective-permute-start(f32[96,128]{1,0:T(8,128)S(1)} %bitcast.8), channel_id=1, source_target_pairs={{1,0},{2,1},{3,2},{4,3},{5,4},{6,5},{7,6},{8,7},{9,8},{10,9},{11,1... | collective-permute-start | bytes 147464 | tf_op jit(solution)/shard_map/ppermute | solution.py:456
  14.7 0.0 copy-start.5
  14.8 0.0 copy-start.6
  14.8 0.0 copy-start.8
  14.8 0.1 pad_add_fusion.place_ref
  14.9 4.3 %collective-permute-done.1.rate_before_ref.rate_before = f32[96,128]{1,0:T(8,128)S(1)} collective-permute-done((f32[96,128]{1,0:T(8,128)S(1)}, f32[96,128]{1,0:T(8,128)S(1)}, u32[]{:S(2)}, u32[]{:S(2)}) %collective-permute-start.1) | collective-permute-done | bytes 49184 | tf_op jit(solution)/shard_map/ppermute | solution.py:456
  19.1 1.9 %collective-permute-done.rate_after_ref.rate_after = f32[96,128]{1,0:T(8,128)S(1)} collective-permute-done((f32[96,128]{1,0:T(8,128)S(1)}, f32[96,128]{1,0:T(8,128)S(1)}, u32[]{:S(2)}, u32[]{:S(2)}) %collective-permute-start) | collective-permute-done | bytes 49184 | tf_op jit(solution)/shard_map/ppermute | solution.py:456
  21.1 2.3 %all-to-all-done.region_ref = f32[16,96,128]{2,1,0:T(8,128)S(1)} async-done(((f32[16,96,128]{2,1,0:T(8,128)}), f32[16,96,128]{2,1,0:T(8,128)S(1)}, u32[]{:S(2)}, u32[]{:S(2)}) %all-to-all-start) | async-done | bytes 786464 | tf_op jit(solution)/shard_map/all_to_all | solution.py:451
  23.3 0.0 copy-done.2
  23.3 0.0 copy-done.3
  23.3 0.0 copy-done.4
  23.3 0.0 copy-done.7
  23.4 0.0 copy-done.5
  23.4 0.0 copy-done.6
  23.4 0.0 copy-done.8
  23.4 3.6 %first_solve.1 = (f32[16,48,128]{2,1,0:T(8,128)S(1)}, f32[8,8,128]{2,1,0:T(8,128)S(1)}, f32[2,96,128]{2,1,0:T(8,128)S(1)}) custom-call(s32[2]{0:T(128)S(1)} %pad_add_fusion.place_ref, s32[4,16]{1,0:T(4,128)S(1)} %copy-done.6, f32[3]{0:T(128)S(1)} %copy-done.8, f32[3,4]{1,0:T(4,128)S(1)} %copy-done.7, f32[16,96,128]{2,1,0:T(8,128)S(1)} %all-to-all-done.region_ref, ...), custom_call_target="tpu_custom_call" | custom-call | tf_op jit(solution)/shard_map/first_solve/pallas_call | solution.py:423
  27.0 12.5 %all_to_all.25.ends_ref = f32[8,8,128]{2,1,0:T(8,128)S(1)} all-to-all(f32[8,8,128]{2,1,0:T(8,128)S(1)} %get-tuple-element.21), channel_id=1, replica_groups=mesh['vessel'=8,'tissue'=16] {'vessel'}, dimensions={0} | all-to-all | bytes 65536 | tf_op jit(solution)/shard_map/all_to_all | solution.py:451
  39.5 0.0 copy-start
  39.5 12.5 %all_to_all.26.recv_ref = f32[16,48,128]{2,1,0:T(8,128)S(1)} all-to-all(f32[16,48,128]{2,1,0:T(8,128)S(1)} %get-tuple-element.19), channel_id=1, replica_groups=mesh['vessel'=8,'tissue'=16] {'tissue'}, dimensions={0} | all-to-all | bytes 786432 | tf_op jit(solution)/shard_map/all_to_all | solution.py:451
  52.0 0.0 copy-done
  52.0 2.9 %first_scatter.1 = (f32[3,10,24,128]{3,2,1,0:T(8,128)S(1)}, f32[3,10,24,128]{3,2,1,0:T(8,128)S(1)}, f32[3,96,128]{2,1,0:T(8,128)S(1)}, f32[8,128]{1,0:T(8,128)S(1)}) custom-call(f32[16,48,128]{2,1,0:T(8,128)S(1)} %all_to_all.26.recv_ref, f32[96,128]{1,0:T(8,128)S(1)} %bitcast.5, f32[2,96,128]{2,1,0:T(8,128)S(1)} %get-tuple-element.20.around_ref, ...), custom_call_target="tpu_custom_call" | custom-call | tf_op jit(solution)/shard_map/first_scatter/pallas_call | solution.py:423
  54.9 4.0 %collective-permute-start.2 = (f32[3,10,24,128]{3,2,1,0:T(8,128)S(1)}, f32[3,10,24,128]{3,2,1,0:T(8,128)S(1)}, u32[]{:S(2)}, u32[]{:S(2)}) collective-permute-start(f32[3,10,24,128]{3,2,1,0:T(8,128)S(1)} %get-tuple-element.22), channel_id=1, source_target_pairs={{0,16},{16,32},{32,48},{48,64},{64,80},{80,96},{96,112},{1,17},{17... | collective-permute-start | bytes 1105928 | tf_op jit(solution)/shard_map/ppermute | solution.py:456
  58.9 1.9 %collective-permute-start.3 = (f32[3,10,24,128]{3,2,1,0:T(8,128)S(1)}, f32[3,10,24,128]{3,2,1,0:T(8,128)S(1)}, u32[]{:S(2)}, u32[]{:S(2)}) collective-permute-start(f32[3,10,24,128]{3,2,1,0:T(8,128)S(1)} %get-tuple-element.23), channel_id=1, source_target_pairs={{16,0},{32,16},{48,32},{64,48},{80,64},{96,80},{112,96},{17,1},{33... | collective-permute-start | bytes 1105928 | tf_op jit(solution)/shard_map/ppermute | solution.py:456
  60.8 2.5 %collective-permute-done.2.below = f32[3,10,24,128]{3,2,1,0:T(8,128)S(1)} collective-permute-done((f32[3,10,24,128]{3,2,1,0:T(8,128)S(1)}, f32[3,10,24,128]{3,2,1,0:T(8,128)S(1)}, u32[]{:S(2)}, u32[]{:S(2)}) %collective-permute-start.2) | collective-permute-done | bytes 368672 | tf_op jit(solution)/shard_map/ppermute | solution.py:456
  63.3 4.4 %collective-permute-done.3.above = f32[3,10,24,128]{3,2,1,0:T(8,128)S(1)} collective-permute-done((f32[3,10,24,128]{3,2,1,0:T(8,128)S(1)}, f32[3,10,24,128]{3,2,1,0:T(8,128)S(1)}, u32[]{:S(2)}, u32[]{:S(2)}) %collective-permute-start.3) | collective-permute-done | bytes 368672 | tf_op jit(solution)/shard_map/ppermute | solution.py:456
  67.7 2.6 %first_sweeps.1 = (f32[96,128]{1,0:T(8,128)S(1)}, f32[96,128]{1,0:T(8,128)S(1)}, f32[3,12,16,128]{3,2,1,0:T(8,128)S(1)}, f32[12,16,128]{2,1,0:T(8,128)S(1)}, f32[16,16,128]{2,1,0:T(8,128)S(1)}) custom-call(s32[2]{0:T(128)S(1)} %pad_add_fusion.place_ref, f32[3,10,24,128]{3,2,1,0:T(8,128)S(1)} %collective-permute-done.2.below, ...), custom_call_target="tpu_custom_call" | custom-call | tf_op jit(solution)/shard_map/first_sweeps/pallas_call | solution.py:423
  70.3 0.0 copy-start.9
  70.3 9.5 %all_to_all.27.values_ref = f32[16,16,128]{2,1,0:T(8,128)S(1)} all-to-all(f32[16,16,128]{2,1,0:T(8,128)S(1)} %get-tuple-element.26), channel_id=1, replica_groups=mesh['vessel'=8,'tissue'=16] {'tissue'}, dimensions={0} | all-to-all | bytes 262144 | tf_op jit(solution)/shard_map/all_to_all | solution.py:451
  79.8 0.0 copy-done.9
  79.8 3.0 %second_solve.1 = (f32[16,48,128]{2,1,0:T(8,128)S(1)}, f32[3,4,256]{2,1,0:T(4,128)}) custom-call(s32[4]{0:T(128)S(1)} %copy-done.9, s32[4,16]{1,0:T(4,128)S(1)} %copy-done.6, f32[3]{0:T(128)S(1)} %copy-done.8, f32[3,4]{1,0:T(4,128)S(1)} %copy-done.7, f32[16,16,128]{2,1,0:T(8,128)S(1)} %all_to_all.27.values_ref, s32[4,16,128]{2,1,0:T(8,128)S(1)} %copy-done.2, ...), custom_call_target="tpu_custom_call" | custom-call | tf_op jit(solution)/shard_map/second_solve/pallas_call | solution.py:423
  82.7 11.0 %all_to_all.28.recv_ref = f32[16,48,128]{2,1,0:T(8,128)S(1)} all-to-all(f32[16,48,128]{2,1,0:T(8,128)S(1)} %get-tuple-element.27), channel_id=1, replica_groups=mesh['vessel'=8,'tissue'=16] {'tissue'}, dimensions={0} | all-to-all | bytes 786432 | tf_op jit(solution)/shard_map/all_to_all | solution.py:451
  93.8 2.8 %second_scatter.1 = (f32[3,7,16,128]{3,2,1,0:T(8,128)S(1)}, f32[3,7,16,128]{3,2,1,0:T(8,128)S(1)}, f32[2,96,128]{2,1,0:T(8,128)S(1)}) custom-call(f32[16,48,128]{2,1,0:T(8,128)S(1)} %all_to_all.28.recv_ref, f32[96,128]{1,0:T(8,128)S(1)} %get-tuple-element.28.tissue_ref, f32[96,128]{1,0:T(8,128)S(1)} %get-tuple-element.29.around_ref.side_ref), custom_call_target="tpu_custom_call" | custom-call | tf_op jit(solution)/shard_map/second_scatter/pallas_call | solution.py:423
  96.6 5.2 %collective-permute-start.4 = (f32[3,7,16,128]{3,2,1,0:T(8,128)S(1)}, f32[3,7,16,128]{3,2,1,0:T(8,128)S(1)}, u32[]{:S(2)}, u32[]{:S(2)}) collective-permute-start(f32[3,7,16,128]{3,2,1,0:T(8,128)S(1)} %get-tuple-element.30), channel_id=1, source_target_pairs={{0,16},{16,32},{32,48},{48,64},{64,80},{80,96},{96,112},{1,17},{17... | collective-permute-start | bytes 516104 | tf_op jit(solution)/shard_map/ppermute | solution.py:456
  101.8 1.9 %collective-permute-start.5 = (f32[3,7,16,128]{3,2,1,0:T(8,128)S(1)}, f32[3,7,16,128]{3,2,1,0:T(8,128)S(1)}, u32[]{:S(2)}, u32[]{:S(2)}) collective-permute-start(f32[3,7,16,128]{3,2,1,0:T(8,128)S(1)} %get-tuple-element.31), channel_id=1, source_target_pairs={{16,0},{32,16},{48,32},{64,48},{80,64},{96,80},{112,96},{17,1},{33... | collective-permute-start | bytes 516104 | tf_op jit(solution)/shard_map/ppermute | solution.py:456
  103.7 0.4 collective-permute-done.4.below
  104.1 4.4 %collective-permute-done.5.above = f32[3,7,16,128]{3,2,1,0:T(8,128)S(1)} collective-permute-done((f32[3,7,16,128]{3,2,1,0:T(8,128)S(1)}, f32[3,7,16,128]{3,2,1,0:T(8,128)S(1)}, u32[]{:S(2)}, u32[]{:S(2)}) %collective-permute-start.5) | collective-permute-done | bytes 172064 | tf_op jit(solution)/shard_map/ppermute | solution.py:456
  108.5 1.1 second_sweeps.1
Async XLA Ops:
  2.4 7.8 %copy-start.1 = (f32[3,4,8,128]{3,2,1,0:T(8,128)S(1)}, f32[3,4,8,128]{3,2,1,0:T(8,128)}, u32[]{:S(2)}) copy-start(f32[3,4,8,128]{3,2,1,0:T(8,128)} %param.11) | copy-start | bytes 147460
  2.4 20.9 %copy-start.2 = (s32[4,16,128]{2,1,0:T(8,128)S(1)}, s32[4,16,128]{2,1,0:T(8,128)}, u32[]{:S(2)}) copy-start(s32[4,16,128]{2,1,0:T(8,128)} %voxel_ref.3) | copy-start | bytes 98308
  2.4 20.9 %copy-start.3 = (s32[4,16,128]{2,1,0:T(8,128)S(1)}, s32[4,16,128]{2,1,0:T(8,128)}, u32[]{:S(2)}) copy-start(s32[4,16,128]{2,1,0:T(8,128)} %segment_ref.3) | copy-start | bytes 98308
  2.4 20.9 %copy-start.4 = (f32[4,16,128]{2,1,0:T(8,128)S(1)}, f32[4,16,128]{2,1,0:T(8,128)}, u32[]{:S(2)}) copy-start(f32[4,16,128]{2,1,0:T(8,128)} %weight_ref.3) | copy-start | bytes 98308
  2.4 20.9 %copy-start.7 = (f32[3,4]{1,0:T(4,128)S(1)}, f32[3,4]{1,0:T(4,128)}, u32[]{:S(2)}) copy-start(f32[3,4]{1,0:T(4,128)} %inlet_ref.3) | copy-start | bytes 148
  2.4 20.9 %all-to-all-start = ((f32[16,96,128]{2,1,0:T(8,128)}), f32[16,96,128]{2,1,0:T(8,128)S(1)}, u32[]{:S(2)}, u32[]{:S(2)}) async-start(f32[16,96,128]{2,1,0:T(8,128)} %broadcast_in_dim.8), calls=%async_computation | async-start | bytes 1572864 | tf_op jit(solution)/shard_map/all_to_all | solution.py:451
  10.2 9.0 %collective-permute-start.1 = (f32[96,128]{1,0:T(8,128)S(1)}, f32[96,128]{1,0:T(8,128)S(1)}, u32[]{:S(2)}, u32[]{:S(2)}) collective-permute-start(f32[96,128]{1,0:T(8,128)S(1)} %bitcast.7), channel_id=1, source_target_pairs={{0,1},{1,2},{2,3},{3,4},{4,5},{5,6},{6,7},{7,8},{8,9},{9,10},{10,1... | collective-permute-start | bytes 147464 | tf_op jit(solution)/shard_map/ppermute | solution.py:456
  13.4 7.6 %collective-permute-start = (f32[96,128]{1,0:T(8,128)S(1)}, f32[96,128]{1,0:T(8,128)S(1)}, u32[]{:S(2)}, u32[]{:S(2)}) collective-permute-start(f32[96,128]{1,0:T(8,128)S(1)} %bitcast.8), channel_id=1, source_target_pairs={{1,0},{2,1},{3,2},{4,3},{5,4},{6,5},{7,6},{8,7},{9,8},{10,9},{11,1... | collective-permute-start | bytes 147464 | tf_op jit(solution)/shard_map/ppermute | solution.py:456
  14.7 8.6 %copy-start.5 = (f32[4,256]{1,0:T(4,128)S(1)}, f32[4,256]{1,0:T(4,128)}, u32[]{:S(2)}) copy-start(f32[4,256]{1,0:T(4,128)} %flow_ref.3) | copy-start | bytes 12292
  14.8 8.6 %copy-start.6 = (s32[4,16]{1,0:T(4,128)S(1)}, s32[4,16]{1,0:T(4,128)}, u32[]{:S(2)}) copy-start(s32[4,16]{1,0:T(4,128)} %count_ref.3) | copy-start | bytes 772
  14.8 8.6 %copy-start.8 = (f32[3]{0:T(128)S(1)}, f32[3]{0:T(128)}, u32[]{:S(2)}) copy-start(f32[3]{0:T(128)} %perm_ref.3) | copy-start | bytes 40
  39.5 12.5 %copy-start = (f32[3,4,8,128]{3,2,1,0:T(8,128)S(1)}, f32[3,4,8,128]{3,2,1,0:T(8,128)}, u32[]{:S(2)}) copy-start(f32[3,4,8,128]{3,2,1,0:T(8,128)} %param.10) | copy-start | bytes 147460
  54.9 8.5 %collective-permute-start.2 = (f32[3,10,24,128]{3,2,1,0:T(8,128)S(1)}, f32[3,10,24,128]{3,2,1,0:T(8,128)S(1)}, u32[]{:S(2)}, u32[]{:S(2)}) collective-permute-start(f32[3,10,24,128]{3,2,1,0:T(8,128)S(1)} %get-tuple-element.22), channel_id=1, source_target_pairs={{0,16},{16,32},{32,48},{48,64},{64,80},{80,96},{96,112},{1,17},{17... | collective-permute-start | bytes 1105928 | tf_op jit(solution)/shard_map/ppermute | solution.py:456
  58.9 8.8 %collective-permute-start.3 = (f32[3,10,24,128]{3,2,1,0:T(8,128)S(1)}, f32[3,10,24,128]{3,2,1,0:T(8,128)S(1)}, u32[]{:S(2)}, u32[]{:S(2)}) collective-permute-start(f32[3,10,24,128]{3,2,1,0:T(8,128)S(1)} %get-tuple-element.23), channel_id=1, source_target_pairs={{16,0},{32,16},{48,32},{64,48},{80,64},{96,80},{112,96},{17,1},{33... | collective-permute-start | bytes 1105928 | tf_op jit(solution)/shard_map/ppermute | solution.py:456
  70.3 9.5 %copy-start.9 = (s32[4]{0:T(128)S(1)}, s32[4]{0:T(128)}, u32[]{:S(2)}) copy-start(s32[4]{0:T(128)} %upstream_ref.1) | copy-start | bytes 52
  96.6 7.5 %collective-permute-start.4 = (f32[3,7,16,128]{3,2,1,0:T(8,128)S(1)}, f32[3,7,16,128]{3,2,1,0:T(8,128)S(1)}, u32[]{:S(2)}, u32[]{:S(2)}) collective-permute-start(f32[3,7,16,128]{3,2,1,0:T(8,128)S(1)} %get-tuple-element.30), channel_id=1, source_target_pairs={{0,16},{16,32},{32,48},{48,64},{64,80},{80,96},{96,112},{1,17},{17... | collective-permute-start | bytes 516104 | tf_op jit(solution)/shard_map/ppermute | solution.py:456
  101.8 6.7 %collective-permute-start.5 = (f32[3,7,16,128]{3,2,1,0:T(8,128)S(1)}, f32[3,7,16,128]{3,2,1,0:T(8,128)S(1)}, u32[]{:S(2)}, u32[]{:S(2)}) collective-permute-start(f32[3,7,16,128]{3,2,1,0:T(8,128)S(1)} %get-tuple-element.31), channel_id=1, source_target_pairs={{16,0},{32,16},{48,32},{64,48},{80,64},{96,80},{112,96},{17,1},{33... | collective-permute-start | bytes 516104 | tf_op jit(solution)/shard_map/ppermute | solution.py:456

commit v3 on v2

v3 whole, which is shorter than its diff:
```python
import jax
import jax.numpy as jnp
from jax import lax
from jax.experimental import pallas as pl
from jax.experimental.pallas import tpu as pltpu
from jax.sharding import PartitionSpec as P


SEG = 256
SWEEPS = 4
DIFFUSION = (1.0, 0.7, 0.7)
BRICKS = 16
PARTS = 8
F32 = jnp.float32
BF16 = jnp.bfloat16
VMEM_LIMIT = 16 * 1024 * 1024
SENDERS = 4
SCAN_STEPS = 8
WEIGHTS, CELLS, TABLES = 0, 2, 4
DECAY, GAIN, SCALE, INLET = 8, 9, 10, 11


def rows_of(shape):
    return lax.broadcasted_iota(jnp.int32, shape, 0)


def lanes_of(shape):
    return lax.broadcasted_iota(jnp.int32, shape, 1)


def matmul(lhs, rhs):
    return lax.dot_general(lhs, rhs, (((1,), (0,)), ((), ())), preferred_element_type=F32)


def matmul_nt(lhs, rhs):
    return lax.dot_general(lhs, rhs, (((1,), (1,)), ((), ())), preferred_element_type=F32)


def split(value):
    high = value.astype(BF16).astype(F32)
    return high, value - high


def packed(row):
    return jnp.broadcast_to(row, (16, 128)).astype(F32).astype(BF16)


def matches(index, size):
    row = rows_of((16, 128)).astype(F32).astype(BF16)
    wanted = packed(index)
    return [row + BF16(i) == wanted for i in range(0, size, 16)]


def onehot(index, size):
    one, zero = jnp.ones((16, 128), BF16), jnp.zeros((16, 128), BF16)
    return jnp.concatenate([jnp.where(hit, one, zero) for hit in matches(index, size)], axis=0)


def split_brick(brick):
    high, low = split(brick)
    return jnp.concatenate([high, low], axis=1).astype(BF16)


def gather_slots(brick_split, cells):
    hot = jnp.concatenate([onehot(cell & 127, 128) for cell in cells], axis=1)
    found = matmul(brick_split, jnp.concatenate([hot, hot], axis=0))
    values = []
    for i, cell in enumerate(cells):
        here = rows_of((32, 128)) == (cell >> 7)
        part = found[:, i * 128 : (i + 1) * 128]
        values.append(
            [
                jnp.sum(jnp.where(here, part[32 * k : 32 * k + 32], 0.0), axis=0, keepdims=True)
                for k in range(3)
            ]
        )
    return values


def pair_tile(rows):
    row = rows_of((8, 128))
    tile = jnp.broadcast_to(rows[7], (8, 128))
    for i in range(7):
        tile = jnp.where(row == i, rows[i], tile)
    return tile


def spread_kernel(tissue_hbm, rate_hbm, bricks_ref, both_ref, sems):
    copies = [
        pltpu.make_async_copy(ref, both_ref.at[i], sems.at[i]) for i, ref in enumerate((tissue_hbm, rate_hbm))
    ]
    for copy in copies:
        copy.start()
    copies[0].wait()
    for t in range(BRICKS):
        bricks_ref[t] = both_ref[0]
    copies[1].wait()


def wide(ref, i):
    return jnp.concatenate([ref[i, t] for t in range(BRICKS)], axis=1)


def read_table(slots, i):
    tiles = [slots[TABLES + i // 4, 4 * (i % 4) + j] for j in range(4)]
    return jnp.concatenate([jnp.concatenate(tiles[:2], axis=1), jnp.concatenate(tiles[2:], axis=1)], axis=0)


def write_table(slots, i, value):
    for j in range(4):
        rows, lanes = 8 * (j // 2), 128 * (j % 2)
        slots[TABLES + i // 4, 4 * (i % 4) + j] = value[rows : rows + 8, lanes : lanes + 128]


def by_half(rows, upper):
    high, low = split(rows)
    return jnp.concatenate(
        [
            jnp.where(upper, 0.0, high),
            jnp.where(upper, 0.0, low),
            jnp.where(upper, high, 0.0),
            jnp.where(upper, low, 0.0),
        ],
        axis=0,
    ).astype(BF16)


def sum_segments(rows, pair, weights, hots):
    lhs = by_half(rows, weights < 0.0)
    sums = []
    for block in (2 * pair, 2 * pair + 1):
        part = matmul_nt(lhs, wide(hots, block))
        sums.append(jnp.concatenate([part[0:8] + part[8:16], part[16:24] + part[24:32]], axis=1))
    return jnp.where(rows_of((8, SEG)) < 4, sums[0], sums[1])


def column_of(ref, at):
    row = rows_of((16, 1))
    column = jnp.zeros((16, 1), F32)
    for block in range(4):
        for k in range(3):
            column = jnp.where(row == 4 * block + k, ref[at(block, k)], column)
    return column


def prepare_kernel(*refs):
    slots, hots = refs[7:9]
    segment_ref, weight_ref, voxel_ref, flow_ref, count_ref, perm_ref, inlet_ref = refs[9:16]
    sems = refs[16]
    copies = [pltpu.make_async_copy(refs[i], refs[9 + i], sems.at[i]) for i in range(7)]
    for copy in copies:
        copy.start()
    for copy in copies:
        copy.wait()
    row = rows_of((8, 128))
    lane = lanes_of((1, 128))

    def brick(t, carry):
        for pair in range(2):
            weights, cells = [], []
            for block in (2 * pair, 2 * pair + 1):
                weight = weight_ref[block, pl.ds(t, 1), :]
                weight = jnp.where(lane < count_ref[block, t], weight, 0.0)
                segment = segment_ref[block, pl.ds(t, 1), :]
                weights.append(jnp.where(segment >= 128, -weight, weight))
                cells.append(voxel_ref[block, pl.ds(t, 1), :].astype(F32))
                hots[block, t] = onehot(segment & 127, 128)
            slots[WEIGHTS + pair, t] = jnp.where(row < 4, weights[0], weights[1])
            slots[CELLS + pair, t] = jnp.where(row < 4, cells[0], cells[1])
        return carry

    lax.fori_loop(0, BRICKS, brick, 0, unroll=4)
    row = rows_of((8, SEG))
    scale = jnp.broadcast_to(column_of(perm_ref, lambda block, k: k), (16, SEG))
    write_table(slots, SCALE, scale)
    inlet = column_of(inlet_ref, lambda block, k: (k, block))
    write_table(slots, INLET, jnp.broadcast_to(inlet, (16, SEG)))
    weight_sums, speeds = [], []
    for pair in range(2):
        weights = wide(slots, WEIGHTS + pair)
        weight_sums.append(sum_segments(jnp.abs(weights), pair, weights, hots))
        speeds.append(jnp.where(row < 4, flow_ref[2 * pair : 2 * pair + 1], flow_ref[2 * pair + 1 : 2 * pair + 2]))
    speed = jnp.concatenate(speeds, axis=0)
    inverse = 1.0 / (speed + scale * jnp.concatenate(weight_sums, axis=0))
    decay = speed * inverse
    write_table(slots, DECAY, decay)
    write_table(slots, GAIN, scale * inverse)
    lane = lanes_of(decay.shape)
    for i in range(SCAN_STEPS):
        inside = lane >= 2**i
        write_table(slots, i, jnp.where(inside, decay, 0.0))
        decay = decay * jnp.where(inside, pltpu.roll(decay, 2**i, 1), 1.0)


def solve_blocks(inflow, values, slots, hots, send_ref, narrow):
    gathered = []
    for pair in range(2):
        weights = wide(slots, WEIGHTS + pair)
        gathered.append(sum_segments(wide(values, pair) * jnp.abs(weights), pair, weights, hots))
    vessel = read_table(slots, GAIN) * jnp.concatenate(gathered, axis=0)
    vessel = vessel + jnp.where(lanes_of((16, SEG)) == 0, read_table(slots, DECAY) * inflow, 0.0)
    for i in range(SCAN_STEPS):
        vessel = vessel + read_table(slots, i) * pltpu.roll(vessel, 2**i, 1)

    send_ref[0, 32:48] = jnp.zeros((16, 128), F32)
    send_ref[BRICKS - 1, 16:32] = jnp.zeros((16, 128), F32)
    tile_row = rows_of((8, 128))
    scale = read_table(slots, SCALE)[0:8, 0:128]
    for pair in range(2):
        high, low = split(vessel[8 * pair : 8 * pair + 8])
        lhs = jnp.concatenate(
            [high[:, :128], low[:, :128], high[:, 128:], low[:, 128:]], axis=0
        ).astype(BF16)
        found = [matmul(lhs, wide(hots, block)) for block in (2 * pair, 2 * pair + 1)]
        for t in range(BRICKS):
            weights = slots[WEIGHTS + pair, t]
            part = [value[:, t * 128 : (t + 1) * 128] for value in found]
            part = [jnp.where(tile_row < 4, part[0][8 * i : 8 * i + 8], part[1][8 * i : 8 * i + 8]) for i in range(4)]
            at_slot = jnp.where(weights < 0.0, part[2] + part[3], part[0] + part[1])
            flux = scale * jnp.abs(weights) * (at_slot - values[pair, t])
            cell = slots[CELLS + pair, t]
            cell_row = (tile_row & 3) == 3
            here = slice(8 * pair, 8 * pair + 8)
            own = jnp.where(cell_row, cell, flux)
            first = last = own
            if narrow:
                is_first = ((cell.astype(jnp.int32) >> 7) & 7) < 4
                first = jnp.where(cell_row | is_first, own, 0.0)
                last = jnp.where(is_first & ~cell_row, 0.0, own)
            send_ref[t, here] = own
            if t > 0:
                send_ref[t - 1, 16 + 8 * pair : 24 + 8 * pair] = first
            if t < BRICKS - 1:
                send_ref[t + 1, 32 + 8 * pair : 40 + 8 * pair] = last
    return vessel


def first_solve_kernel(region_ref, slots, hots, send_ref, ends_ref, values):
    def brick(t, carry):
        cells = [slots[CELLS + block // 2, t, 4 * (block % 2) : 4 * (block % 2) + 1].astype(jnp.int32) for block in range(4)]
        found = gather_slots(split_brick(region_ref[t]), cells)
        for pair in range(2):
            values[pair, t] = pair_tile([*found[2 * pair], 0.0, *found[2 * pair + 1], 0.0])
        return carry

    lax.fori_loop(0, BRICKS, brick, 0, unroll=4)
    vessel = solve_blocks(read_table(slots, INLET), values, slots, hots, send_ref, False)
    spot = lanes_of((16, 128)) == rows_of((16, 128))
    ends = jnp.sum(jnp.where(spot, vessel[:, SEG - 1 : SEG], 0.0), axis=0, keepdims=True)
    ends_ref[...] = jnp.broadcast_to(ends[None], (PARTS, 8, 128))


def second_solve_kernel(upstream_ref, values_ref, slots, hots, send_ref, vessel_ref, values):
    spare = (rows_of((8, 128)) & 3) == 3
    for t in range(BRICKS):
        for pair in range(2):
            values[pair, t] = jnp.where(spare, 0.0, values_ref[t, 8 * pair : 8 * pair + 8])
    row, lane = rows_of((16, 128)), lanes_of((16, 128))
    picked = jnp.zeros((16, 128), F32)
    for block in range(4):
        feeder = upstream_ref[block]
        device = feeder >> 2
        ends = values_ref[device & 15, 3:4, :]
        spot = (device >> 4) * 16 + (feeder & 3) * 4
        picked = jnp.where(((row >> 2) == block) & (lane == spot + (row & 3)), ends, picked)
    inflow = 0.5 * (read_table(slots, INLET) + jnp.sum(picked, axis=1, keepdims=True))
    vessel = solve_blocks(inflow, values, slots, hots, send_ref, True)
    for block in range(4):
        for k in range(3):
            vessel_ref[k, block : block + 1, :] = vessel[4 * block + k : 4 * block + k + 1]


def scatter_slots(recv_ref, source, groups):
    source[...] = jnp.zeros((len(groups), 192, 128), F32)
    zero = jnp.zeros((16, 128), BF16)

    def senders(i, carry):
        for j, tiles in enumerate(groups):
            hots, parts = [], []
            for q in range(SENDERS):
                s = i * SENDERS + q
                for start in tiles:
                    for base in (start, start + 4):
                        cell = recv_ref[s, base + 3 : base + 4, :].astype(jnp.int32)
                        hots.append(onehot(cell & 127, 128))
                        here = matches(cell >> 7, 32)
                        highs, lows = [], []
                        for k in range(3):
                            flux = jnp.broadcast_to(recv_ref[s, base + k : base + k + 1, :], (16, 128))
                            high = flux.astype(BF16)
                            low = (flux - high.astype(F32)).astype(BF16)
                            highs += [jnp.where(hit, high, zero) for hit in here]
                            lows += [jnp.where(hit, low, zero) for hit in here]
                        parts.append(jnp.concatenate(highs + lows, axis=0))
            source[j] += matmul_nt(jnp.concatenate(parts, axis=1), jnp.concatenate(hots, axis=1))
        return carry

    lax.fori_loop(0, BRICKS // SENDERS, senders, 0, unroll=2)
    return [source[j, 0:96] + source[j, 96:192] for j in range(len(groups))]


def planes(value):
    return value.reshape(3, 4, 8, 128)


def write_messages(tissues, sources, up_ref, down_ref):
    for i, (value, source) in enumerate(zip(tissues, sources)):
        here = slice(8 * i, 8 * i + 8)
        value, source = planes(value), planes(source)
        up_ref[:, 0:4, here] = value
        down_ref[:, 0:4, here] = value
        up_ref[:, 4:7, here] = source[:, 1:4]
        down_ref[:, 4:7, here] = source[:, 0:3]


def first_scatter_kernel(recv_ref, both_ref, after_ref, before_ref, up_ref, down_ref, sources_ref, scratch):
    sources = scatter_slots(recv_ref, scratch, ((0, 8), (16, 24), (32, 40)))
    for i in range(3):
        sources_ref[i] = sources[i]
    ring = (both_ref, after_ref, before_ref)
    write_messages([ref[0] for ref in ring], sources, up_ref, down_ref)
    for i, ref in enumerate(ring):
        here = slice(8 * i, 8 * i + 8)
        value = planes(ref[1])
        up_ref[:, 7:10, here] = value[:, 1:4]
        down_ref[:, 7:10, here] = value[:, 0:3]


def second_scatter_kernel(recv_ref, tissue_ref, around_ref, up_ref, down_ref, sources_ref, scratch):
    sources = scatter_slots(recv_ref, scratch, ((0, 8), (16, 24, 32, 40)))
    for i in range(2):
        sources_ref[i] = sources[i]
    write_messages((tissue_ref[...], around_ref[...]), sources, up_ref, down_ref)


def fill(now, source, below, above, tissues, sources):
    for k in range(3):
        now[k, 0:4] = below[k, 0:4]
        now[k, 8:12] = above[k, 0:4]
        source[k, 1:4] = below[k, 4:7]
        source[k, 8:11] = above[k, 4:7]
        for i in range(len(tissues)):
            now[k, 4:8, 8 * i : 8 * i + 8] = planes(tissues[i])[k]
            source[k, 4:8, 8 * i : 8 * i + 8] = planes(sources[i])[k]


def run_sweeps(now, later, source, inverse, produced):
    count = now.shape[2]
    lane = lanes_of((count, 128))
    old, new = now, later
    for sweep in range(1, SWEEPS + 1):
        for k in range(3):
            for z in range(sweep, 12 - sweep):
                middle = old[k, z]
                total = old[k, z - 1] + old[k, z + 1]
                total = total + pltpu.roll(middle, 1, 0) + pltpu.roll(middle, count - 1, 0)
                total = total + jnp.where(lane > 0, pltpu.roll(middle, 1, 1), 0.0)
                total = total + jnp.where(lane < 127, pltpu.roll(middle, 127, 1), 0.0)
                total = source[k, z] + DIFFUSION[k] * total
                if k == 2:
                    total = total + produced[z] * old[1, z]
                new[k, z] = total * inverse[k, z]
        old, new = new, old
    return old


def beside(after, before):
    low = lax.broadcasted_iota(jnp.int32, after.shape, after.ndim - 2) < 4
    return jnp.where(low, after, before)


def first_sweeps_kernel(
    below, above, both_ref, after_ref, before_ref, sources_ref, recv_ref, ends_ref,
    out_ref, side_ref, inverse_ref, produced_ref, send_ref, now, later, source, inverse, produced,
):
    ring = (both_ref, after_ref, before_ref)
    fill(now, source, below, above, [ref[0] for ref in ring], [sources_ref[i] for i in range(3)])
    for k in range(3):
        rates = [planes(ref[1])[k] for ref in ring]
        for z in range(1, 11):
            if z < 4:
                rate = below[k, z + 6]
            elif z < 8:
                rate = jnp.concatenate([value[z - 4] for value in rates], axis=0)
            else:
                rate = above[k, z - 1]
            value = jnp.where(rate > 0.0, 1.0 / (6.0 * DIFFUSION[k] + rate), 0.0)
            inverse[k, z] = value
            inverse_ref[k, z, 0:8] = value[0:8]
            inverse_ref[k, z, 8:16] = beside(value[8:16], value[16:24])
            if k == 1:
                rate = 2.0 * rate
                produced[z] = rate
                produced_ref[z, 0:8] = rate[0:8]
                produced_ref[z, 8:16] = beside(rate[8:16], rate[16:24])
    final = run_sweeps(now, later, source, inverse, produced)
    brick = final[:, 4:8, 0:8].reshape(96, 128)
    out_ref[...] = brick
    side_ref[...] = beside(final[:, 4:8, 8:16], final[:, 4:8, 16:24]).reshape(96, 128)
    brick_split = split_brick(brick)
    ends = ends_ref[0, 0:1]
    for part in range(1, PARTS):
        ends = ends + pltpu.roll(ends_ref[part], 16 * part, 1)[0:1]

    def receiver(s, carry):
        cells = [recv_ref[s, 4 * b + 3 : 4 * b + 4, :].astype(jnp.int32) for b in range(4)]
        found = gather_slots(brick_split, cells)
        for pair in range(2):
            send_ref[s, 8 * pair : 8 * pair + 8] = pair_tile(
                [*found[2 * pair], ends, *found[2 * pair + 1], ends]
            )
        return carry

    lax.fori_loop(0, BRICKS, receiver, 0, unroll=4)


def second_sweeps_kernel(
    below, above, tissue_ref, side_ref, sources_ref, inverse, produced, out_ref, now, later, source
):
    fill(now, source, below, above, [tissue_ref[...], side_ref[...]], [sources_ref[i] for i in range(2)])
    final = run_sweeps(now, later, source, inverse, produced)
    out_ref[...] = final[:, 4:8, 0:8]


VMEM = pl.BlockSpec(memory_space=pltpu.VMEM)
SMEM = pl.BlockSpec(memory_space=pltpu.SMEM)
HBM = pl.BlockSpec(memory_space=pltpu.HBM)


def call(kernel, name, outs, args, scratch, spaces=None):
    spaces = spaces or [VMEM] * len(args)
    args = [
        arg if space is SMEM else pltpu.with_memory_space_constraint(arg, space.memory_space)
        for arg, space in zip(args, spaces)
    ]
    return pl.pallas_call(
        kernel,
        out_shape=[jax.ShapeDtypeStruct(out, F32) if isinstance(out, tuple) else out for out in outs],
        in_specs=spaces,
        out_specs=[VMEM] * len(outs),
        scratch_shapes=scratch,
        compiler_params=pltpu.CompilerParams(vmem_limit_bytes=VMEM_LIMIT),
        name=name,
    )(*args)


def shards(
    tissue_start,
    consumption,
    inlet,
    flow,
    permeability,
    intersection_count,
    intersection_segment,
    intersection_voxel,
    intersection_weight,
    upstream,
):
    def exchange(value, axis):
        return lax.all_to_all(value, axis, 0, 0, tiled=True)

    def shift(value, axis, step):
        size = lax.axis_size(axis)
        pairs = [(i, i + step) for i in range(size) if 0 <= i + step < size]
        return lax.ppermute(value, axis, pairs)

    ring, large_ring = (3, 12, 16, 128), (3, 12, 24, 128)
    values_scratch = [pltpu.VMEM((2, BRICKS, 8, 128), F32)]

    bricks, both = call(
        spread_kernel,
        "spread",
        [(BRICKS, 96, 128), (2, 96, 128)],
        [tissue_start.reshape(96, 128), consumption.reshape(96, 128)],
        [pltpu.SemaphoreType.DMA((2,))],
        [HBM] * 2,
    )
    region = exchange(bricks, "tissue")
    after = shift(both, "tissue", -1)
    before = shift(both, "tissue", 1)
    slot_array = intersection_voxel.shape
    prepared = call(
        prepare_kernel,
        "prepare",
        [
            (7, BRICKS, 8, 128),
            jax.ShapeDtypeStruct((4, BRICKS, 128, 128), BF16),
        ],
        [
            intersection_segment,
            intersection_weight,
            intersection_voxel,
            flow,
            intersection_count,
            permeability,
            inlet,
        ],
        [
            pltpu.VMEM(slot_array, jnp.int32),
            pltpu.VMEM(slot_array, F32),
            pltpu.VMEM(slot_array, jnp.int32),
            pltpu.VMEM(flow.shape, F32),
            pltpu.SMEM(intersection_count.shape, jnp.int32),
            pltpu.SMEM(permeability.shape, F32),
            pltpu.SMEM(inlet.shape, F32),
            pltpu.SemaphoreType.DMA((7,)),
        ],
        [HBM] * 7,
    )
    region, after, before = lax.optimization_barrier((region, after, before))
    send, ends = call(
        first_solve_kernel,
        "first_solve",
        [(BRICKS, 48, 128), (PARTS, 8, 128)],
        [region, *prepared],
        values_scratch,
    )
    received = exchange(send, "tissue")
    ends = exchange(ends, "vessel")
    up, down, sources = call(
        first_scatter_kernel,
        "first_scatter",
        [(3, 10, 24, 128), (3, 10, 24, 128), (3, 96, 128)],
        [received, both, after, before],
        [pltpu.VMEM((3, 192, 128), F32)],
    )
    below = shift(up, "vessel", 1)
    above = shift(down, "vessel", -1)
    tissue, side, inverse, produced, send = call(
        first_sweeps_kernel,
        "first_sweeps",
        [(96, 128), (96, 128), ring, ring[1:], (BRICKS, 16, 128)],
        [below, above, both, after, before, sources, received, ends],
        [pltpu.VMEM(large_ring, F32)] * 4 + [pltpu.VMEM(large_ring[1:], F32)],
    )
    values = exchange(send, "tissue")
    send, vessel = call(
        second_solve_kernel,
        "second_solve",
        [(BRICKS, 48, 128), (3, 4, SEG)],
        [upstream, values, *prepared],
        values_scratch,
        [SMEM] + [VMEM] * 3,
    )
    received = exchange(send, "tissue")
    up, down, sources = call(
        second_scatter_kernel,
        "second_scatter",
        [(3, 7, 16, 128), (3, 7, 16, 128), (2, 96, 128)],
        [received, tissue, side],
        [pltpu.VMEM((2, 192, 128), F32)],
    )
    below = shift(up, "vessel", 1)
    above = shift(down, "vessel", -1)
    (tissue,) = call(
        second_sweeps_kernel,
        "second_sweeps",
        [(3, 4, 8, 128)],
        [below, above, tissue, side, sources, inverse, produced],
        [pltpu.VMEM(ring, F32)] * 3,
    )
    return tissue, vessel


def solution(mesh):
    return jax.shard_map(
        shards,
        mesh=mesh,
        in_specs=(
            P(None, "vessel", "tissue", None),
            P(None, "vessel", "tissue", None),
            P(None, ("vessel", "tissue")),
            P(("vessel", "tissue"), None),
            P(),
            P(("vessel", "tissue"), None),
            P(("vessel", "tissue"), None, None),
            P(("vessel", "tissue"), None, None),
            P(("vessel", "tissue"), None, None),
            P(("vessel", "tissue")),
        ),
        out_specs=(P(None, "vessel", "tissue", None), P(None, ("vessel", "tissue"), None)),
        check_vma=False,
    )
```

time: 110 us -> 103 us (0.936)
  waiting for transfers between devices: 20.2 us -> 10.1 us
  Pallas kernels: 15.9 us -> 18.6 us
  starting transfers between devices: 25.3 us -> 26.9 us
  local copies, waits for them, and re-layouts: 1.82 us -> 0.64 us
    ppermute x6, waiting for transfers between devices: 17.9 us -> 9.5 us  [shift(): return lax.ppermute(value, axis, pairs)]
    pallas_call x6 -> x8, Pallas kernels: 15.9 us -> 18.6 us  [call(): pl.pallas_call(kernel, out_shape=[jax.ShapeDtypeStruct(out, F32) if isins...]
    broadcast_in_dim x1 -> x0, local copies, waits for them, and re-layouts: 1.77 us -> none  [shards(): bricks = jnp.broadcast_to(tissue[None], (BRICKS, 96, 128))]
    ppermute x6, starting transfers between devices: 17.6 us -> 19.3 us  [shift(): return lax.ppermute(value, axis, pairs)]
    all_to_all x1, waiting for transfers between devices: 2.26 us -> 0.58 us  [exchange(): return lax.all_to_all(value, axis, 0, 0, tiled=True)]
  transfers between devices with their start and end apart: 7 -> 7, of which waited for: 7 -> 5; matrix products, arithmetic and copies ran while one was open for 0% -> 0% of each run, Pallas kernels for 0% -> 3%
where the time goes in v3:
time: 103 us
  blocking collectives  45.8 us (44%)
  starting transfers between devices  26.9 us (26%)
  Pallas kernels  18.6 us (18%)
  waiting for transfers between devices  10.1 us (10%)
    all_to_all x4, blocking collectives, exchange(): return lax.all_to_all(value, axis, 0, 0, tiled=True)  45.8 us
    ppermute x6, starting transfers between devices, shift(): return lax.ppermute(value, axis, pairs)  19.3 us
    pallas_call x8, Pallas kernels, call(): pl.pallas_call(kernel, out_shape=[jax.ShapeDtypeStruct(out, F32) if isins...  18.6 us
    ppermute x6, waiting for transfers between devices, shift(): return lax.ppermute(value, axis, pairs)  9.5 us
    all_to_all x1, starting transfers between devices, exchange(): return lax.all_to_all(value, axis, 0, 0, tiled=True)  7.6 us
  transfers between devices with their start and end apart: 7, of which 5 were waited for; matrix products, arithmetic and copies ran while one was open for 0% of the time, Pallas kernels for 3%

profile of v3, /device:TPU:1, one launch (start us, length us, event | category | flops | bytes accessed | tf_op | source)
XLA Modules:
  0.0 102.8 jit_solution(9519542130358067224)
XLA Ops:
  0.6 1.8 %spread.1 = (f32[16,96,128]{2,1,0:T(8,128)}, f32[2,96,128]{2,1,0:T(8,128)S(1)}) custom-call(f32[96,128]{1,0:T(8,128)} %bitcast.2, f32[96,128]{1,0:T(8,128)} %bitcast.3), custom_call_target="tpu_custom_call" | custom-call | tf_op jit(solution)/shard_map/spread/pallas_call | solution.py:436
  2.4 7.6 %all-to-all-start = ((f32[16,96,128]{2,1,0:T(8,128)}), f32[16,96,128]{2,1,0:T(8,128)S(1)}, u32[]{:S(2)}, u32[]{:S(2)}) async-start(f32[16,96,128]{2,1,0:T(8,128)} %get-tuple-element.24), calls=%async_computation | async-start | bytes 1572864 | tf_op jit(solution)/shard_map/all_to_all | solution.py:460
  10.0 3.3 %collective-permute-start.1 = (f32[2,96,128]{2,1,0:T(8,128)S(1)}, f32[2,96,128]{2,1,0:T(8,128)S(1)}, u32[]{:S(2)}, u32[]{:S(2)}) collective-permute-start(f32[2,96,128]{2,1,0:T(8,128)S(1)} %get-tuple-element.25.both_ref), channel_id=1, source_target_pairs={{0,1},{1,2},{2,3},{3,4},{4,5},{5,6},{6,7},{7,8},{8,9},{9,10},{10,1... | collective-permute-start | bytes 294920 | tf_op jit(solution)/shard_map/ppermute | solution.py:465
  13.3 1.3 %collective-permute-start = (f32[2,96,128]{2,1,0:T(8,128)S(1)}, f32[2,96,128]{2,1,0:T(8,128)S(1)}, u32[]{:S(2)}, u32[]{:S(2)}) collective-permute-start(f32[2,96,128]{2,1,0:T(8,128)S(1)} %get-tuple-element.25.both_ref), channel_id=1, source_target_pairs={{1,0},{2,1},{3,2},{4,3},{5,4},{6,5},{7,6},{8,7},{9,8},{10,9},{11,1... | collective-permute-start | bytes 294920 | tf_op jit(solution)/shard_map/ppermute | solution.py:465
  14.6 2.7 %prepare.1 = (f32[7,16,8,128]{3,2,1,0:T(8,128)S(1)}, bf16[4,16,128,128]{3,2,1,0:T(8,128)(2,1)S(1)}) custom-call(s32[4,16,128]{2,1,0:T(8,128)} %refs_0_.1, f32[4,16,128]{2,1,0:T(8,128)} %refs_1_.1, s32[4,16,128]{2,1,0:T(8,128)} %refs_2_.1, f32[4,256]{1,0:T(4,128)} %refs_3_.1, s32[4,16]{1,0:T(4,128)} %refs_4_.1, f32[3]{0:T(128)} %refs_5_.1, f32[3,4]{1,0:T(4,128)} %refs_6_.1), custom_call_target="tpu_custom_call" | custom-call | tf_op jit(solution)/shard_map/prepare/pallas_call | solution.py:436
  17.3 2.8 %collective-permute-done.1.before_ref = f32[2,96,128]{2,1,0:T(8,128)S(1)} collective-permute-done((f32[2,96,128]{2,1,0:T(8,128)S(1)}, f32[2,96,128]{2,1,0:T(8,128)S(1)}, u32[]{:S(2)}, u32[]{:S(2)}) %collective-permute-start.1) | collective-permute-done | bytes 98336 | tf_op jit(solution)/shard_map/ppermute | solution.py:465
  20.0 1.9 %collective-permute-done.after_ref = f32[2,96,128]{2,1,0:T(8,128)S(1)} collective-permute-done((f32[2,96,128]{2,1,0:T(8,128)S(1)}, f32[2,96,128]{2,1,0:T(8,128)S(1)}, u32[]{:S(2)}, u32[]{:S(2)}) %collective-permute-start) | collective-permute-done | bytes 98336 | tf_op jit(solution)/shard_map/ppermute | solution.py:465
  22.0 0.0 copy-start
  22.0 0.6 copy-done
  22.6 0.6 all-to-all-done.region_ref
  23.2 0.0 copy-start.1
  23.2 2.9 %first_solve.1 = (f32[16,48,128]{2,1,0:T(8,128)S(1)}, f32[8,8,128]{2,1,0:T(8,128)S(1)}) custom-call(f32[16,96,128]{2,1,0:T(8,128)S(1)} %all-to-all-done.region_ref, f32[7,16,8,128]{3,2,1,0:T(8,128)S(1)} %get-tuple-element.27.slots, bf16[4,16,128,128]{3,2,1,0:T(8,128)(2,1)S(1)} %get-tuple-element.28.hots), custom_call_target="tpu_custom_call" | custom-call | tf_op jit(solution)/shard_map/first_solve/pallas_call | solution.py:436
  26.1 0.0 copy-start.2
  26.1 14.8 %all_to_all.25.recv_ref = f32[16,48,128]{2,1,0:T(8,128)S(1)} all-to-all(f32[16,48,128]{2,1,0:T(8,128)S(1)} %get-tuple-element.29), channel_id=1, replica_groups=mesh['vessel'=8,'tissue'=16] {'tissue'}, dimensions={0} | all-to-all | bytes 786432 | tf_op jit(solution)/shard_map/all_to_all | solution.py:460
  40.9 0.0 copy-done.1
  40.9 2.8 %first_scatter.1 = (f32[3,10,24,128]{3,2,1,0:T(8,128)S(1)}, f32[3,10,24,128]{3,2,1,0:T(8,128)S(1)}, f32[3,96,128]{2,1,0:T(8,128)S(1)}) custom-call(f32[16,48,128]{2,1,0:T(8,128)S(1)} %all_to_all.25.recv_ref, f32[2,96,128]{2,1,0:T(8,128)S(1)} %get-tuple-element.25.both_ref, f32[2,96,128]{2,1,0:T(8,128)S(1)} %copy-done.1, ...), custom_call_target="tpu_custom_call" | custom-call | tf_op jit(solution)/shard_map/first_scatter/pallas_call | solution.py:436
  43.7 5.8 %collective-permute-start.2 = (f32[3,10,24,128]{3,2,1,0:T(8,128)S(1)}, f32[3,10,24,128]{3,2,1,0:T(8,128)S(1)}, u32[]{:S(2)}, u32[]{:S(2)}) collective-permute-start(f32[3,10,24,128]{3,2,1,0:T(8,128)S(1)} %get-tuple-element.32), channel_id=1, source_target_pairs={{0,16},{16,32},{32,48},{48,64},{64,80},{80,96},{96,112},{1,17},{17... | collective-permute-start | bytes 1105928 | tf_op jit(solution)/shard_map/ppermute | solution.py:465
  49.5 1.9 %collective-permute-start.3 = (f32[3,10,24,128]{3,2,1,0:T(8,128)S(1)}, f32[3,10,24,128]{3,2,1,0:T(8,128)S(1)}, u32[]{:S(2)}, u32[]{:S(2)}) collective-permute-start(f32[3,10,24,128]{3,2,1,0:T(8,128)S(1)} %get-tuple-element.33), channel_id=1, source_target_pairs={{16,0},{32,16},{48,32},{64,48},{80,64},{96,80},{112,96},{17,1},{33... | collective-permute-start | bytes 1105928 | tf_op jit(solution)/shard_map/ppermute | solution.py:465
  51.4 10.0 %all_to_all.26.ends_ref = f32[8,8,128]{2,1,0:T(8,128)S(1)} all-to-all(f32[8,8,128]{2,1,0:T(8,128)S(1)} %get-tuple-element.35), channel_id=1, replica_groups=mesh['vessel'=8,'tissue'=16] {'vessel'}, dimensions={0} | all-to-all | bytes 65536 | tf_op jit(solution)/shard_map/all_to_all | solution.py:460
  61.5 0.0 collective-permute-done.2.below
  61.5 0.0 collective-permute-done.3.above
  61.5 2.0 %first_sweeps.1 = (f32[96,128]{1,0:T(8,128)S(1)}, f32[96,128]{1,0:T(8,128)S(1)}, f32[3,12,16,128]{3,2,1,0:T(8,128)S(1)}, f32[12,16,128]{2,1,0:T(8,128)S(1)}, f32[16,16,128]{2,1,0:T(8,128)S(1)}) custom-call(f32[3,10,24,128]{3,2,1,0:T(8,128)S(1)} %collective-permute-done.2.below, f32[3,10,24,128]{3,2,1,0:T(8,128)S(1)} %collective-permute-done.3.above, ...), custom_call_target="tpu_custom_call" | custom-call | tf_op jit(solution)/shard_map/first_sweeps/pallas_call | solution.py:436
  63.4 9.5 %all_to_all.27.values_ref = f32[16,16,128]{2,1,0:T(8,128)S(1)} all-to-all(f32[16,16,128]{2,1,0:T(8,128)S(1)} %get-tuple-element.36), channel_id=1, replica_groups=mesh['vessel'=8,'tissue'=16] {'tissue'}, dimensions={0} | all-to-all | bytes 262144 | tf_op jit(solution)/shard_map/all_to_all | solution.py:460
  73.0 0.0 copy-done.2
  73.0 2.6 %second_solve.1 = (f32[16,48,128]{2,1,0:T(8,128)S(1)}, f32[3,4,256]{2,1,0:T(4,128)}) custom-call(s32[4]{0:T(128)S(1)} %copy-done.2, f32[16,16,128]{2,1,0:T(8,128)S(1)} %all_to_all.27.values_ref, f32[7,16,8,128]{3,2,1,0:T(8,128)S(1)} %get-tuple-element.27.slots, bf16[4,16,128,128]{3,2,1,0:T(8,128)(2,1)S(1)} %get-tuple-element.28.hots), custom_call_target="tpu_custom_call" | custom-call | tf_op jit(solution)/shard_map/second_solve/pallas_call | solution.py:436
  75.6 11.5 %all_to_all.28.recv_ref = f32[16,48,128]{2,1,0:T(8,128)S(1)} all-to-all(f32[16,48,128]{2,1,0:T(8,128)S(1)} %get-tuple-element.37), channel_id=1, replica_groups=mesh['vessel'=8,'tissue'=16] {'tissue'}, dimensions={0} | all-to-all | bytes 786432 | tf_op jit(solution)/shard_map/all_to_all | solution.py:460
  87.0 2.8 %second_scatter.1 = (f32[3,7,16,128]{3,2,1,0:T(8,128)S(1)}, f32[3,7,16,128]{3,2,1,0:T(8,128)S(1)}, f32[2,96,128]{2,1,0:T(8,128)S(1)}) custom-call(f32[16,48,128]{2,1,0:T(8,128)S(1)} %all_to_all.28.recv_ref, f32[96,128]{1,0:T(8,128)S(1)} %get-tuple-element.38.tissue_ref, f32[96,128]{1,0:T(8,128)S(1)} %get-tuple-element.39.around_ref.side_ref), custom_call_target="tpu_custom_call" | custom-call | tf_op jit(solution)/shard_map/second_scatter/pallas_call | solution.py:436
  89.9 5.2 %collective-permute-start.4 = (f32[3,7,16,128]{3,2,1,0:T(8,128)S(1)}, f32[3,7,16,128]{3,2,1,0:T(8,128)S(1)}, u32[]{:S(2)}, u32[]{:S(2)}) collective-permute-start(f32[3,7,16,128]{3,2,1,0:T(8,128)S(1)} %get-tuple-element.40), channel_id=1, source_target_pairs={{0,16},{16,32},{32,48},{48,64},{64,80},{80,96},{96,112},{1,17},{17... | collective-permute-start | bytes 516104 | tf_op jit(solution)/shard_map/ppermute | solution.py:465
  95.0 1.9 %collective-permute-start.5 = (f32[3,7,16,128]{3,2,1,0:T(8,128)S(1)}, f32[3,7,16,128]{3,2,1,0:T(8,128)S(1)}, u32[]{:S(2)}, u32[]{:S(2)}) collective-permute-start(f32[3,7,16,128]{3,2,1,0:T(8,128)S(1)} %get-tuple-element.41), channel_id=1, source_target_pairs={{16,0},{32,16},{48,32},{64,48},{80,64},{96,80},{112,96},{17,1},{33... | collective-permute-start | bytes 516104 | tf_op jit(solution)/shard_map/ppermute | solution.py:465
  97.0 0.4 collective-permute-done.4.below
  97.4 4.4 %collective-permute-done.5.above = f32[3,7,16,128]{3,2,1,0:T(8,128)S(1)} collective-permute-done((f32[3,7,16,128]{3,2,1,0:T(8,128)S(1)}, f32[3,7,16,128]{3,2,1,0:T(8,128)S(1)}, u32[]{:S(2)}, u32[]{:S(2)}) %collective-permute-start.5) | collective-permute-done | bytes 172064 | tf_op jit(solution)/shard_map/ppermute | solution.py:465
  101.8 1.0 %second_sweeps.1 = f32[3,4,8,128]{3,2,1,0:T(8,128)} custom-call(f32[3,7,16,128]{3,2,1,0:T(8,128)S(1)} %collective-permute-done.4.below, f32[3,7,16,128]{3,2,1,0:T(8,128)S(1)} %collective-permute-done.5.above, f32[96,128]{1,0:T(8,128)S(1)} %get-tuple-element.38.tissue_ref, f32[96,128]{1,0:T(8,128)S(1)} %get-tuple-element.39.around_ref.side_ref, ...), custom_call_target="tpu_custom_call" | custom-call | tf_op jit(solution)/shard_map/second_sweeps/pallas_call | solution.py:436
Async XLA Ops:
  2.4 20.8 %all-to-all-start = ((f32[16,96,128]{2,1,0:T(8,128)}), f32[16,96,128]{2,1,0:T(8,128)S(1)}, u32[]{:S(2)}, u32[]{:S(2)}) async-start(f32[16,96,128]{2,1,0:T(8,128)} %get-tuple-element.24), calls=%async_computation | async-start | bytes 1572864 | tf_op jit(solution)/shard_map/all_to_all | solution.py:460
  10.0 10.0 %collective-permute-start.1 = (f32[2,96,128]{2,1,0:T(8,128)S(1)}, f32[2,96,128]{2,1,0:T(8,128)S(1)}, u32[]{:S(2)}, u32[]{:S(2)}) collective-permute-start(f32[2,96,128]{2,1,0:T(8,128)S(1)} %get-tuple-element.25.both_ref), channel_id=1, source_target_pairs={{0,1},{1,2},{2,3},{3,4},{4,5},{5,6},{6,7},{7,8},{8,9},{9,10},{10,1... | collective-permute-start | bytes 294920 | tf_op jit(solution)/shard_map/ppermute | solution.py:465
  13.3 8.7 %collective-permute-start = (f32[2,96,128]{2,1,0:T(8,128)S(1)}, f32[2,96,128]{2,1,0:T(8,128)S(1)}, u32[]{:S(2)}, u32[]{:S(2)}) collective-permute-start(f32[2,96,128]{2,1,0:T(8,128)S(1)} %get-tuple-element.25.both_ref), channel_id=1, source_target_pairs={{1,0},{2,1},{3,2},{4,3},{5,4},{6,5},{7,6},{8,7},{9,8},{10,9},{11,1... | collective-permute-start | bytes 294920 | tf_op jit(solution)/shard_map/ppermute | solution.py:465
  22.0 0.6 copy-start
  23.2 17.7 %copy-start.1 = (f32[2,96,128]{2,1,0:T(8,128)S(1)}, f32[2,96,128]{2,1,0:T(8,128)}, u32[]{:S(2)}) copy-start(f32[2,96,128]{2,1,0:T(8,128)} %copy-done) | copy-start | bytes 294916
  26.1 46.9 %copy-start.2 = (s32[4]{0:T(128)S(1)}, s32[4]{0:T(128)}, u32[]{:S(2)}) copy-start(s32[4]{0:T(128)} %upstream_ref.1) | copy-start | bytes 52
  43.7 17.8 %collective-permute-start.2 = (f32[3,10,24,128]{3,2,1,0:T(8,128)S(1)}, f32[3,10,24,128]{3,2,1,0:T(8,128)S(1)}, u32[]{:S(2)}, u32[]{:S(2)}) collective-permute-start(f32[3,10,24,128]{3,2,1,0:T(8,128)S(1)} %get-tuple-element.32), channel_id=1, source_target_pairs={{0,16},{16,32},{32,48},{48,64},{64,80},{80,96},{96,112},{1,17},{17... | collective-permute-start | bytes 1105928 | tf_op jit(solution)/shard_map/ppermute | solution.py:465
  49.5 12.0 %collective-permute-start.3 = (f32[3,10,24,128]{3,2,1,0:T(8,128)S(1)}, f32[3,10,24,128]{3,2,1,0:T(8,128)S(1)}, u32[]{:S(2)}, u32[]{:S(2)}) collective-permute-start(f32[3,10,24,128]{3,2,1,0:T(8,128)S(1)} %get-tuple-element.33), channel_id=1, source_target_pairs={{16,0},{32,16},{48,32},{64,48},{80,64},{96,80},{112,96},{17,1},{33... | collective-permute-start | bytes 1105928 | tf_op jit(solution)/shard_map/ppermute | solution.py:465
  89.9 7.5 %collective-permute-start.4 = (f32[3,7,16,128]{3,2,1,0:T(8,128)S(1)}, f32[3,7,16,128]{3,2,1,0:T(8,128)S(1)}, u32[]{:S(2)}, u32[]{:S(2)}) collective-permute-start(f32[3,7,16,128]{3,2,1,0:T(8,128)S(1)} %get-tuple-element.40), channel_id=1, source_target_pairs={{0,16},{16,32},{32,48},{48,64},{64,80},{80,96},{96,112},{1,17},{17... | collective-permute-start | bytes 516104 | tf_op jit(solution)/shard_map/ppermute | solution.py:465
  95.0 6.7 %collective-permute-start.5 = (f32[3,7,16,128]{3,2,1,0:T(8,128)S(1)}, f32[3,7,16,128]{3,2,1,0:T(8,128)S(1)}, u32[]{:S(2)}, u32[]{:S(2)}) collective-permute-start(f32[3,7,16,128]{3,2,1,0:T(8,128)S(1)} %get-tuple-element.41), channel_id=1, source_target_pairs={{16,0},{32,16},{48,32},{64,48},{80,64},{96,80},{112,96},{17,1},{33... | collective-permute-start | bytes 516104 | tf_op jit(solution)/shard_map/ppermute | solution.py:465

commit v4 on v3

--- a/solution.py
+++ b/solution.py
@@ -85,16 +85,20 @@
     return tile
 
 
-def spread_kernel(tissue_hbm, rate_hbm, bricks_ref, both_ref, sems):
-    copies = [
-        pltpu.make_async_copy(ref, both_ref.at[i], sems.at[i]) for i, ref in enumerate((tissue_hbm, rate_hbm))
+def spread_kernel(tissue_hbm, rate_hbm, bricks_hbm, tissue_ref, rate_ref, sems):
+    arguments = [
+        pltpu.make_async_copy(tissue_hbm, tissue_ref, sems.at[BRICKS]),
+        pltpu.make_async_copy(rate_hbm, rate_ref, sems.at[BRICKS + 1]),
     ]
-    for copy in copies:
+    bricks = [pltpu.make_async_copy(tissue_ref, bricks_hbm.at[t], sems.at[t]) for t in range(BRICKS)]
+    for copy in arguments:
         copy.start()
-    copies[0].wait()
-    for t in range(BRICKS):
-        bricks_ref[t] = both_ref[0]
-    copies[1].wait()
+    arguments[0].wait()
+    for copy in bricks:
+        copy.start()
+    arguments[1].wait()
+    for copy in bricks:
+        copy.wait()
 
 
 def wide(ref, i):
@@ -235,7 +239,7 @@
     return vessel
 
 
-def first_solve_kernel(region_ref, slots, hots, send_ref, ends_ref, values):
+def first_solve_kernel(region_ref, slots, hots, send_ref, ends_ref, around_ref, values):
     def brick(t, carry):
         cells = [slots[CELLS + block // 2, t, 4 * (block % 2) : 4 * (block % 2) + 1].astype(jnp.int32) for block in range(4)]
         found = gather_slots(split_brick(region_ref[t]), cells)
@@ -248,6 +252,9 @@
     spot = lanes_of((16, 128)) == rows_of((16, 128))
     ends = jnp.sum(jnp.where(spot, vessel[:, SEG - 1 : SEG], 0.0), axis=0, keepdims=True)
     ends_ref[...] = jnp.broadcast_to(ends[None], (PARTS, 8, 128))
+    t = lax.axis_index("tissue")
+    around_ref[0] = jnp.where(t < BRICKS - 1, region_ref[jnp.minimum(t + 1, BRICKS - 1)], 0.0)
+    around_ref[1] = jnp.where(t > 0, region_ref[jnp.maximum(t - 1, 0)], 0.0)
 
 
 def second_solve_kernel(upstream_ref, values_ref, slots, hots, send_ref, vessel_ref, values):
@@ -270,12 +277,13 @@
             vessel_ref[k, block : block + 1, :] = vessel[4 * block + k : 4 * block + k + 1]
 
 
-def scatter_slots(recv_ref, source, groups):
-    source[...] = jnp.zeros((len(groups), 192, 128), F32)
+def scatter_slots(recv_ref, sources):
     zero = jnp.zeros((16, 128), BF16)
+    for source, _, _ in sources:
+        source[...] = jnp.zeros(source.shape, F32)
 
     def senders(i, carry):
-        for j, tiles in enumerate(groups):
+        for source, tiles, size in sources:
             hots, parts = [], []
             for q in range(SENDERS):
                 s = i * SENDERS + q
@@ -283,7 +291,10 @@
                     for base in (start, start + 4):
                         cell = recv_ref[s, base + 3 : base + 4, :].astype(jnp.int32)
                         hots.append(onehot(cell & 127, 128))
-                        here = matches(cell >> 7, 32)
+                        row = cell >> 7
+                        if size == 16:
+                            row = (row >> 3) * 4 + (row & 3)
+                        here = matches(row, size)
                         highs, lows = [], []
                         for k in range(3):
                             flux = jnp.broadcast_to(recv_ref[s, base + k : base + k + 1, :], (16, 128))
@@ -292,53 +303,76 @@
                             highs += [jnp.where(hit, high, zero) for hit in here]
                             lows += [jnp.where(hit, low, zero) for hit in here]
                         parts.append(jnp.concatenate(highs + lows, axis=0))
-            source[j] += matmul_nt(jnp.concatenate(parts, axis=1), jnp.concatenate(hots, axis=1))
+            source[...] += matmul_nt(jnp.concatenate(parts, axis=1), jnp.concatenate(hots, axis=1))
         return carry
 
     lax.fori_loop(0, BRICKS // SENDERS, senders, 0, unroll=2)
-    return [source[j, 0:96] + source[j, 96:192] for j in range(len(groups))]
+    return [source[0 : 3 * size] + source[3 * size : 6 * size] for source, _, size in sources]
+
+
+def interleave(first, last):
+    first, last = first.reshape(6, 8, 128), last.reshape(6, 8, 128)
+    low = lax.broadcasted_iota(jnp.int32, (6, 8, 128), 1) < 4
+    even = jnp.where(low, first, pltpu.roll(last, 4, 1))
+    odd = jnp.where(low, pltpu.roll(first, 4, 1), last)
+    return jnp.concatenate([value[i] for i in range(6) for value in (even, odd)], axis=0)
 
 
 def planes(value):
     return value.reshape(3, 4, 8, 128)
 
 
-def write_messages(tissues, sources, up_ref, down_ref):
+def is_even():
+    return lax.axis_index("vessel") % 2 == 0
+
+
+def toward(value, near):
+    upward = is_even() if near else ~is_even()
+    return jnp.where(upward, value[:, 1:4], value[:, 0:3])
+
+
+def write_messages(tissues, sources, near_ref, far_ref):
     for i, (value, source) in enumerate(zip(tissues, sources)):
         here = slice(8 * i, 8 * i + 8)
         value, source = planes(value), planes(source)
-        up_ref[:, 0:4, here] = value
-        down_ref[:, 0:4, here] = value
-        up_ref[:, 4:7, here] = source[:, 1:4]
-        down_ref[:, 4:7, here] = source[:, 0:3]
-
-
-def first_scatter_kernel(recv_ref, both_ref, after_ref, before_ref, up_ref, down_ref, sources_ref, scratch):
-    sources = scatter_slots(recv_ref, scratch, ((0, 8), (16, 24), (32, 40)))
+        for ref, near in ((near_ref, True), (far_ref, False)):
+            ref[:, 0:4, here] = value
+            ref[:, 4:7, here] = toward(source, near)
+
+
+def first_scatter_kernel(
+    recv_ref, tissue_ref, around_ref, rate_ref, after_ref, before_ref, near_ref, far_ref, sources_ref, *sums
+):
+    sources = scatter_slots(recv_ref, [(sums[i], (16 * i, 16 * i + 8), 32) for i in range(3)])
     for i in range(3):
         sources_ref[i] = sources[i]
-    ring = (both_ref, after_ref, before_ref)
-    write_messages([ref[0] for ref in ring], sources, up_ref, down_ref)
-    for i, ref in enumerate(ring):
+    write_messages([tissue_ref[...], around_ref[0], around_ref[1]], sources, near_ref, far_ref)
+    for i, ref in enumerate((rate_ref, after_ref, before_ref)):
         here = slice(8 * i, 8 * i + 8)
-        value = planes(ref[1])
-        up_ref[:, 7:10, here] = value[:, 1:4]
-        down_ref[:, 7:10, here] = value[:, 0:3]
-
-
-def second_scatter_kernel(recv_ref, tissue_ref, around_ref, up_ref, down_ref, sources_ref, scratch):
-    sources = scatter_slots(recv_ref, scratch, ((0, 8), (16, 24, 32, 40)))
+        value = planes(ref[...])
+        near_ref[:, 7:10, here] = toward(value, True)
+        far_ref[:, 7:10, here] = toward(value, False)
+
+
+def second_scatter_kernel(recv_ref, tissue_ref, side_ref, near_ref, far_ref, sources_ref, *sums):
+    own, first, last = scatter_slots(
+        recv_ref, [(sums[i], (16 * i, 16 * i + 8), 32 if i == 0 else 16) for i in range(3)]
+    )
+    sources = [own, interleave(first, last)]
     for i in range(2):
         sources_ref[i] = sources[i]
-    write_messages((tissue_ref[...], around_ref[...]), sources, up_ref, down_ref)
-
-
-def fill(now, source, below, above, tissues, sources):
+    write_messages([tissue_ref[...], side_ref[...]], sources, near_ref, far_ref)
+
+
+def neighbours(near, far, k, where):
+    near, far = near[k, where], far[k, where]
+    return jnp.where(is_even(), far, near), jnp.where(is_even(), near, far)
+
+
+def fill(now, source, near, far, tissues, sources):
     for k in range(3):
-        now[k, 0:4] = below[k, 0:4]
-        now[k, 8:12] = above[k, 0:4]
-        source[k, 1:4] = below[k, 4:7]
-        source[k, 8:11] = above[k, 4:7]
+        now[k, 0:4], now[k, 8:12] = neighbours(near, far, k, slice(0, 4))
+        source[k, 1:4], source[k, 8:11] = neighbours(near, far, k, slice(4, 7))
         for i in range(len(tissues)):
             now[k, 4:8, 8 * i : 8 * i + 8] = planes(tissues[i])[k]
             source[k, 4:8, 8 * i : 8 * i + 8] = planes(sources[i])[k]
@@ -370,20 +404,21 @@
 
 
 def first_sweeps_kernel(
-    below, above, both_ref, after_ref, before_ref, sources_ref, recv_ref, ends_ref,
+    near, far, tissue_ref, around_ref, rate_ref, after_ref, before_ref, sources_ref, recv_ref, ends_ref,
     out_ref, side_ref, inverse_ref, produced_ref, send_ref, now, later, source, inverse, produced,
 ):
-    ring = (both_ref, after_ref, before_ref)
-    fill(now, source, below, above, [ref[0] for ref in ring], [sources_ref[i] for i in range(3)])
+    tissues = [tissue_ref[...], around_ref[0], around_ref[1]]
+    fill(now, source, near, far, tissues, [sources_ref[i] for i in range(3)])
     for k in range(3):
-        rates = [planes(ref[1])[k] for ref in ring]
+        rates = [planes(ref[...])[k] for ref in (rate_ref, after_ref, before_ref)]
+        below, above = neighbours(near, far, k, slice(7, 10))
         for z in range(1, 11):
             if z < 4:
-                rate = below[k, z + 6]
+                rate = below[z - 1]
             elif z < 8:
                 rate = jnp.concatenate([value[z - 4] for value in rates], axis=0)
             else:
-                rate = above[k, z - 1]
+                rate = above[z - 8]
             value = jnp.where(rate > 0.0, 1.0 / (6.0 * DIFFUSION[k] + rate), 0.0)
             inverse[k, z] = value
             inverse_ref[k, z, 0:8] = value[0:8]
@@ -415,9 +450,9 @@
 
 
 def second_sweeps_kernel(
-    below, above, tissue_ref, side_ref, sources_ref, inverse, produced, out_ref, now, later, source
+    near, far, tissue_ref, side_ref, sources_ref, inverse, produced, out_ref, now, later, source
 ):
-    fill(now, source, below, above, [tissue_ref[...], side_ref[...]], [sources_ref[i] for i in range(2)])
+    fill(now, source, near, far, [tissue_ref[...], side_ref[...]], [sources_ref[i] for i in range(2)])
     final = run_sweeps(now, later, source, inverse, produced)
     out_ref[...] = final[:, 4:8, 0:8]
 
@@ -427,7 +462,7 @@
 HBM = pl.BlockSpec(memory_space=pltpu.HBM)
 
 
-def call(kernel, name, outs, args, scratch, spaces=None):
+def call(kernel, name, outs, args, scratch, spaces=None, out_spaces=None):
     spaces = spaces or [VMEM] * len(args)
     args = [
         arg if space is SMEM else pltpu.with_memory_space_constraint(arg, space.memory_space)
@@ -437,7 +472,7 @@
         kernel,
         out_shape=[jax.ShapeDtypeStruct(out, F32) if isinstance(out, tuple) else out for out in outs],
         in_specs=spaces,
-        out_specs=[VMEM] * len(outs),
+        out_specs=out_spaces or [VMEM] * len(outs),
         scratch_shapes=scratch,
         compiler_params=pltpu.CompilerParams(vmem_limit_bytes=VMEM_LIMIT),
         name=name,
@@ -464,20 +499,25 @@
         pairs = [(i, i + step) for i in range(size) if 0 <= i + step < size]
         return lax.ppermute(value, axis, pairs)
 
+    def swap(value, first):
+        starts = range(first, lax.axis_size("vessel") - 1, 2)
+        return lax.ppermute(value, "vessel", [pair for i in starts for pair in ((i, i + 1), (i + 1, i))])
+
     ring, large_ring = (3, 12, 16, 128), (3, 12, 24, 128)
     values_scratch = [pltpu.VMEM((2, BRICKS, 8, 128), F32)]
 
-    bricks, both = call(
+    bricks, tissue, rate = call(
         spread_kernel,
         "spread",
-        [(BRICKS, 96, 128), (2, 96, 128)],
+        [(BRICKS, 96, 128), (96, 128), (96, 128)],
         [tissue_start.reshape(96, 128), consumption.reshape(96, 128)],
-        [pltpu.SemaphoreType.DMA((2,))],
+        [pltpu.SemaphoreType.DMA((BRICKS + 2,))],
         [HBM] * 2,
+        [HBM, VMEM, VMEM],
     )
     region = exchange(bricks, "tissue")
-    after = shift(both, "tissue", -1)
-    before = shift(both, "tissue", 1)
+    after = shift(rate, "tissue", -1)
+    before = shift(rate, "tissue", 1)
     slot_array = intersection_voxel.shape
     prepared = call(
         prepare_kernel,
@@ -508,29 +548,28 @@
         [HBM] * 7,
     )
     region, after, before = lax.optimization_barrier((region, after, before))
-    send, ends = call(
+    send, ends, around = call(
         first_solve_kernel,
         "first_solve",
-        [(BRICKS, 48, 128), (PARTS, 8, 128)],
+        [(BRICKS, 48, 128), (PARTS, 8, 128), (2, 96, 128)],
         [region, *prepared],
         values_scratch,
     )
     received = exchange(send, "tissue")
     ends = exchange(ends, "vessel")
-    up, down, sources = call(
+    near, far, sources = call(
         first_scatter_kernel,
         "first_scatter",
         [(3, 10, 24, 128), (3, 10, 24, 128), (3, 96, 128)],
-        [received, both, after, before],
-        [pltpu.VMEM((3, 192, 128), F32)],
-    )
-    below = shift(up, "vessel", 1)
-    above = shift(down, "vessel", -1)
+        [received, tissue, around, rate, after, before],
+        [pltpu.VMEM((192, 128), F32)] * 3,
+    )
+    near, far = swap(near, 0), swap(far, 1)
     tissue, side, inverse, produced, send = call(
         first_sweeps_kernel,
         "first_sweeps",
         [(96, 128), (96, 128), ring, ring[1:], (BRICKS, 16, 128)],
-        [below, above, both, after, before, sources, received, ends],
+        [near, far, tissue, around, rate, after, before, sources, received, ends],
         [pltpu.VMEM(large_ring, F32)] * 4 + [pltpu.VMEM(large_ring[1:], F32)],
     )
     values = exchange(send, "tissue")
@@ -543,20 +582,19 @@
         [SMEM] + [VMEM] * 3,
     )
     received = exchange(send, "tissue")
-    up, down, sources = call(
+    near, far, sources = call(
         second_scatter_kernel,
         "second_scatter",
         [(3, 7, 16, 128), (3, 7, 16, 128), (2, 96, 128)],
         [received, tissue, side],
-        [pltpu.VMEM((2, 192, 128), F32)],
-    )
-    below = shift(up, "vessel", 1)
-    above = shift(down, "vessel", -1)
+        [pltpu.VMEM((rows, 128), F32) for rows in (192, 96, 96)],
+    )
+    near, far = swap(near, 0), swap(far, 1)
     (tissue,) = call(
         second_sweeps_kernel,
         "second_sweeps",
         [(3, 4, 8, 128)],
-        [below, above, tissue, side, sources, inverse, produced],
+        [near, far, tissue, side, sources, inverse, produced],
         [pltpu.VMEM(ring, F32)] * 3,
     )
     return tissue, vessel

time: 103 us -> 97.1 us (0.943)
  starting transfers between devices: 26.9 us -> 23.9 us
  blocking collectives: 45.8 us -> 43.1 us
    ppermute x6 -> x2, starting transfers between devices: 19.3 us -> 4.55 us  [shift(): return lax.ppermute(value, axis, pairs)]
    ppermute x0 -> x4, starting transfers between devices: none -> 11.7 us  [swap(): lax.ppermute(value, 'vessel', [pair for i in starts for pair in ((i, i +...]
    ppermute x6 -> x2, waiting for transfers between devices: 9.5 us -> 3.65 us  [shift(): return lax.ppermute(value, axis, pairs)]
    ppermute x0 -> x4, waiting for transfers between devices: none -> 4.61 us  [swap(): lax.ppermute(value, 'vessel', [pair for i in starts for pair in ((i, i +...]
    all_to_all x4, blocking collectives: 45.8 us -> 43.1 us  [exchange(): return lax.all_to_all(value, axis, 0, 0, tiled=True)]
    all_to_all x1, waiting for transfers between devices: 0.58 us -> 2.26 us  [exchange(): return lax.all_to_all(value, axis, 0, 0, tiled=True)]
  transfers between devices with their start and end apart: 7 -> 7, of which waited for: 5 -> 4; matrix products, arithmetic and copies ran while one was open for 0% -> 0% of each run, Pallas kernels for 3% -> 3%
where the time goes in v4:
time: 97.1 us; the launch traced here: 96.6 us
  blocking collectives  43.1 us (44%)
  starting transfers between devices  23.9 us (25%)
  Pallas kernels  18.3 us (19%)
  waiting for transfers between devices  10.5 us (11%)
    all_to_all x4, blocking collectives, exchange(): return lax.all_to_all(value, axis, 0, 0, tiled=True)  43.1 us
    pallas_call x8, Pallas kernels, call(): pl.pallas_call(kernel, out_shape=[jax.ShapeDtypeStruct(out, F32) if isins...  18.3 us
    ppermute x4, starting transfers between devices, swap(): lax.ppermute(value, 'vessel', [pair for i in starts for pair in ((i, i +...  11.7 us
    all_to_all x1, starting transfers between devices, exchange(): return lax.all_to_all(value, axis, 0, 0, tiled=True)  7.6 us
    ppermute x4, waiting for transfers between devices, swap(): lax.ppermute(value, 'vessel', [pair for i in starts for pair in ((i, i +...  4.61 us
    ppermute x2, starting transfers between devices, shift(): return lax.ppermute(value, axis, pairs)  4.55 us
    ppermute x2, waiting for transfers between devices, shift(): return lax.ppermute(value, axis, pairs)  3.65 us
    all_to_all x1, waiting for transfers between devices, exchange(): return lax.all_to_all(value, axis, 0, 0, tiled=True)  2.26 us
  transfers between devices with their start and end apart: 7, of which 4 were waited for; matrix products, arithmetic and copies ran while one was open for 0% of the time, Pallas kernels for 3%

profile of v4, /device:TPU:1, one launch (start us, length us, event | category | flops | bytes accessed | tf_op | source)
XLA Modules:
  0.0 96.6 jit_solution(3389544464813958222)
XLA Ops:
  0.6 1.9 %spread.1 = (f32[16,96,128]{2,1,0:T(8,128)}, f32[96,128]{1,0:T(8,128)S(1)}, f32[96,128]{1,0:T(8,128)S(1)}) custom-call(f32[96,128]{1,0:T(8,128)} %bitcast.2, f32[96,128]{1,0:T(8,128)} %bitcast.3), custom_call_target="tpu_custom_call" | custom-call | tf_op jit(solution)/shard_map/spread/pallas_call | solution.py:471
  2.5 7.6 %all-to-all-start = ((f32[16,96,128]{2,1,0:T(8,128)}), f32[16,96,128]{2,1,0:T(8,128)S(1)}, u32[]{:S(2)}, u32[]{:S(2)}) async-start(f32[16,96,128]{2,1,0:T(8,128)} %get-tuple-element.26), calls=%async_computation | async-start | bytes 1572864 | tf_op jit(solution)/shard_map/all_to_all | solution.py:495
  10.1 3.3 %collective-permute-start.1 = (f32[96,128]{1,0:T(8,128)S(1)}, f32[96,128]{1,0:T(8,128)S(1)}, u32[]{:S(2)}, u32[]{:S(2)}) collective-permute-start(f32[96,128]{1,0:T(8,128)S(1)} %get-tuple-element.27.rate_ref), channel_id=1, source_target_pairs={{0,1},{1,2},{2,3},{3,4},{4,5},{5,6},{6,7},{7,8},{8,9},{9,10},{10,1... | collective-permute-start | bytes 147464 | tf_op jit(solution)/shard_map/ppermute | solution.py:500
  13.4 1.3 %collective-permute-start = (f32[96,128]{1,0:T(8,128)S(1)}, f32[96,128]{1,0:T(8,128)S(1)}, u32[]{:S(2)}, u32[]{:S(2)}) collective-permute-start(f32[96,128]{1,0:T(8,128)S(1)} %get-tuple-element.27.rate_ref), channel_id=1, source_target_pairs={{1,0},{2,1},{3,2},{4,3},{5,4},{6,5},{7,6},{8,7},{9,8},{10,9},{11,1... | collective-permute-start | bytes 147464 | tf_op jit(solution)/shard_map/ppermute | solution.py:500
  14.7 2.7 %prepare.1 = (f32[7,16,8,128]{3,2,1,0:T(8,128)S(1)}, bf16[4,16,128,128]{3,2,1,0:T(8,128)(2,1)S(1)}) custom-call(s32[4,16,128]{2,1,0:T(8,128)} %refs_0_.1, f32[4,16,128]{2,1,0:T(8,128)} %refs_1_.1, s32[4,16,128]{2,1,0:T(8,128)} %refs_2_.1, f32[4,256]{1,0:T(4,128)} %refs_3_.1, s32[4,16]{1,0:T(4,128)} %refs_4_.1, f32[3]{0:T(128)} %refs_5_.1, f32[3,4]{1,0:T(4,128)} %refs_6_.1), custom_call_target="tpu_custom_call" | custom-call | tf_op jit(solution)/shard_map/prepare/pallas_call | solution.py:471
  17.4 1.7 %collective-permute-done.1.before_ref = f32[96,128]{1,0:T(8,128)S(1)} collective-permute-done((f32[96,128]{1,0:T(8,128)S(1)}, f32[96,128]{1,0:T(8,128)S(1)}, u32[]{:S(2)}, u32[]{:S(2)}) %collective-permute-start.1) | collective-permute-done | bytes 49184 | tf_op jit(solution)/shard_map/ppermute | solution.py:500
  19.1 1.9 %collective-permute-done.after_ref = f32[96,128]{1,0:T(8,128)S(1)} collective-permute-done((f32[96,128]{1,0:T(8,128)S(1)}, f32[96,128]{1,0:T(8,128)S(1)}, u32[]{:S(2)}, u32[]{:S(2)}) %collective-permute-start) | collective-permute-done | bytes 49184 | tf_op jit(solution)/shard_map/ppermute | solution.py:500
  21.0 2.3 %all-to-all-done.region_ref = f32[16,96,128]{2,1,0:T(8,128)S(1)} async-done(((f32[16,96,128]{2,1,0:T(8,128)}), f32[16,96,128]{2,1,0:T(8,128)S(1)}, u32[]{:S(2)}, u32[]{:S(2)}) %all-to-all-start) | async-done | bytes 786464 | tf_op jit(solution)/shard_map/all_to_all | solution.py:495
  23.3 2.9 %first_solve.1 = (f32[16,48,128]{2,1,0:T(8,128)S(1)}, f32[8,8,128]{2,1,0:T(8,128)S(1)}, f32[2,96,128]{2,1,0:T(8,128)S(1)}) custom-call(f32[16,96,128]{2,1,0:T(8,128)S(1)} %all-to-all-done.region_ref, f32[7,16,8,128]{3,2,1,0:T(8,128)S(1)} %get-tuple-element.29.slots, bf16[4,16,128,128]{3,2,1,0:T(8,128)(2,1)S(1)} %get-tuple-element.30.hots), custom_call_target="tpu_custom_call" | custom-call | tf_op jit(solution)/shard_map/first_solve/pallas_call | solution.py:471
  26.2 0.0 copy-start
  26.2 12.7 %all_to_all.25.recv_ref = f32[16,48,128]{2,1,0:T(8,128)S(1)} all-to-all(f32[16,48,128]{2,1,0:T(8,128)S(1)} %get-tuple-element.31), channel_id=1, replica_groups=mesh['vessel'=8,'tissue'=16] {'tissue'}, dimensions={0} | all-to-all | bytes 786432 | tf_op jit(solution)/shard_map/all_to_all | solution.py:495
  38.8 2.9 %first_scatter.1 = (f32[3,10,24,128]{3,2,1,0:T(8,128)S(1)}, f32[3,10,24,128]{3,2,1,0:T(8,128)S(1)}, f32[3,96,128]{2,1,0:T(8,128)S(1)}) custom-call(f32[16,48,128]{2,1,0:T(8,128)S(1)} %all_to_all.25.recv_ref, f32[96,128]{1,0:T(8,128)S(1)} %get-tuple-element.32.tissue_ref, f32[2,96,128]{2,1,0:T(8,128)S(1)} %get-tuple-element.33.around_ref, ...), custom_call_target="tpu_custom_call" | custom-call | tf_op jit(solution)/shard_map/first_scatter/pallas_call | solution.py:471
  41.7 3.0 %collective-permute-start.2 = (f32[3,10,24,128]{3,2,1,0:T(8,128)S(1)}, f32[3,10,24,128]{3,2,1,0:T(8,128)S(1)}, u32[]{:S(2)}, u32[]{:S(2)}) collective-permute-start(f32[3,10,24,128]{3,2,1,0:T(8,128)S(1)} %get-tuple-element.36), channel_id=1, source_target_pairs={{0,16},{16,0},{32,48},{48,32},{64,80},{80,64},{96,112},{112,96},{1... | collective-permute-start | bytes 1105928 | tf_op jit(solution)/shard_map/ppermute | solution.py:504
  44.7 3.4 %collective-permute-start.3 = (f32[3,10,24,128]{3,2,1,0:T(8,128)S(1)}, f32[3,10,24,128]{3,2,1,0:T(8,128)S(1)}, u32[]{:S(2)}, u32[]{:S(2)}) collective-permute-start(f32[3,10,24,128]{3,2,1,0:T(8,128)S(1)} %get-tuple-element.37), channel_id=1, source_target_pairs={{16,32},{32,16},{48,64},{64,48},{80,96},{96,80},{17,33},{33,17},{4... | collective-permute-start | bytes 1105928 | tf_op jit(solution)/shard_map/ppermute | solution.py:504
  48.2 9.5 %all_to_all.26.ends_ref = f32[8,8,128]{2,1,0:T(8,128)S(1)} all-to-all(f32[8,8,128]{2,1,0:T(8,128)S(1)} %get-tuple-element.39), channel_id=1, replica_groups=mesh['vessel'=8,'tissue'=16] {'vessel'}, dimensions={0} | all-to-all | bytes 65536 | tf_op jit(solution)/shard_map/all_to_all | solution.py:495
  57.7 0.0 collective-permute-done.2.near
  57.7 0.0 collective-permute-done.3.far
  57.7 2.0 %first_sweeps.1 = (f32[96,128]{1,0:T(8,128)S(1)}, f32[96,128]{1,0:T(8,128)S(1)}, f32[3,12,16,128]{3,2,1,0:T(8,128)S(1)}, f32[12,16,128]{2,1,0:T(8,128)S(1)}, f32[16,16,128]{2,1,0:T(8,128)S(1)}) custom-call(f32[3,10,24,128]{3,2,1,0:T(8,128)S(1)} %collective-permute-done.2.near, f32[3,10,24,128]{3,2,1,0:T(8,128)S(1)} %collective-permute-done.3.far, ...), custom_call_target="tpu_custom_call" | custom-call | tf_op jit(solution)/shard_map/first_sweeps/pallas_call | solution.py:471
  59.6 9.5 %all_to_all.27.values_ref = f32[16,16,128]{2,1,0:T(8,128)S(1)} all-to-all(f32[16,16,128]{2,1,0:T(8,128)S(1)} %get-tuple-element.40), channel_id=1, replica_groups=mesh['vessel'=8,'tissue'=16] {'tissue'}, dimensions={0} | all-to-all | bytes 262144 | tf_op jit(solution)/shard_map/all_to_all | solution.py:495
  69.2 0.0 copy-done
  69.2 2.6 %second_solve.1 = (f32[16,48,128]{2,1,0:T(8,128)S(1)}, f32[3,4,256]{2,1,0:T(4,128)}) custom-call(s32[4]{0:T(128)S(1)} %copy-done, f32[16,16,128]{2,1,0:T(8,128)S(1)} %all_to_all.27.values_ref, f32[7,16,8,128]{3,2,1,0:T(8,128)S(1)} %get-tuple-element.29.slots, bf16[4,16,128,128]{3,2,1,0:T(8,128)(2,1)S(1)} %get-tuple-element.30.hots), custom_call_target="tpu_custom_call" | custom-call | tf_op jit(solution)/shard_map/second_solve/pallas_call | solution.py:471
  71.8 11.5 %all_to_all.28.recv_ref = f32[16,48,128]{2,1,0:T(8,128)S(1)} all-to-all(f32[16,48,128]{2,1,0:T(8,128)S(1)} %get-tuple-element.41), channel_id=1, replica_groups=mesh['vessel'=8,'tissue'=16] {'tissue'}, dimensions={0} | all-to-all | bytes 786432 | tf_op jit(solution)/shard_map/all_to_all | solution.py:495
  83.2 2.4 %second_scatter.1 = (f32[3,7,16,128]{3,2,1,0:T(8,128)S(1)}, f32[3,7,16,128]{3,2,1,0:T(8,128)S(1)}, f32[2,96,128]{2,1,0:T(8,128)S(1)}) custom-call(f32[16,48,128]{2,1,0:T(8,128)S(1)} %all_to_all.28.recv_ref, f32[96,128]{1,0:T(8,128)S(1)} %get-tuple-element.42.tissue_ref, f32[96,128]{1,0:T(8,128)S(1)} %get-tuple-element.43.side_ref), custom_call_target="tpu_custom_call" | custom-call | tf_op jit(solution)/shard_map/second_scatter/pallas_call | solution.py:471
  85.7 3.2 %collective-permute-start.4 = (f32[3,7,16,128]{3,2,1,0:T(8,128)S(1)}, f32[3,7,16,128]{3,2,1,0:T(8,128)S(1)}, u32[]{:S(2)}, u32[]{:S(2)}) collective-permute-start(f32[3,7,16,128]{3,2,1,0:T(8,128)S(1)} %get-tuple-element.44), channel_id=1, source_target_pairs={{0,16},{16,0},{32,48},{48,32},{64,80},{80,64},{96,112},{112,96},{1... | collective-permute-start | bytes 516104 | tf_op jit(solution)/shard_map/ppermute | solution.py:504
  88.8 2.1 %collective-permute-start.5 = (f32[3,7,16,128]{3,2,1,0:T(8,128)S(1)}, f32[3,7,16,128]{3,2,1,0:T(8,128)S(1)}, u32[]{:S(2)}, u32[]{:S(2)}) collective-permute-start(f32[3,7,16,128]{3,2,1,0:T(8,128)S(1)} %get-tuple-element.45), channel_id=1, source_target_pairs={{16,32},{32,16},{48,64},{64,48},{80,96},{96,80},{17,33},{33,17},{4... | collective-permute-start | bytes 516104 | tf_op jit(solution)/shard_map/ppermute | solution.py:504
  90.9 0.0 collective-permute-done.4.near
  90.9 4.6 %collective-permute-done.5.far = f32[3,7,16,128]{3,2,1,0:T(8,128)S(1)} collective-permute-done((f32[3,7,16,128]{3,2,1,0:T(8,128)S(1)}, f32[3,7,16,128]{3,2,1,0:T(8,128)S(1)}, u32[]{:S(2)}, u32[]{:S(2)}) %collective-permute-start.5) | collective-permute-done | bytes 172064 | tf_op jit(solution)/shard_map/ppermute | solution.py:504
  95.5 1.1 %second_sweeps.1 = f32[3,4,8,128]{3,2,1,0:T(8,128)} custom-call(f32[3,7,16,128]{3,2,1,0:T(8,128)S(1)} %collective-permute-done.4.near, f32[3,7,16,128]{3,2,1,0:T(8,128)S(1)} %collective-permute-done.5.far, f32[96,128]{1,0:T(8,128)S(1)} %get-tuple-element.42.tissue_ref, f32[96,128]{1,0:T(8,128)S(1)} %get-tuple-element.43.side_ref, ...), custom_call_target="tpu_custom_call" | custom-call | tf_op jit(solution)/shard_map/second_sweeps/pallas_call | solution.py:471
Async XLA Ops:
  2.5 20.8 %all-to-all-start = ((f32[16,96,128]{2,1,0:T(8,128)}), f32[16,96,128]{2,1,0:T(8,128)S(1)}, u32[]{:S(2)}, u32[]{:S(2)}) async-start(f32[16,96,128]{2,1,0:T(8,128)} %get-tuple-element.26), calls=%async_computation | async-start | bytes 1572864 | tf_op jit(solution)/shard_map/all_to_all | solution.py:495
  10.1 9.0 %collective-permute-start.1 = (f32[96,128]{1,0:T(8,128)S(1)}, f32[96,128]{1,0:T(8,128)S(1)}, u32[]{:S(2)}, u32[]{:S(2)}) collective-permute-start(f32[96,128]{1,0:T(8,128)S(1)} %get-tuple-element.27.rate_ref), channel_id=1, source_target_pairs={{0,1},{1,2},{2,3},{3,4},{4,5},{5,6},{6,7},{7,8},{8,9},{9,10},{10,1... | collective-permute-start | bytes 147464 | tf_op jit(solution)/shard_map/ppermute | solution.py:500
  13.4 7.6 %collective-permute-start = (f32[96,128]{1,0:T(8,128)S(1)}, f32[96,128]{1,0:T(8,128)S(1)}, u32[]{:S(2)}, u32[]{:S(2)}) collective-permute-start(f32[96,128]{1,0:T(8,128)S(1)} %get-tuple-element.27.rate_ref), channel_id=1, source_target_pairs={{1,0},{2,1},{3,2},{4,3},{5,4},{6,5},{7,6},{8,7},{9,8},{10,9},{11,1... | collective-permute-start | bytes 147464 | tf_op jit(solution)/shard_map/ppermute | solution.py:500
  26.2 43.0 %copy-start = (s32[4]{0:T(128)S(1)}, s32[4]{0:T(128)}, u32[]{:S(2)}) copy-start(s32[4]{0:T(128)} %upstream_ref.1) | copy-start | bytes 52
  41.7 16.0 %collective-permute-start.2 = (f32[3,10,24,128]{3,2,1,0:T(8,128)S(1)}, f32[3,10,24,128]{3,2,1,0:T(8,128)S(1)}, u32[]{:S(2)}, u32[]{:S(2)}) collective-permute-start(f32[3,10,24,128]{3,2,1,0:T(8,128)S(1)} %get-tuple-element.36), channel_id=1, source_target_pairs={{0,16},{16,0},{32,48},{48,32},{64,80},{80,64},{96,112},{112,96},{1... | collective-permute-start | bytes 1105928 | tf_op jit(solution)/shard_map/ppermute | solution.py:504
  44.7 12.9 %collective-permute-start.3 = (f32[3,10,24,128]{3,2,1,0:T(8,128)S(1)}, f32[3,10,24,128]{3,2,1,0:T(8,128)S(1)}, u32[]{:S(2)}, u32[]{:S(2)}) collective-permute-start(f32[3,10,24,128]{3,2,1,0:T(8,128)S(1)} %get-tuple-element.37), channel_id=1, source_target_pairs={{16,32},{32,16},{48,64},{64,48},{80,96},{96,80},{17,33},{33,17},{4... | collective-permute-start | bytes 1105928 | tf_op jit(solution)/shard_map/ppermute | solution.py:504
  85.7 5.3 %collective-permute-start.4 = (f32[3,7,16,128]{3,2,1,0:T(8,128)S(1)}, f32[3,7,16,128]{3,2,1,0:T(8,128)S(1)}, u32[]{:S(2)}, u32[]{:S(2)}) collective-permute-start(f32[3,7,16,128]{3,2,1,0:T(8,128)S(1)} %get-tuple-element.44), channel_id=1, source_target_pairs={{0,16},{16,0},{32,48},{48,32},{64,80},{80,64},{96,112},{112,96},{1... | collective-permute-start | bytes 516104 | tf_op jit(solution)/shard_map/ppermute | solution.py:504
  88.8 6.7 %collective-permute-start.5 = (f32[3,7,16,128]{3,2,1,0:T(8,128)S(1)}, f32[3,7,16,128]{3,2,1,0:T(8,128)S(1)}, u32[]{:S(2)}, u32[]{:S(2)}) collective-permute-start(f32[3,7,16,128]{3,2,1,0:T(8,128)S(1)} %get-tuple-element.45), channel_id=1, source_target_pairs={{16,32},{32,16},{48,64},{64,48},{80,96},{96,80},{17,33},{33,17},{4... | collective-permute-start | bytes 516104 | tf_op jit(solution)/shard_map/ppermute | solution.py:504

commit v5 on v4

--- a/solution.py
+++ b/solution.py
@@ -306,7 +306,7 @@
             source[...] += matmul_nt(jnp.concatenate(parts, axis=1), jnp.concatenate(hots, axis=1))
         return carry
 
-    lax.fori_loop(0, BRICKS // SENDERS, senders, 0, unroll=2)
+    lax.fori_loop(0, BRICKS // SENDERS, senders, 0, unroll=4)
     return [source[0 : 3 * size] + source[3 * size : 6 * size] for source, _, size in sources]
 
 
@@ -322,13 +322,18 @@
     return value.reshape(3, 4, 8, 128)
 
 
-def is_even():
-    return lax.axis_index("vessel") % 2 == 0
-
-
-def toward(value, near):
-    upward = is_even() if near else ~is_even()
-    return jnp.where(upward, value[:, 1:4], value[:, 0:3])
+def is_even(axis):
+    return lax.axis_index(axis) % 2 == 0
+
+
+def in_order(axis, near, far):
+    even = is_even(axis)
+    return jnp.where(even, far, near), jnp.where(even, near, far)
+
+
+def toward(value, near, count=3):
+    upward = is_even("vessel") if near else ~is_even("vessel")
+    return jnp.where(upward, value[:, 4 - count : 4], value[:, 0:count])
 
 
 def write_messages(tissues, sources, near_ref, far_ref):
@@ -341,17 +346,17 @@
 
 
 def first_scatter_kernel(
-    recv_ref, tissue_ref, around_ref, rate_ref, after_ref, before_ref, near_ref, far_ref, sources_ref, *sums
+    recv_ref, tissue_ref, around_ref, rate_ref, rate_near_ref, rate_far_ref, near_ref, far_ref, sources_ref, *sums
 ):
     sources = scatter_slots(recv_ref, [(sums[i], (16 * i, 16 * i + 8), 32) for i in range(3)])
     for i in range(3):
         sources_ref[i] = sources[i]
     write_messages([tissue_ref[...], around_ref[0], around_ref[1]], sources, near_ref, far_ref)
-    for i, ref in enumerate((rate_ref, after_ref, before_ref)):
+    before, after = in_order("tissue", rate_near_ref[...], rate_far_ref[...])
+    for i, value in enumerate((rate_ref[...], after, before)):
         here = slice(8 * i, 8 * i + 8)
-        value = planes(ref[...])
-        near_ref[:, 7:10, here] = toward(value, True)
-        far_ref[:, 7:10, here] = toward(value, False)
+        near_ref[:, 7:10, here] = toward(planes(value), True)
+        far_ref[:, 7:10, here] = toward(planes(value), False)
 
 
 def second_scatter_kernel(recv_ref, tissue_ref, side_ref, near_ref, far_ref, sources_ref, *sums):
@@ -361,18 +366,17 @@
     sources = [own, interleave(first, last)]
     for i in range(2):
         sources_ref[i] = sources[i]
-    write_messages([tissue_ref[...], side_ref[...]], sources, near_ref, far_ref)
-
-
-def neighbours(near, far, k, where):
-    near, far = near[k, where], far[k, where]
-    return jnp.where(is_even(), far, near), jnp.where(is_even(), near, far)
-
-
-def fill(now, source, near, far, tissues, sources):
+    tissue, side = planes(tissue_ref[...]), planes(side_ref[...])
+    own, beyond = planes(sources[0]), planes(sources[1])
+    for ref, near in ((near_ref, True), (far_ref, False)):
+        ref[:, 0:4] = tissue
+        ref[:, 4:7] = toward(own, near)
+        ref[:, 7:10] = toward(side, near)
+        ref[:, 10:12] = toward(beyond, near, 2)
+
+
+def fill(now, source, tissues, sources):
     for k in range(3):
-        now[k, 0:4], now[k, 8:12] = neighbours(near, far, k, slice(0, 4))
-        source[k, 1:4], source[k, 8:11] = neighbours(near, far, k, slice(4, 7))
         for i in range(len(tissues)):
             now[k, 4:8, 8 * i : 8 * i + 8] = planes(tissues[i])[k]
             source[k, 4:8, 8 * i : 8 * i + 8] = planes(sources[i])[k]
@@ -404,14 +408,17 @@
 
 
 def first_sweeps_kernel(
-    near, far, tissue_ref, around_ref, rate_ref, after_ref, before_ref, sources_ref, recv_ref, ends_ref,
+    near, far, tissue_ref, around_ref, rate_ref, rate_near_ref, rate_far_ref, sources_ref, recv_ref, ends_ref,
     out_ref, side_ref, inverse_ref, produced_ref, send_ref, now, later, source, inverse, produced,
 ):
     tissues = [tissue_ref[...], around_ref[0], around_ref[1]]
-    fill(now, source, near, far, tissues, [sources_ref[i] for i in range(3)])
+    fill(now, source, tissues, [sources_ref[i] for i in range(3)])
+    before, after = in_order("tissue", rate_near_ref[...], rate_far_ref[...])
     for k in range(3):
-        rates = [planes(ref[...])[k] for ref in (rate_ref, after_ref, before_ref)]
-        below, above = neighbours(near, far, k, slice(7, 10))
+        now[k, 0:4], now[k, 8:12] = in_order("vessel", near[k, 0:4], far[k, 0:4])
+        source[k, 1:4], source[k, 8:11] = in_order("vessel", near[k, 4:7], far[k, 4:7])
+        rates = [planes(value)[k] for value in (rate_ref[...], after, before)]
+        below, above = in_order("vessel", near[k, 7:10], far[k, 7:10])
         for z in range(1, 11):
             if z < 4:
                 rate = below[z - 1]
@@ -452,7 +459,16 @@
 def second_sweeps_kernel(
     near, far, tissue_ref, side_ref, sources_ref, inverse, produced, out_ref, now, later, source
 ):
-    fill(now, source, near, far, [tissue_ref[...], side_ref[...]], [sources_ref[i] for i in range(2)])
+    fill(now, source, [tissue_ref[...], side_ref[...]], [sources_ref[i] for i in range(2)])
+    zero = jnp.zeros((8, 128), F32)
+    for k in range(3):
+        below, above = in_order("vessel", near[k], far[k])
+        now[k, 0:4, 0:8], now[k, 8:12, 0:8] = below[0:4], above[0:4]
+        source[k, 1:4, 0:8], source[k, 8:11, 0:8] = below[4:7], above[4:7]
+        now[k, 1:4, 8:16], now[k, 8:11, 8:16] = below[7:10], above[7:10]
+        source[k, 2:4, 8:16], source[k, 8:10, 8:16] = below[10:12], above[10:12]
+        now[k, 0, 8:16] = now[k, 11, 8:16] = zero
+        source[k, 1, 8:16] = source[k, 10, 8:16] = zero
     final = run_sweeps(now, later, source, inverse, produced)
     out_ref[...] = final[:, 4:8, 0:8]
 
@@ -494,14 +510,9 @@
     def exchange(value, axis):
         return lax.all_to_all(value, axis, 0, 0, tiled=True)
 
-    def shift(value, axis, step):
-        size = lax.axis_size(axis)
-        pairs = [(i, i + step) for i in range(size) if 0 <= i + step < size]
-        return lax.ppermute(value, axis, pairs)
-
-    def swap(value, first):
-        starts = range(first, lax.axis_size("vessel") - 1, 2)
-        return lax.ppermute(value, "vessel", [pair for i in starts for pair in ((i, i + 1), (i + 1, i))])
+    def swap(value, axis, first):
+        starts = range(first, lax.axis_size(axis) - 1, 2)
+        return lax.ppermute(value, axis, [pair for i in starts for pair in ((i, i + 1), (i + 1, i))])
 
     ring, large_ring = (3, 12, 16, 128), (3, 12, 24, 128)
     values_scratch = [pltpu.VMEM((2, BRICKS, 8, 128), F32)]
@@ -516,8 +527,7 @@
         [HBM, VMEM, VMEM],
     )
     region = exchange(bricks, "tissue")
-    after = shift(rate, "tissue", -1)
-    before = shift(rate, "tissue", 1)
+    rate_near, rate_far = swap(rate, "tissue", 0), swap(rate, "tissue", 1)
     slot_array = intersection_voxel.shape
     prepared = call(
         prepare_kernel,
@@ -547,7 +557,7 @@
         ],
         [HBM] * 7,
     )
-    region, after, before = lax.optimization_barrier((region, after, before))
+    region, rate_near, rate_far = lax.optimization_barrier((region, rate_near, rate_far))
     send, ends, around = call(
         first_solve_kernel,
         "first_solve",
@@ -561,15 +571,15 @@
         first_scatter_kernel,
         "first_scatter",
         [(3, 10, 24, 128), (3, 10, 24, 128), (3, 96, 128)],
-        [received, tissue, around, rate, after, before],
+        [received, tissue, around, rate, rate_near, rate_far],
         [pltpu.VMEM((192, 128), F32)] * 3,
     )
-    near, far = swap(near, 0), swap(far, 1)
+    near, far = swap(near, "vessel", 0), swap(far, "vessel", 1)
     tissue, side, inverse, produced, send = call(
         first_sweeps_kernel,
         "first_sweeps",
         [(96, 128), (96, 128), ring, ring[1:], (BRICKS, 16, 128)],
-        [near, far, tissue, around, rate, after, before, sources, received, ends],
+        [near, far, tissue, around, rate, rate_near, rate_far, sources, received, ends],
         [pltpu.VMEM(large_ring, F32)] * 4 + [pltpu.VMEM(large_ring[1:], F32)],
     )
     values = exchange(send, "tissue")
@@ -585,11 +595,11 @@
     near, far, sources = call(
         second_scatter_kernel,
         "second_scatter",
-        [(3, 7, 16, 128), (3, 7, 16, 128), (2, 96, 128)],
+        [(3, 12, 8, 128), (3, 12, 8, 128), (2, 96, 128)],
         [received, tissue, side],
         [pltpu.VMEM((rows, 128), F32) for rows in (192, 96, 96)],
     )
-    near, far = swap(near, 0), swap(far, 1)
+    near, far = swap(near, "vessel", 0), swap(far, "vessel", 1)
     (tissue,) = call(
         second_sweeps_kernel,
         "second_sweeps",

time: 97.1 us -> 96.2 us (level)
  transfers between devices with their start and end apart: 7 -> 7, of which waited for: 4 -> 3; matrix products, arithmetic and copies ran while one was open for 0% -> 0% of each run, Pallas kernels for 3% -> 3%
where the time goes in v5:
time: 96.2 us; the launch traced here: 95.7 us
  blocking collectives  43.6 us (45%)
  starting transfers between devices  23.3 us (24%)
  Pallas kernels  17.8 us (19%)
  waiting for transfers between devices  10.3 us (11%)
    all_to_all x4, blocking collectives, exchange(): return lax.all_to_all(value, axis, 0, 0, tiled=True)  43.6 us
    pallas_call x8, Pallas kernels, call(): pl.pallas_call(kernel, out_shape=[jax.ShapeDtypeStruct(out, F32) if isins...  17.8 us
    ppermute x6, starting transfers between devices, swap(): lax.ppermute(value, axis, [pair for i in starts for pair in ((i, i + 1),...  15.7 us
    ppermute x6, waiting for transfers between devices, swap(): lax.ppermute(value, axis, [pair for i in starts for pair in ((i, i + 1),...  8.03 us
    all_to_all x1, starting transfers between devices, exchange(): return lax.all_to_all(value, axis, 0, 0, tiled=True)  7.6 us
    all_to_all x1, waiting for transfers between devices, exchange(): return lax.all_to_all(value, axis, 0, 0, tiled=True)  2.26 us
  transfers between devices with their start and end apart: 7, of which 3 were waited for; matrix products, arithmetic and copies ran while one was open for 0% of the time, Pallas kernels for 3%

profile of v5, /device:TPU:1, one launch (start us, length us, event | category | flops | bytes accessed | tf_op | source)
XLA Modules:
  0.0 95.7 jit_solution(3731625361100081032)
XLA Ops:
  0.6 1.9 %spread.1 = (f32[16,96,128]{2,1,0:T(8,128)}, f32[96,128]{1,0:T(8,128)S(1)}, f32[96,128]{1,0:T(8,128)S(1)}) custom-call(f32[96,128]{1,0:T(8,128)} %bitcast.2, f32[96,128]{1,0:T(8,128)} %bitcast.3), custom_call_target="tpu_custom_call" | custom-call | tf_op jit(solution)/shard_map/spread/pallas_call | solution.py:487
  2.5 7.6 %all-to-all-start = ((f32[16,96,128]{2,1,0:T(8,128)}), f32[16,96,128]{2,1,0:T(8,128)S(1)}, u32[]{:S(2)}, u32[]{:S(2)}) async-start(f32[16,96,128]{2,1,0:T(8,128)} %get-tuple-element.26), calls=%async_computation | async-start | bytes 1572864 | tf_op jit(solution)/shard_map/all_to_all | solution.py:511
  10.1 0.7 collective-permute-start.1
  10.8 3.9 %collective-permute-start = (f32[96,128]{1,0:T(8,128)S(1)}, f32[96,128]{1,0:T(8,128)S(1)}, u32[]{:S(2)}, u32[]{:S(2)}) collective-permute-start(f32[96,128]{1,0:T(8,128)S(1)} %get-tuple-element.27.rate_ref), channel_id=1, source_target_pairs={{0,1},{1,0},{2,3},{3,2},{4,5},{5,4},{6,7},{7,6},{8,9},{9,8},{10,11... | collective-permute-start | bytes 147464 | tf_op jit(solution)/shard_map/ppermute | solution.py:515
  14.6 2.7 %prepare.1 = (f32[7,16,8,128]{3,2,1,0:T(8,128)S(1)}, bf16[4,16,128,128]{3,2,1,0:T(8,128)(2,1)S(1)}) custom-call(s32[4,16,128]{2,1,0:T(8,128)} %refs_0_.1, f32[4,16,128]{2,1,0:T(8,128)} %refs_1_.1, s32[4,16,128]{2,1,0:T(8,128)} %refs_2_.1, f32[4,256]{1,0:T(4,128)} %refs_3_.1, s32[4,16]{1,0:T(4,128)} %refs_4_.1, f32[3]{0:T(128)} %refs_5_.1, f32[3,4]{1,0:T(4,128)} %refs_6_.1), custom_call_target="tpu_custom_call" | custom-call | tf_op jit(solution)/shard_map/prepare/pallas_call | solution.py:487
  17.3 0.0 collective-permute-done.1.rate_far_ref
  17.3 3.7 %collective-permute-done.rate_near_ref = f32[96,128]{1,0:T(8,128)S(1)} collective-permute-done((f32[96,128]{1,0:T(8,128)S(1)}, f32[96,128]{1,0:T(8,128)S(1)}, u32[]{:S(2)}, u32[]{:S(2)}) %collective-permute-start) | collective-permute-done | bytes 49184 | tf_op jit(solution)/shard_map/ppermute | solution.py:515
  21.0 2.3 %all-to-all-done.region_ref = f32[16,96,128]{2,1,0:T(8,128)S(1)} async-done(((f32[16,96,128]{2,1,0:T(8,128)}), f32[16,96,128]{2,1,0:T(8,128)S(1)}, u32[]{:S(2)}, u32[]{:S(2)}) %all-to-all-start) | async-done | bytes 786464 | tf_op jit(solution)/shard_map/all_to_all | solution.py:511
  23.3 2.9 %first_solve.1 = (f32[16,48,128]{2,1,0:T(8,128)S(1)}, f32[8,8,128]{2,1,0:T(8,128)S(1)}, f32[2,96,128]{2,1,0:T(8,128)S(1)}) custom-call(f32[16,96,128]{2,1,0:T(8,128)S(1)} %all-to-all-done.region_ref, f32[7,16,8,128]{3,2,1,0:T(8,128)S(1)} %get-tuple-element.29.slots, bf16[4,16,128,128]{3,2,1,0:T(8,128)(2,1)S(1)} %get-tuple-element.30.hots), custom_call_target="tpu_custom_call" | custom-call | tf_op jit(solution)/shard_map/first_solve/pallas_call | solution.py:487
  26.2 0.0 copy-start
  26.2 13.1 %all_to_all.25.recv_ref = f32[16,48,128]{2,1,0:T(8,128)S(1)} all-to-all(f32[16,48,128]{2,1,0:T(8,128)S(1)} %get-tuple-element.31), channel_id=1, replica_groups=mesh['vessel'=8,'tissue'=16] {'tissue'}, dimensions={0} | all-to-all | bytes 786432 | tf_op jit(solution)/shard_map/all_to_all | solution.py:511
  39.3 2.6 %first_scatter.1 = (f32[3,10,24,128]{3,2,1,0:T(8,128)S(1)}, f32[3,10,24,128]{3,2,1,0:T(8,128)S(1)}, f32[3,96,128]{2,1,0:T(8,128)S(1)}) custom-call(f32[16,48,128]{2,1,0:T(8,128)S(1)} %all_to_all.25.recv_ref, f32[96,128]{1,0:T(8,128)S(1)} %get-tuple-element.32.tissue_ref, f32[2,96,128]{2,1,0:T(8,128)S(1)} %get-tuple-element.33.around_ref, ...), custom_call_target="tpu_custom_call" | custom-call | tf_op jit(solution)/shard_map/first_scatter/pallas_call | solution.py:487
  41.9 2.4 %collective-permute-start.2 = (f32[3,10,24,128]{3,2,1,0:T(8,128)S(1)}, f32[3,10,24,128]{3,2,1,0:T(8,128)S(1)}, u32[]{:S(2)}, u32[]{:S(2)}) collective-permute-start(f32[3,10,24,128]{3,2,1,0:T(8,128)S(1)} %get-tuple-element.36), channel_id=1, source_target_pairs={{0,16},{16,0},{32,48},{48,32},{64,80},{80,64},{96,112},{112,96},{1... | collective-permute-start | bytes 1105928 | tf_op jit(solution)/shard_map/ppermute | solution.py:515
  44.3 3.4 %collective-permute-start.3 = (f32[3,10,24,128]{3,2,1,0:T(8,128)S(1)}, f32[3,10,24,128]{3,2,1,0:T(8,128)S(1)}, u32[]{:S(2)}, u32[]{:S(2)}) collective-permute-start(f32[3,10,24,128]{3,2,1,0:T(8,128)S(1)} %get-tuple-element.37), channel_id=1, source_target_pairs={{16,32},{32,16},{48,64},{64,48},{80,96},{96,80},{17,33},{33,17},{4... | collective-permute-start | bytes 1105928 | tf_op jit(solution)/shard_map/ppermute | solution.py:515
  47.8 9.5 %all_to_all.26.ends_ref = f32[8,8,128]{2,1,0:T(8,128)S(1)} all-to-all(f32[8,8,128]{2,1,0:T(8,128)S(1)} %get-tuple-element.39), channel_id=1, replica_groups=mesh['vessel'=8,'tissue'=16] {'vessel'}, dimensions={0} | all-to-all | bytes 65536 | tf_op jit(solution)/shard_map/all_to_all | solution.py:511
  57.2 0.0 collective-permute-done.2.near
  57.3 0.0 collective-permute-done.3.far
  57.3 2.0 %first_sweeps.1 = (f32[96,128]{1,0:T(8,128)S(1)}, f32[96,128]{1,0:T(8,128)S(1)}, f32[3,12,16,128]{3,2,1,0:T(8,128)S(1)}, f32[12,16,128]{2,1,0:T(8,128)S(1)}, f32[16,16,128]{2,1,0:T(8,128)S(1)}) custom-call(f32[3,10,24,128]{3,2,1,0:T(8,128)S(1)} %collective-permute-done.2.near, f32[3,10,24,128]{3,2,1,0:T(8,128)S(1)} %collective-permute-done.3.far, ...), custom_call_target="tpu_custom_call" | custom-call | tf_op jit(solution)/shard_map/first_sweeps/pallas_call | solution.py:487
  59.2 9.6 %all_to_all.27.values_ref = f32[16,16,128]{2,1,0:T(8,128)S(1)} all-to-all(f32[16,16,128]{2,1,0:T(8,128)S(1)} %get-tuple-element.40), channel_id=1, replica_groups=mesh['vessel'=8,'tissue'=16] {'tissue'}, dimensions={0} | all-to-all | bytes 262144 | tf_op jit(solution)/shard_map/all_to_all | solution.py:511
  68.8 0.0 copy-done
  68.8 2.6 %second_solve.1 = (f32[16,48,128]{2,1,0:T(8,128)S(1)}, f32[3,4,256]{2,1,0:T(4,128)}) custom-call(s32[4]{0:T(128)S(1)} %copy-done, f32[16,16,128]{2,1,0:T(8,128)S(1)} %all_to_all.27.values_ref, f32[7,16,8,128]{3,2,1,0:T(8,128)S(1)} %get-tuple-element.29.slots, bf16[4,16,128,128]{3,2,1,0:T(8,128)(2,1)S(1)} %get-tuple-element.30.hots), custom_call_target="tpu_custom_call" | custom-call | tf_op jit(solution)/shard_map/second_solve/pallas_call | solution.py:487
  71.4 11.5 %all_to_all.28.recv_ref = f32[16,48,128]{2,1,0:T(8,128)S(1)} all-to-all(f32[16,48,128]{2,1,0:T(8,128)S(1)} %get-tuple-element.41), channel_id=1, replica_groups=mesh['vessel'=8,'tissue'=16] {'tissue'}, dimensions={0} | all-to-all | bytes 786432 | tf_op jit(solution)/shard_map/all_to_all | solution.py:511
  82.8 2.2 %second_scatter.1 = (f32[3,12,8,128]{3,2,1,0:T(8,128)S(1)}, f32[3,12,8,128]{3,2,1,0:T(8,128)S(1)}, f32[2,96,128]{2,1,0:T(8,128)S(1)}) custom-call(f32[16,48,128]{2,1,0:T(8,128)S(1)} %all_to_all.28.recv_ref, f32[96,128]{1,0:T(8,128)S(1)} %get-tuple-element.42.tissue_ref, f32[96,128]{1,0:T(8,128)S(1)} %get-tuple-element.43.side_ref), custom_call_target="tpu_custom_call" | custom-call | tf_op jit(solution)/shard_map/second_scatter/pallas_call | solution.py:487
  85.0 3.2 %collective-permute-start.4 = (f32[3,12,8,128]{3,2,1,0:T(8,128)S(1)}, f32[3,12,8,128]{3,2,1,0:T(8,128)S(1)}, u32[]{:S(2)}, u32[]{:S(2)}) collective-permute-start(f32[3,12,8,128]{3,2,1,0:T(8,128)S(1)} %get-tuple-element.44), channel_id=1, source_target_pairs={{0,16},{16,0},{32,48},{48,32},{64,80},{80,64},{96,112},{112,96},{1... | collective-permute-start | bytes 442376 | tf_op jit(solution)/shard_map/ppermute | solution.py:515
  88.2 2.1 %collective-permute-start.5 = (f32[3,12,8,128]{3,2,1,0:T(8,128)S(1)}, f32[3,12,8,128]{3,2,1,0:T(8,128)S(1)}, u32[]{:S(2)}, u32[]{:S(2)}) collective-permute-start(f32[3,12,8,128]{3,2,1,0:T(8,128)S(1)} %get-tuple-element.45), channel_id=1, source_target_pairs={{16,32},{32,16},{48,64},{64,48},{80,96},{96,80},{17,33},{33,17},{4... | collective-permute-start | bytes 442376 | tf_op jit(solution)/shard_map/ppermute | solution.py:515
  90.3 0.0 collective-permute-done.4.near
  90.3 4.3 %collective-permute-done.5.far = f32[3,12,8,128]{3,2,1,0:T(8,128)S(1)} collective-permute-done((f32[3,12,8,128]{3,2,1,0:T(8,128)S(1)}, f32[3,12,8,128]{3,2,1,0:T(8,128)S(1)}, u32[]{:S(2)}, u32[]{:S(2)}) %collective-permute-start.5) | collective-permute-done | bytes 147488 | tf_op jit(solution)/shard_map/ppermute | solution.py:515
  94.6 1.1 %second_sweeps.1 = f32[3,4,8,128]{3,2,1,0:T(8,128)} custom-call(f32[3,12,8,128]{3,2,1,0:T(8,128)S(1)} %collective-permute-done.4.near, f32[3,12,8,128]{3,2,1,0:T(8,128)S(1)} %collective-permute-done.5.far, f32[96,128]{1,0:T(8,128)S(1)} %get-tuple-element.42.tissue_ref, f32[96,128]{1,0:T(8,128)S(1)} %get-tuple-element.43.side_ref, ...), custom_call_target="tpu_custom_call" | custom-call | tf_op jit(solution)/shard_map/second_sweeps/pallas_call | solution.py:487
Async XLA Ops:
  2.5 20.8 %all-to-all-start = ((f32[16,96,128]{2,1,0:T(8,128)}), f32[16,96,128]{2,1,0:T(8,128)S(1)}, u32[]{:S(2)}, u32[]{:S(2)}) async-start(f32[16,96,128]{2,1,0:T(8,128)} %get-tuple-element.26), calls=%async_computation | async-start | bytes 1572864 | tf_op jit(solution)/shard_map/all_to_all | solution.py:511
  10.1 7.2 %collective-permute-start.1 = (f32[96,128]{1,0:T(8,128)S(1)}, f32[96,128]{1,0:T(8,128)S(1)}, u32[]{:S(2)}, u32[]{:S(2)}) collective-permute-start(f32[96,128]{1,0:T(8,128)S(1)} %get-tuple-element.27.rate_ref), channel_id=1, source_target_pairs={{1,2},{2,1},{3,4},{4,3},{5,6},{6,5},{7,8},{8,7},{9,10},{10,9},{11,... | collective-permute-start | bytes 147464 | tf_op jit(solution)/shard_map/ppermute | solution.py:515
  10.8 10.2 %collective-permute-start = (f32[96,128]{1,0:T(8,128)S(1)}, f32[96,128]{1,0:T(8,128)S(1)}, u32[]{:S(2)}, u32[]{:S(2)}) collective-permute-start(f32[96,128]{1,0:T(8,128)S(1)} %get-tuple-element.27.rate_ref), channel_id=1, source_target_pairs={{0,1},{1,0},{2,3},{3,2},{4,5},{5,4},{6,7},{7,6},{8,9},{9,8},{10,11... | collective-permute-start | bytes 147464 | tf_op jit(solution)/shard_map/ppermute | solution.py:515
  26.2 42.6 %copy-start = (s32[4]{0:T(128)S(1)}, s32[4]{0:T(128)}, u32[]{:S(2)}) copy-start(s32[4]{0:T(128)} %upstream_ref.1) | copy-start | bytes 52
  41.9 15.4 %collective-permute-start.2 = (f32[3,10,24,128]{3,2,1,0:T(8,128)S(1)}, f32[3,10,24,128]{3,2,1,0:T(8,128)S(1)}, u32[]{:S(2)}, u32[]{:S(2)}) collective-permute-start(f32[3,10,24,128]{3,2,1,0:T(8,128)S(1)} %get-tuple-element.36), channel_id=1, source_target_pairs={{0,16},{16,0},{32,48},{48,32},{64,80},{80,64},{96,112},{112,96},{1... | collective-permute-start | bytes 1105928 | tf_op jit(solution)/shard_map/ppermute | solution.py:515
  44.3 12.9 %collective-permute-start.3 = (f32[3,10,24,128]{3,2,1,0:T(8,128)S(1)}, f32[3,10,24,128]{3,2,1,0:T(8,128)S(1)}, u32[]{:S(2)}, u32[]{:S(2)}) collective-permute-start(f32[3,10,24,128]{3,2,1,0:T(8,128)S(1)} %get-tuple-element.37), channel_id=1, source_target_pairs={{16,32},{32,16},{48,64},{64,48},{80,96},{96,80},{17,33},{33,17},{4... | collective-permute-start | bytes 1105928 | tf_op jit(solution)/shard_map/ppermute | solution.py:515
  85.0 5.3 %collective-permute-start.4 = (f32[3,12,8,128]{3,2,1,0:T(8,128)S(1)}, f32[3,12,8,128]{3,2,1,0:T(8,128)S(1)}, u32[]{:S(2)}, u32[]{:S(2)}) collective-permute-start(f32[3,12,8,128]{3,2,1,0:T(8,128)S(1)} %get-tuple-element.44), channel_id=1, source_target_pairs={{0,16},{16,0},{32,48},{48,32},{64,80},{80,64},{96,112},{112,96},{1... | collective-permute-start | bytes 442376 | tf_op jit(solution)/shard_map/ppermute | solution.py:515
  88.2 6.5 %collective-permute-start.5 = (f32[3,12,8,128]{3,2,1,0:T(8,128)S(1)}, f32[3,12,8,128]{3,2,1,0:T(8,128)S(1)}, u32[]{:S(2)}, u32[]{:S(2)}) collective-permute-start(f32[3,12,8,128]{3,2,1,0:T(8,128)S(1)} %get-tuple-element.45), channel_id=1, source_target_pairs={{16,32},{32,16},{48,64},{64,48},{80,96},{96,80},{17,33},{33,17},{4... | collective-permute-start | bytes 442376 | tf_op jit(solution)/shard_map/ppermute | solution.py:515

commit v6 on v5

--- a/solution.py
+++ b/solution.py
@@ -15,9 +15,9 @@
 BF16 = jnp.bfloat16
 VMEM_LIMIT = 16 * 1024 * 1024
 SENDERS = 4
-SCAN_STEPS = 8
-WEIGHTS, CELLS, TABLES = 0, 2, 4
-DECAY, GAIN, SCALE, INLET = 8, 9, 10, 11
+SCAN_STEPS = 4
+CELLS, WEIGHTS, TABLES = 0, 4, 1
+DECAY, GAIN, SCALE, INLET = 12, 13, 14, 15
 
 
 def rows_of(shape):
@@ -105,6 +105,15 @@
     return jnp.concatenate([ref[i, t] for t in range(BRICKS)], axis=1)
 
 
+def pair_slots(slots, t, kind, pair):
+    even = kind + 2 * pair
+    return jnp.where(rows_of((8, 128)) < 4, slots[0, t, even : even + 1], slots[0, t, even + 1 : even + 2])
+
+
+def pair_weights(slots, pair):
+    return jnp.concatenate([pair_slots(slots, t, WEIGHTS, pair) for t in range(BRICKS)], axis=1)
+
+
 def read_table(slots, i):
     tiles = [slots[TABLES + i // 4, 4 * (i % 4) + j] for j in range(4)]
     return jnp.concatenate([jnp.concatenate(tiles[:2], axis=1), jnp.concatenate(tiles[2:], axis=1)], axis=0)
@@ -156,21 +165,16 @@
         copy.start()
     for copy in copies:
         copy.wait()
-    row = rows_of((8, 128))
     lane = lanes_of((1, 128))
 
     def brick(t, carry):
-        for pair in range(2):
-            weights, cells = [], []
-            for block in (2 * pair, 2 * pair + 1):
-                weight = weight_ref[block, pl.ds(t, 1), :]
-                weight = jnp.where(lane < count_ref[block, t], weight, 0.0)
-                segment = segment_ref[block, pl.ds(t, 1), :]
-                weights.append(jnp.where(segment >= 128, -weight, weight))
-                cells.append(voxel_ref[block, pl.ds(t, 1), :].astype(F32))
-                hots[block, t] = onehot(segment & 127, 128)
-            slots[WEIGHTS + pair, t] = jnp.where(row < 4, weights[0], weights[1])
-            slots[CELLS + pair, t] = jnp.where(row < 4, cells[0], cells[1])
+        for block in range(4):
+            weight = weight_ref[block, pl.ds(t, 1), :]
+            weight = jnp.where(lane < count_ref[block, t], weight, 0.0)
+            segment = segment_ref[block, pl.ds(t, 1), :]
+            hots[block, t] = onehot(segment & 127, 128)
+            slots[0, t, CELLS + block : CELLS + block + 1] = voxel_ref[block, pl.ds(t, 1), :].astype(F32)
+            slots[0, t, WEIGHTS + block : WEIGHTS + block + 1] = jnp.where(segment >= 128, -weight, weight)
         return carry
 
     lax.fori_loop(0, BRICKS, brick, 0, unroll=4)
@@ -181,7 +185,7 @@
     write_table(slots, INLET, jnp.broadcast_to(inlet, (16, SEG)))
     weight_sums, speeds = [], []
     for pair in range(2):
-        weights = wide(slots, WEIGHTS + pair)
+        weights = pair_weights(slots, pair)
         weight_sums.append(sum_segments(jnp.abs(weights), pair, weights, hots))
         speeds.append(jnp.where(row < 4, flow_ref[2 * pair : 2 * pair + 1], flow_ref[2 * pair + 1 : 2 * pair + 2]))
     speed = jnp.concatenate(speeds, axis=0)
@@ -191,20 +195,25 @@
     write_table(slots, GAIN, scale * inverse)
     lane = lanes_of(decay.shape)
     for i in range(SCAN_STEPS):
-        inside = lane >= 2**i
-        write_table(slots, i, jnp.where(inside, decay, 0.0))
-        decay = decay * jnp.where(inside, pltpu.roll(decay, 2**i, 1), 1.0)
+        step = 4**i
+        once = jnp.where(lane >= step, decay, 0.0)
+        twice = once * pltpu.roll(once, step, 1)
+        thrice = once * pltpu.roll(twice, step, 1)
+        for j, value in enumerate((once, twice, thrice)):
+            write_table(slots, 3 * i + j, value)
+        decay = thrice * pltpu.roll(once, 3 * step, 1)
 
 
 def solve_blocks(inflow, values, slots, hots, send_ref, narrow):
     gathered = []
     for pair in range(2):
-        weights = wide(slots, WEIGHTS + pair)
+        weights = pair_weights(slots, pair)
         gathered.append(sum_segments(wide(values, pair) * jnp.abs(weights), pair, weights, hots))
     vessel = read_table(slots, GAIN) * jnp.concatenate(gathered, axis=0)
     vessel = vessel + jnp.where(lanes_of((16, SEG)) == 0, read_table(slots, DECAY) * inflow, 0.0)
     for i in range(SCAN_STEPS):
-        vessel = vessel + read_table(slots, i) * pltpu.roll(vessel, 2**i, 1)
+        earlier = [read_table(slots, 3 * i + j) * pltpu.roll(vessel, (j + 1) * 4**i, 1) for j in range(3)]
+        vessel = (vessel + earlier[0]) + (earlier[1] + earlier[2])
 
     send_ref[0, 32:48] = jnp.zeros((16, 128), F32)
     send_ref[BRICKS - 1, 16:32] = jnp.zeros((16, 128), F32)
@@ -217,12 +226,12 @@
         ).astype(BF16)
         found = [matmul(lhs, wide(hots, block)) for block in (2 * pair, 2 * pair + 1)]
         for t in range(BRICKS):
-            weights = slots[WEIGHTS + pair, t]
+            weights = pair_slots(slots, t, WEIGHTS, pair)
             part = [value[:, t * 128 : (t + 1) * 128] for value in found]
             part = [jnp.where(tile_row < 4, part[0][8 * i : 8 * i + 8], part[1][8 * i : 8 * i + 8]) for i in range(4)]
             at_slot = jnp.where(weights < 0.0, part[2] + part[3], part[0] + part[1])
             flux = scale * jnp.abs(weights) * (at_slot - values[pair, t])
-            cell = slots[CELLS + pair, t]
+            cell = pair_slots(slots, t, CELLS, pair)
             cell_row = (tile_row & 3) == 3
             here = slice(8 * pair, 8 * pair + 8)
             own = jnp.where(cell_row, cell, flux)
@@ -241,7 +250,7 @@
 
 def first_solve_kernel(region_ref, slots, hots, send_ref, ends_ref, around_ref, values):
     def brick(t, carry):
-        cells = [slots[CELLS + block // 2, t, 4 * (block % 2) : 4 * (block % 2) + 1].astype(jnp.int32) for block in range(4)]
+        cells = [slots[0, t, CELLS + block : CELLS + block + 1].astype(jnp.int32) for block in range(4)]
         found = gather_slots(split_brick(region_ref[t]), cells)
         for pair in range(2):
             values[pair, t] = pair_tile([*found[2 * pair], 0.0, *found[2 * pair + 1], 0.0])
@@ -408,7 +417,7 @@
 
 
 def first_sweeps_kernel(
-    near, far, tissue_ref, around_ref, rate_ref, rate_near_ref, rate_far_ref, sources_ref, recv_ref, ends_ref,
+    far, near, tissue_ref, around_ref, rate_ref, rate_near_ref, rate_far_ref, sources_ref, recv_ref, ends_ref,
     out_ref, side_ref, inverse_ref, produced_ref, send_ref, now, later, source, inverse, produced,
 ):
     tissues = [tissue_ref[...], around_ref[0], around_ref[1]]
@@ -457,7 +466,7 @@
 
 
 def second_sweeps_kernel(
-    near, far, tissue_ref, side_ref, sources_ref, inverse, produced, out_ref, now, later, source
+    far, near, tissue_ref, side_ref, sources_ref, inverse, produced, out_ref, now, later, source
 ):
     fill(now, source, [tissue_ref[...], side_ref[...]], [sources_ref[i] for i in range(2)])
     zero = jnp.zeros((8, 128), F32)
@@ -533,7 +542,7 @@
         prepare_kernel,
         "prepare",
         [
-            (7, BRICKS, 8, 128),
+            (5, BRICKS, 8, 128),
             jax.ShapeDtypeStruct((4, BRICKS, 128, 128), BF16),
         ],
         [
@@ -574,12 +583,12 @@
         [received, tissue, around, rate, rate_near, rate_far],
         [pltpu.VMEM((192, 128), F32)] * 3,
     )
-    near, far = swap(near, "vessel", 0), swap(far, "vessel", 1)
+    far, near = swap(far, "vessel", 1), swap(near, "vessel", 0)
     tissue, side, inverse, produced, send = call(
         first_sweeps_kernel,
         "first_sweeps",
         [(96, 128), (96, 128), ring, ring[1:], (BRICKS, 16, 128)],
-        [near, far, tissue, around, rate, rate_near, rate_far, sources, received, ends],
+        [far, near, tissue, around, rate, rate_near, rate_far, sources, received, ends],
         [pltpu.VMEM(large_ring, F32)] * 4 + [pltpu.VMEM(large_ring[1:], F32)],
     )
     values = exchange(send, "tissue")
@@ -599,12 +608,12 @@
         [received, tissue, side],
         [pltpu.VMEM((rows, 128), F32) for rows in (192, 96, 96)],
     )
-    near, far = swap(near, "vessel", 0), swap(far, "vessel", 1)
+    far, near = swap(far, "vessel", 1), swap(near, "vessel", 0)
     (tissue,) = call(
         second_sweeps_kernel,
         "second_sweeps",
         [(3, 4, 8, 128)],
-        [near, far, tissue, side, sources, inverse, produced],
+        [far, near, tissue, side, sources, inverse, produced],
         [pltpu.VMEM(ring, F32)] * 3,
     )
     return tissue, vessel

time: 96.2 us -> 94.6 us (0.983)
  waiting for transfers between devices: 10.3 us -> 8.62 us
    ppermute x6, waiting for transfers between devices: 8.03 us -> 6.36 us  [swap(): lax.ppermute(value, axis, [pair for i in starts for pair in ((i, i + 1),...]
where the time goes in v6:
time: 94.6 us; the launch traced here: 94.1 us
  blocking collectives  43.9 us (46%)
  starting transfers between devices  23.3 us (25%)
  Pallas kernels  17.5 us (18%)
  waiting for transfers between devices  8.62 us (9%)
    all_to_all x4, blocking collectives, exchange(): return lax.all_to_all(value, axis, 0, 0, tiled=True)  43.9 us
    pallas_call x8, Pallas kernels, call(): pl.pallas_call(kernel, out_shape=[jax.ShapeDtypeStruct(out, F32) if isins...  17.5 us
    ppermute x6, starting transfers between devices, swap(): lax.ppermute(value, axis, [pair for i in starts for pair in ((i, i + 1),...  15.7 us
    all_to_all x1, starting transfers between devices, exchange(): return lax.all_to_all(value, axis, 0, 0, tiled=True)  7.6 us
    ppermute x6, waiting for transfers between devices, swap(): lax.ppermute(value, axis, [pair for i in starts for pair in ((i, i + 1),...  6.36 us
    all_to_all x1, waiting for transfers between devices, exchange(): return lax.all_to_all(value, axis, 0, 0, tiled=True)  2.26 us
  transfers between devices with their start and end apart: 7, of which 3 were waited for; matrix products, arithmetic and copies ran while one was open for 0% of the time, Pallas kernels for 3%

profile of v6, /device:TPU:1, one launch (start us, length us, event | category | flops | bytes accessed | tf_op | source)
XLA Modules:
  0.0 94.1 jit_solution(4877090610444670759)
XLA Ops:
  0.6 1.9 %spread.1 = (f32[16,96,128]{2,1,0:T(8,128)}, f32[96,128]{1,0:T(8,128)S(1)}, f32[96,128]{1,0:T(8,128)S(1)}) custom-call(f32[96,128]{1,0:T(8,128)} %bitcast.2, f32[96,128]{1,0:T(8,128)} %bitcast.3), custom_call_target="tpu_custom_call" | custom-call | tf_op jit(solution)/shard_map/spread/pallas_call | solution.py:496
  2.5 7.6 %all-to-all-start = ((f32[16,96,128]{2,1,0:T(8,128)}), f32[16,96,128]{2,1,0:T(8,128)S(1)}, u32[]{:S(2)}, u32[]{:S(2)}) async-start(f32[16,96,128]{2,1,0:T(8,128)} %get-tuple-element.26), calls=%async_computation | async-start | bytes 1572864 | tf_op jit(solution)/shard_map/all_to_all | solution.py:520
  10.1 0.7 collective-permute-start.1
  10.8 3.9 %collective-permute-start = (f32[96,128]{1,0:T(8,128)S(1)}, f32[96,128]{1,0:T(8,128)S(1)}, u32[]{:S(2)}, u32[]{:S(2)}) collective-permute-start(f32[96,128]{1,0:T(8,128)S(1)} %get-tuple-element.27.rate_ref), channel_id=1, source_target_pairs={{0,1},{1,0},{2,3},{3,2},{4,5},{5,4},{6,7},{7,6},{8,9},{9,8},{10,11... | collective-permute-start | bytes 147464 | tf_op jit(solution)/shard_map/ppermute | solution.py:524
  14.6 2.7 %prepare.1 = (f32[5,16,8,128]{3,2,1,0:T(8,128)S(1)}, bf16[4,16,128,128]{3,2,1,0:T(8,128)(2,1)S(1)}) custom-call(s32[4,16,128]{2,1,0:T(8,128)} %refs_0_.1, f32[4,16,128]{2,1,0:T(8,128)} %refs_1_.1, s32[4,16,128]{2,1,0:T(8,128)} %refs_2_.1, f32[4,256]{1,0:T(4,128)} %refs_3_.1, s32[4,16]{1,0:T(4,128)} %refs_4_.1, f32[3]{0:T(128)} %refs_5_.1, f32[3,4]{1,0:T(4,128)} %refs_6_.1), custom_call_target="tpu_custom_call" | custom-call | tf_op jit(solution)/shard_map/prepare/pallas_call | solution.py:496
  17.4 0.0 collective-permute-done.1.rate_far_ref
  17.4 3.6 %collective-permute-done.rate_near_ref = f32[96,128]{1,0:T(8,128)S(1)} collective-permute-done((f32[96,128]{1,0:T(8,128)S(1)}, f32[96,128]{1,0:T(8,128)S(1)}, u32[]{:S(2)}, u32[]{:S(2)}) %collective-permute-start) | collective-permute-done | bytes 49184 | tf_op jit(solution)/shard_map/ppermute | solution.py:524
  21.0 2.3 %all-to-all-done.region_ref = f32[16,96,128]{2,1,0:T(8,128)S(1)} async-done(((f32[16,96,128]{2,1,0:T(8,128)}), f32[16,96,128]{2,1,0:T(8,128)S(1)}, u32[]{:S(2)}, u32[]{:S(2)}) %all-to-all-start) | async-done | bytes 786464 | tf_op jit(solution)/shard_map/all_to_all | solution.py:520
  23.3 2.7 %first_solve.1 = (f32[16,48,128]{2,1,0:T(8,128)S(1)}, f32[8,8,128]{2,1,0:T(8,128)S(1)}, f32[2,96,128]{2,1,0:T(8,128)S(1)}) custom-call(f32[16,96,128]{2,1,0:T(8,128)S(1)} %all-to-all-done.region_ref, f32[5,16,8,128]{3,2,1,0:T(8,128)S(1)} %get-tuple-element.29.slots, bf16[4,16,128,128]{3,2,1,0:T(8,128)(2,1)S(1)} %get-tuple-element.30.hots), custom_call_target="tpu_custom_call" | custom-call | tf_op jit(solution)/shard_map/first_solve/pallas_call | solution.py:496
  26.0 0.0 copy-start
  26.0 13.1 %all_to_all.25.recv_ref = f32[16,48,128]{2,1,0:T(8,128)S(1)} all-to-all(f32[16,48,128]{2,1,0:T(8,128)S(1)} %get-tuple-element.31), channel_id=1, replica_groups=mesh['vessel'=8,'tissue'=16] {'tissue'}, dimensions={0} | all-to-all | bytes 786432 | tf_op jit(solution)/shard_map/all_to_all | solution.py:520
  39.1 2.6 %first_scatter.1 = (f32[3,10,24,128]{3,2,1,0:T(8,128)S(1)}, f32[3,10,24,128]{3,2,1,0:T(8,128)S(1)}, f32[3,96,128]{2,1,0:T(8,128)S(1)}) custom-call(f32[16,48,128]{2,1,0:T(8,128)S(1)} %all_to_all.25.recv_ref, f32[96,128]{1,0:T(8,128)S(1)} %get-tuple-element.32.tissue_ref, f32[2,96,128]{2,1,0:T(8,128)S(1)} %get-tuple-element.33.around_ref, ...), custom_call_target="tpu_custom_call" | custom-call | tf_op jit(solution)/shard_map/first_scatter/pallas_call | solution.py:496
  41.7 5.8 %collective-permute-start.2 = (f32[3,10,24,128]{3,2,1,0:T(8,128)S(1)}, f32[3,10,24,128]{3,2,1,0:T(8,128)S(1)}, u32[]{:S(2)}, u32[]{:S(2)}) collective-permute-start(f32[3,10,24,128]{3,2,1,0:T(8,128)S(1)} %get-tuple-element.36), channel_id=1, source_target_pairs={{16,32},{32,16},{48,64},{64,48},{80,96},{96,80},{17,33},{33,17},{4... | collective-permute-start | bytes 1105928 | tf_op jit(solution)/shard_map/ppermute | solution.py:524
  47.5 0.1 collective-permute-start.3
  47.6 9.9 %all_to_all.26.ends_ref = f32[8,8,128]{2,1,0:T(8,128)S(1)} all-to-all(f32[8,8,128]{2,1,0:T(8,128)S(1)} %get-tuple-element.39), channel_id=1, replica_groups=mesh['vessel'=8,'tissue'=16] {'vessel'}, dimensions={0} | all-to-all | bytes 65536 | tf_op jit(solution)/shard_map/all_to_all | solution.py:520
  57.4 0.0 collective-permute-done.2.far
  57.4 0.0 collective-permute-done.3.near
  57.4 2.0 %first_sweeps.1 = (f32[96,128]{1,0:T(8,128)S(1)}, f32[96,128]{1,0:T(8,128)S(1)}, f32[3,12,16,128]{3,2,1,0:T(8,128)S(1)}, f32[12,16,128]{2,1,0:T(8,128)S(1)}, f32[16,16,128]{2,1,0:T(8,128)S(1)}) custom-call(f32[3,10,24,128]{3,2,1,0:T(8,128)S(1)} %collective-permute-done.2.far, f32[3,10,24,128]{3,2,1,0:T(8,128)S(1)} %collective-permute-done.3.near, ...), custom_call_target="tpu_custom_call" | custom-call | tf_op jit(solution)/shard_map/first_sweeps/pallas_call | solution.py:496
  59.4 9.5 %all_to_all.27.values_ref = f32[16,16,128]{2,1,0:T(8,128)S(1)} all-to-all(f32[16,16,128]{2,1,0:T(8,128)S(1)} %get-tuple-element.40), channel_id=1, replica_groups=mesh['vessel'=8,'tissue'=16] {'tissue'}, dimensions={0} | all-to-all | bytes 262144 | tf_op jit(solution)/shard_map/all_to_all | solution.py:520
  69.0 0.0 copy-done
  69.0 2.4 %second_solve.1 = (f32[16,48,128]{2,1,0:T(8,128)S(1)}, f32[3,4,256]{2,1,0:T(4,128)}) custom-call(s32[4]{0:T(128)S(1)} %copy-done, f32[16,16,128]{2,1,0:T(8,128)S(1)} %all_to_all.27.values_ref, f32[5,16,8,128]{3,2,1,0:T(8,128)S(1)} %get-tuple-element.29.slots, bf16[4,16,128,128]{3,2,1,0:T(8,128)(2,1)S(1)} %get-tuple-element.30.hots), custom_call_target="tpu_custom_call" | custom-call | tf_op jit(solution)/shard_map/second_solve/pallas_call | solution.py:496
  71.3 11.5 %all_to_all.28.recv_ref = f32[16,48,128]{2,1,0:T(8,128)S(1)} all-to-all(f32[16,48,128]{2,1,0:T(8,128)S(1)} %get-tuple-element.41), channel_id=1, replica_groups=mesh['vessel'=8,'tissue'=16] {'tissue'}, dimensions={0} | all-to-all | bytes 786432 | tf_op jit(solution)/shard_map/all_to_all | solution.py:520
  82.8 2.2 %second_scatter.1 = (f32[3,12,8,128]{3,2,1,0:T(8,128)S(1)}, f32[3,12,8,128]{3,2,1,0:T(8,128)S(1)}, f32[2,96,128]{2,1,0:T(8,128)S(1)}) custom-call(f32[16,48,128]{2,1,0:T(8,128)S(1)} %all_to_all.28.recv_ref, f32[96,128]{1,0:T(8,128)S(1)} %get-tuple-element.42.tissue_ref, f32[96,128]{1,0:T(8,128)S(1)} %get-tuple-element.43.side_ref), custom_call_target="tpu_custom_call" | custom-call | tf_op jit(solution)/shard_map/second_scatter/pallas_call | solution.py:496
  85.0 5.2 %collective-permute-start.4 = (f32[3,12,8,128]{3,2,1,0:T(8,128)S(1)}, f32[3,12,8,128]{3,2,1,0:T(8,128)S(1)}, u32[]{:S(2)}, u32[]{:S(2)}) collective-permute-start(f32[3,12,8,128]{3,2,1,0:T(8,128)S(1)} %get-tuple-element.44), channel_id=1, source_target_pairs={{16,32},{32,16},{48,64},{64,48},{80,96},{96,80},{17,33},{33,17},{4... | collective-permute-start | bytes 442376 | tf_op jit(solution)/shard_map/ppermute | solution.py:524
  90.2 0.1 collective-permute-start.5
  90.3 2.7 %collective-permute-done.4.far = f32[3,12,8,128]{3,2,1,0:T(8,128)S(1)} collective-permute-done((f32[3,12,8,128]{3,2,1,0:T(8,128)S(1)}, f32[3,12,8,128]{3,2,1,0:T(8,128)S(1)}, u32[]{:S(2)}, u32[]{:S(2)}) %collective-permute-start.4) | collective-permute-done | bytes 147488 | tf_op jit(solution)/shard_map/ppermute | solution.py:524
  93.0 0.0 collective-permute-done.5.near
  93.0 1.1 %second_sweeps.1 = f32[3,4,8,128]{3,2,1,0:T(8,128)} custom-call(f32[3,12,8,128]{3,2,1,0:T(8,128)S(1)} %collective-permute-done.4.far, f32[3,12,8,128]{3,2,1,0:T(8,128)S(1)} %collective-permute-done.5.near, f32[96,128]{1,0:T(8,128)S(1)} %get-tuple-element.42.tissue_ref, f32[96,128]{1,0:T(8,128)S(1)} %get-tuple-element.43.side_ref, ...), custom_call_target="tpu_custom_call" | custom-call | tf_op jit(solution)/shard_map/second_sweeps/pallas_call | solution.py:496
Async XLA Ops:
  2.5 20.8 %all-to-all-start = ((f32[16,96,128]{2,1,0:T(8,128)}), f32[16,96,128]{2,1,0:T(8,128)S(1)}, u32[]{:S(2)}, u32[]{:S(2)}) async-start(f32[16,96,128]{2,1,0:T(8,128)} %get-tuple-element.26), calls=%async_computation | async-start | bytes 1572864 | tf_op jit(solution)/shard_map/all_to_all | solution.py:520
  10.1 7.3 %collective-permute-start.1 = (f32[96,128]{1,0:T(8,128)S(1)}, f32[96,128]{1,0:T(8,128)S(1)}, u32[]{:S(2)}, u32[]{:S(2)}) collective-permute-start(f32[96,128]{1,0:T(8,128)S(1)} %get-tuple-element.27.rate_ref), channel_id=1, source_target_pairs={{1,2},{2,1},{3,4},{4,3},{5,6},{6,5},{7,8},{8,7},{9,10},{10,9},{11,... | collective-permute-start | bytes 147464 | tf_op jit(solution)/shard_map/ppermute | solution.py:524
  10.8 10.2 %collective-permute-start = (f32[96,128]{1,0:T(8,128)S(1)}, f32[96,128]{1,0:T(8,128)S(1)}, u32[]{:S(2)}, u32[]{:S(2)}) collective-permute-start(f32[96,128]{1,0:T(8,128)S(1)} %get-tuple-element.27.rate_ref), channel_id=1, source_target_pairs={{0,1},{1,0},{2,3},{3,2},{4,5},{5,4},{6,7},{7,6},{8,9},{9,8},{10,11... | collective-permute-start | bytes 147464 | tf_op jit(solution)/shard_map/ppermute | solution.py:524
  26.0 43.0 %copy-start = (s32[4]{0:T(128)S(1)}, s32[4]{0:T(128)}, u32[]{:S(2)}) copy-start(s32[4]{0:T(128)} %upstream_ref.1) | copy-start | bytes 52
  41.7 15.8 %collective-permute-start.2 = (f32[3,10,24,128]{3,2,1,0:T(8,128)S(1)}, f32[3,10,24,128]{3,2,1,0:T(8,128)S(1)}, u32[]{:S(2)}, u32[]{:S(2)}) collective-permute-start(f32[3,10,24,128]{3,2,1,0:T(8,128)S(1)} %get-tuple-element.36), channel_id=1, source_target_pairs={{16,32},{32,16},{48,64},{64,48},{80,96},{96,80},{17,33},{33,17},{4... | collective-permute-start | bytes 1105928 | tf_op jit(solution)/shard_map/ppermute | solution.py:524
  47.5 10.0 %collective-permute-start.3 = (f32[3,10,24,128]{3,2,1,0:T(8,128)S(1)}, f32[3,10,24,128]{3,2,1,0:T(8,128)S(1)}, u32[]{:S(2)}, u32[]{:S(2)}) collective-permute-start(f32[3,10,24,128]{3,2,1,0:T(8,128)S(1)} %get-tuple-element.37), channel_id=1, source_target_pairs={{0,16},{16,0},{32,48},{48,32},{64,80},{80,64},{96,112},{112,96},{1... | collective-permute-start | bytes 1105928 | tf_op jit(solution)/shard_map/ppermute | solution.py:524
  85.0 8.0 %collective-permute-start.4 = (f32[3,12,8,128]{3,2,1,0:T(8,128)S(1)}, f32[3,12,8,128]{3,2,1,0:T(8,128)S(1)}, u32[]{:S(2)}, u32[]{:S(2)}) collective-permute-start(f32[3,12,8,128]{3,2,1,0:T(8,128)S(1)} %get-tuple-element.44), channel_id=1, source_target_pairs={{16,32},{32,16},{48,64},{64,48},{80,96},{96,80},{17,33},{33,17},{4... | collective-permute-start | bytes 442376 | tf_op jit(solution)/shard_map/ppermute | solution.py:524
  90.2 2.8 %collective-permute-start.5 = (f32[3,12,8,128]{3,2,1,0:T(8,128)S(1)}, f32[3,12,8,128]{3,2,1,0:T(8,128)S(1)}, u32[]{:S(2)}, u32[]{:S(2)}) collective-permute-start(f32[3,12,8,128]{3,2,1,0:T(8,128)S(1)} %get-tuple-element.45), channel_id=1, source_target_pairs={{0,16},{16,0},{32,48},{48,32},{64,80},{80,64},{96,112},{112,96},{1... | collective-permute-start | bytes 442376 | tf_op jit(solution)/shard_map/ppermute | solution.py:524

commit v7 on v6

--- a/solution.py
+++ b/solution.py
@@ -256,7 +256,7 @@
             values[pair, t] = pair_tile([*found[2 * pair], 0.0, *found[2 * pair + 1], 0.0])
         return carry
 
-    lax.fori_loop(0, BRICKS, brick, 0, unroll=4)
+    lax.fori_loop(0, BRICKS, brick, 0, unroll=BRICKS)
     vessel = solve_blocks(read_table(slots, INLET), values, slots, hots, send_ref, False)
     spot = lanes_of((16, 128)) == rows_of((16, 128))
     ends = jnp.sum(jnp.where(spot, vessel[:, SEG - 1 : SEG], 0.0), axis=0, keepdims=True)
@@ -462,7 +462,7 @@
             )
         return carry
 
-    lax.fori_loop(0, BRICKS, receiver, 0, unroll=4)
+    lax.fori_loop(0, BRICKS, receiver, 0, unroll=BRICKS)
 
 
 def second_sweeps_kernel(

time: 94.6 us -> 93.6 us (0.989)
  no operation moved by 1% of the time
where the time goes in v7:
time: 93.6 us; the launch traced here: 93.1 us
  blocking collectives  43.9 us (47%)
  starting transfers between devices  23.3 us (25%)
  Pallas kernels  16.6 us (18%)
  waiting for transfers between devices  8.62 us (9%)
    all_to_all x4, blocking collectives, exchange(): return lax.all_to_all(value, axis, 0, 0, tiled=True)  43.9 us
    pallas_call x8, Pallas kernels, call(): pl.pallas_call(kernel, out_shape=[jax.ShapeDtypeStruct(out, F32) if isins...  16.6 us
    ppermute x6, starting transfers between devices, swap(): lax.ppermute(value, axis, [pair for i in starts for pair in ((i, i + 1),...  15.7 us
    all_to_all x1, starting transfers between devices, exchange(): return lax.all_to_all(value, axis, 0, 0, tiled=True)  7.6 us
    ppermute x6, waiting for transfers between devices, swap(): lax.ppermute(value, axis, [pair for i in starts for pair in ((i, i + 1),...  6.36 us
    all_to_all x1, waiting for transfers between devices, exchange(): return lax.all_to_all(value, axis, 0, 0, tiled=True)  2.26 us
  transfers between devices with their start and end apart: 7, of which 3 were waited for; matrix products, arithmetic and copies ran while one was open for 0% of the time, Pallas kernels for 3%

profile of v7, /device:TPU:1, one launch (start us, length us, event | category | flops | bytes accessed | tf_op | source)
XLA Modules:
  0.0 93.1 jit_solution(3864433290180638035)
XLA Ops:
  0.6 1.9 %spread.1 = (f32[16,96,128]{2,1,0:T(8,128)}, f32[96,128]{1,0:T(8,128)S(1)}, f32[96,128]{1,0:T(8,128)S(1)}) custom-call(f32[96,128]{1,0:T(8,128)} %bitcast.2, f32[96,128]{1,0:T(8,128)} %bitcast.3), custom_call_target="tpu_custom_call" | custom-call | tf_op jit(solution)/shard_map/spread/pallas_call | solution.py:496
  2.5 7.6 %all-to-all-start = ((f32[16,96,128]{2,1,0:T(8,128)}), f32[16,96,128]{2,1,0:T(8,128)S(1)}, u32[]{:S(2)}, u32[]{:S(2)}) async-start(f32[16,96,128]{2,1,0:T(8,128)} %get-tuple-element.26), calls=%async_computation | async-start | bytes 1572864 | tf_op jit(solution)/shard_map/all_to_all | solution.py:520
  10.1 0.7 collective-permute-start.1
  10.8 3.9 %collective-permute-start = (f32[96,128]{1,0:T(8,128)S(1)}, f32[96,128]{1,0:T(8,128)S(1)}, u32[]{:S(2)}, u32[]{:S(2)}) collective-permute-start(f32[96,128]{1,0:T(8,128)S(1)} %get-tuple-element.27.rate_ref), channel_id=1, source_target_pairs={{0,1},{1,0},{2,3},{3,2},{4,5},{5,4},{6,7},{7,6},{8,9},{9,8},{10,11... | collective-permute-start | bytes 147464 | tf_op jit(solution)/shard_map/ppermute | solution.py:524
  14.6 2.7 %prepare.1 = (f32[5,16,8,128]{3,2,1,0:T(8,128)S(1)}, bf16[4,16,128,128]{3,2,1,0:T(8,128)(2,1)S(1)}) custom-call(s32[4,16,128]{2,1,0:T(8,128)} %refs_0_.1, f32[4,16,128]{2,1,0:T(8,128)} %refs_1_.1, s32[4,16,128]{2,1,0:T(8,128)} %refs_2_.1, f32[4,256]{1,0:T(4,128)} %refs_3_.1, s32[4,16]{1,0:T(4,128)} %refs_4_.1, f32[3]{0:T(128)} %refs_5_.1, f32[3,4]{1,0:T(4,128)} %refs_6_.1), custom_call_target="tpu_custom_call" | custom-call | tf_op jit(solution)/shard_map/prepare/pallas_call | solution.py:496
  17.4 0.0 collective-permute-done.1.rate_far_ref
  17.4 3.6 %collective-permute-done.rate_near_ref = f32[96,128]{1,0:T(8,128)S(1)} collective-permute-done((f32[96,128]{1,0:T(8,128)S(1)}, f32[96,128]{1,0:T(8,128)S(1)}, u32[]{:S(2)}, u32[]{:S(2)}) %collective-permute-start) | collective-permute-done | bytes 49184 | tf_op jit(solution)/shard_map/ppermute | solution.py:524
  21.0 2.3 %all-to-all-done.region_ref = f32[16,96,128]{2,1,0:T(8,128)S(1)} async-done(((f32[16,96,128]{2,1,0:T(8,128)}), f32[16,96,128]{2,1,0:T(8,128)S(1)}, u32[]{:S(2)}, u32[]{:S(2)}) %all-to-all-start) | async-done | bytes 786464 | tf_op jit(solution)/shard_map/all_to_all | solution.py:520
  23.3 2.1 %first_solve.1 = (f32[16,48,128]{2,1,0:T(8,128)S(1)}, f32[8,8,128]{2,1,0:T(8,128)S(1)}, f32[2,96,128]{2,1,0:T(8,128)S(1)}) custom-call(f32[16,96,128]{2,1,0:T(8,128)S(1)} %all-to-all-done.region_ref, f32[5,16,8,128]{3,2,1,0:T(8,128)S(1)} %get-tuple-element.29.slots, bf16[4,16,128,128]{3,2,1,0:T(8,128)(2,1)S(1)} %get-tuple-element.30.hots), custom_call_target="tpu_custom_call" | custom-call | tf_op jit(solution)/shard_map/first_solve/pallas_call | solution.py:496
  25.4 0.0 copy-start
  25.4 13.1 %all_to_all.25.recv_ref = f32[16,48,128]{2,1,0:T(8,128)S(1)} all-to-all(f32[16,48,128]{2,1,0:T(8,128)S(1)} %get-tuple-element.31), channel_id=1, replica_groups=mesh['vessel'=8,'tissue'=16] {'tissue'}, dimensions={0} | all-to-all | bytes 786432 | tf_op jit(solution)/shard_map/all_to_all | solution.py:520
  38.5 2.6 %first_scatter.1 = (f32[3,10,24,128]{3,2,1,0:T(8,128)S(1)}, f32[3,10,24,128]{3,2,1,0:T(8,128)S(1)}, f32[3,96,128]{2,1,0:T(8,128)S(1)}) custom-call(f32[16,48,128]{2,1,0:T(8,128)S(1)} %all_to_all.25.recv_ref, f32[96,128]{1,0:T(8,128)S(1)} %get-tuple-element.32.tissue_ref, f32[2,96,128]{2,1,0:T(8,128)S(1)} %get-tuple-element.33.around_ref, ...), custom_call_target="tpu_custom_call" | custom-call | tf_op jit(solution)/shard_map/first_scatter/pallas_call | solution.py:496
  41.1 5.8 %collective-permute-start.2 = (f32[3,10,24,128]{3,2,1,0:T(8,128)S(1)}, f32[3,10,24,128]{3,2,1,0:T(8,128)S(1)}, u32[]{:S(2)}, u32[]{:S(2)}) collective-permute-start(f32[3,10,24,128]{3,2,1,0:T(8,128)S(1)} %get-tuple-element.36), channel_id=1, source_target_pairs={{16,32},{32,16},{48,64},{64,48},{80,96},{96,80},{17,33},{33,17},{4... | collective-permute-start | bytes 1105928 | tf_op jit(solution)/shard_map/ppermute | solution.py:524
  46.9 0.1 collective-permute-start.3
  47.0 9.8 %all_to_all.26.ends_ref = f32[8,8,128]{2,1,0:T(8,128)S(1)} all-to-all(f32[8,8,128]{2,1,0:T(8,128)S(1)} %get-tuple-element.39), channel_id=1, replica_groups=mesh['vessel'=8,'tissue'=16] {'vessel'}, dimensions={0} | all-to-all | bytes 65536 | tf_op jit(solution)/shard_map/all_to_all | solution.py:520
  56.9 0.0 collective-permute-done.2.far
  56.9 0.0 collective-permute-done.3.near
  56.9 1.5 %first_sweeps.1 = (f32[96,128]{1,0:T(8,128)S(1)}, f32[96,128]{1,0:T(8,128)S(1)}, f32[3,12,16,128]{3,2,1,0:T(8,128)S(1)}, f32[12,16,128]{2,1,0:T(8,128)S(1)}, f32[16,16,128]{2,1,0:T(8,128)S(1)}) custom-call(f32[3,10,24,128]{3,2,1,0:T(8,128)S(1)} %collective-permute-done.2.far, f32[3,10,24,128]{3,2,1,0:T(8,128)S(1)} %collective-permute-done.3.near, ...), custom_call_target="tpu_custom_call" | custom-call | tf_op jit(solution)/shard_map/first_sweeps/pallas_call | solution.py:496
  58.4 9.6 %all_to_all.27.values_ref = f32[16,16,128]{2,1,0:T(8,128)S(1)} all-to-all(f32[16,16,128]{2,1,0:T(8,128)S(1)} %get-tuple-element.40), channel_id=1, replica_groups=mesh['vessel'=8,'tissue'=16] {'tissue'}, dimensions={0} | all-to-all | bytes 262144 | tf_op jit(solution)/shard_map/all_to_all | solution.py:520
  68.0 0.0 copy-done
  68.0 2.4 %second_solve.1 = (f32[16,48,128]{2,1,0:T(8,128)S(1)}, f32[3,4,256]{2,1,0:T(4,128)}) custom-call(s32[4]{0:T(128)S(1)} %copy-done, f32[16,16,128]{2,1,0:T(8,128)S(1)} %all_to_all.27.values_ref, f32[5,16,8,128]{3,2,1,0:T(8,128)S(1)} %get-tuple-element.29.slots, bf16[4,16,128,128]{3,2,1,0:T(8,128)(2,1)S(1)} %get-tuple-element.30.hots), custom_call_target="tpu_custom_call" | custom-call | tf_op jit(solution)/shard_map/second_solve/pallas_call | solution.py:496
  70.4 11.4 %all_to_all.28.recv_ref = f32[16,48,128]{2,1,0:T(8,128)S(1)} all-to-all(f32[16,48,128]{2,1,0:T(8,128)S(1)} %get-tuple-element.41), channel_id=1, replica_groups=mesh['vessel'=8,'tissue'=16] {'tissue'}, dimensions={0} | all-to-all | bytes 786432 | tf_op jit(solution)/shard_map/all_to_all | solution.py:520
  81.8 2.2 %second_scatter.1 = (f32[3,12,8,128]{3,2,1,0:T(8,128)S(1)}, f32[3,12,8,128]{3,2,1,0:T(8,128)S(1)}, f32[2,96,128]{2,1,0:T(8,128)S(1)}) custom-call(f32[16,48,128]{2,1,0:T(8,128)S(1)} %all_to_all.28.recv_ref, f32[96,128]{1,0:T(8,128)S(1)} %get-tuple-element.42.tissue_ref, f32[96,128]{1,0:T(8,128)S(1)} %get-tuple-element.43.side_ref), custom_call_target="tpu_custom_call" | custom-call | tf_op jit(solution)/shard_map/second_scatter/pallas_call | solution.py:496
  84.1 5.2 %collective-permute-start.4 = (f32[3,12,8,128]{3,2,1,0:T(8,128)S(1)}, f32[3,12,8,128]{3,2,1,0:T(8,128)S(1)}, u32[]{:S(2)}, u32[]{:S(2)}) collective-permute-start(f32[3,12,8,128]{3,2,1,0:T(8,128)S(1)} %get-tuple-element.44), channel_id=1, source_target_pairs={{16,32},{32,16},{48,64},{64,48},{80,96},{96,80},{17,33},{33,17},{4... | collective-permute-start | bytes 442376 | tf_op jit(solution)/shard_map/ppermute | solution.py:524
  89.2 0.1 collective-permute-start.5
  89.3 2.7 %collective-permute-done.4.far = f32[3,12,8,128]{3,2,1,0:T(8,128)S(1)} collective-permute-done((f32[3,12,8,128]{3,2,1,0:T(8,128)S(1)}, f32[3,12,8,128]{3,2,1,0:T(8,128)S(1)}, u32[]{:S(2)}, u32[]{:S(2)}) %collective-permute-start.4) | collective-permute-done | bytes 147488 | tf_op jit(solution)/shard_map/ppermute | solution.py:524
  92.1 0.0 collective-permute-done.5.near
  92.1 1.1 %second_sweeps.1 = f32[3,4,8,128]{3,2,1,0:T(8,128)} custom-call(f32[3,12,8,128]{3,2,1,0:T(8,128)S(1)} %collective-permute-done.4.far, f32[3,12,8,128]{3,2,1,0:T(8,128)S(1)} %collective-permute-done.5.near, f32[96,128]{1,0:T(8,128)S(1)} %get-tuple-element.42.tissue_ref, f32[96,128]{1,0:T(8,128)S(1)} %get-tuple-element.43.side_ref, ...), custom_call_target="tpu_custom_call" | custom-call | tf_op jit(solution)/shard_map/second_sweeps/pallas_call | solution.py:496
Async XLA Ops:
  2.5 20.8 %all-to-all-start = ((f32[16,96,128]{2,1,0:T(8,128)}), f32[16,96,128]{2,1,0:T(8,128)S(1)}, u32[]{:S(2)}, u32[]{:S(2)}) async-start(f32[16,96,128]{2,1,0:T(8,128)} %get-tuple-element.26), calls=%async_computation | async-start | bytes 1572864 | tf_op jit(solution)/shard_map/all_to_all | solution.py:520
  10.1 7.3 %collective-permute-start.1 = (f32[96,128]{1,0:T(8,128)S(1)}, f32[96,128]{1,0:T(8,128)S(1)}, u32[]{:S(2)}, u32[]{:S(2)}) collective-permute-start(f32[96,128]{1,0:T(8,128)S(1)} %get-tuple-element.27.rate_ref), channel_id=1, source_target_pairs={{1,2},{2,1},{3,4},{4,3},{5,6},{6,5},{7,8},{8,7},{9,10},{10,9},{11,... | collective-permute-start | bytes 147464 | tf_op jit(solution)/shard_map/ppermute | solution.py:524
  10.8 10.2 %collective-permute-start = (f32[96,128]{1,0:T(8,128)S(1)}, f32[96,128]{1,0:T(8,128)S(1)}, u32[]{:S(2)}, u32[]{:S(2)}) collective-permute-start(f32[96,128]{1,0:T(8,128)S(1)} %get-tuple-element.27.rate_ref), channel_id=1, source_target_pairs={{0,1},{1,0},{2,3},{3,2},{4,5},{5,4},{6,7},{7,6},{8,9},{9,8},{10,11... | collective-permute-start | bytes 147464 | tf_op jit(solution)/shard_map/ppermute | solution.py:524
  25.4 42.6 %copy-start = (s32[4]{0:T(128)S(1)}, s32[4]{0:T(128)}, u32[]{:S(2)}) copy-start(s32[4]{0:T(128)} %upstream_ref.1) | copy-start | bytes 52
  41.1 15.7 %collective-permute-start.2 = (f32[3,10,24,128]{3,2,1,0:T(8,128)S(1)}, f32[3,10,24,128]{3,2,1,0:T(8,128)S(1)}, u32[]{:S(2)}, u32[]{:S(2)}) collective-permute-start(f32[3,10,24,128]{3,2,1,0:T(8,128)S(1)} %get-tuple-element.36), channel_id=1, source_target_pairs={{16,32},{32,16},{48,64},{64,48},{80,96},{96,80},{17,33},{33,17},{4... | collective-permute-start | bytes 1105928 | tf_op jit(solution)/shard_map/ppermute | solution.py:524
  46.9 9.9 %collective-permute-start.3 = (f32[3,10,24,128]{3,2,1,0:T(8,128)S(1)}, f32[3,10,24,128]{3,2,1,0:T(8,128)S(1)}, u32[]{:S(2)}, u32[]{:S(2)}) collective-permute-start(f32[3,10,24,128]{3,2,1,0:T(8,128)S(1)} %get-tuple-element.37), channel_id=1, source_target_pairs={{0,16},{16,0},{32,48},{48,32},{64,80},{80,64},{96,112},{112,96},{1... | collective-permute-start | bytes 1105928 | tf_op jit(solution)/shard_map/ppermute | solution.py:524
  84.1 8.0 %collective-permute-start.4 = (f32[3,12,8,128]{3,2,1,0:T(8,128)S(1)}, f32[3,12,8,128]{3,2,1,0:T(8,128)S(1)}, u32[]{:S(2)}, u32[]{:S(2)}) collective-permute-start(f32[3,12,8,128]{3,2,1,0:T(8,128)S(1)} %get-tuple-element.44), channel_id=1, source_target_pairs={{16,32},{32,16},{48,64},{64,48},{80,96},{96,80},{17,33},{33,17},{4... | collective-permute-start | bytes 442376 | tf_op jit(solution)/shard_map/ppermute | solution.py:524
  89.2 2.8 %collective-permute-start.5 = (f32[3,12,8,128]{3,2,1,0:T(8,128)S(1)}, f32[3,12,8,128]{3,2,1,0:T(8,128)S(1)}, u32[]{:S(2)}, u32[]{:S(2)}) collective-permute-start(f32[3,12,8,128]{3,2,1,0:T(8,128)S(1)} %get-tuple-element.45), channel_id=1, source_target_pairs={{0,16},{16,0},{32,48},{48,32},{64,80},{80,64},{96,112},{112,96},{1... | collective-permute-start | bytes 442376 | tf_op jit(solution)/shard_map/ppermute | solution.py:524

commit v8 on v7

--- a/solution.py
+++ b/solution.py
@@ -566,7 +566,6 @@
         ],
         [HBM] * 7,
     )
-    region, rate_near, rate_far = lax.optimization_barrier((region, rate_near, rate_far))
     send, ends, around = call(
         first_solve_kernel,
         "first_solve",
@@ -574,6 +573,7 @@
         [region, *prepared],
         values_scratch,
     )
+    send, rate_near, rate_far = lax.optimization_barrier((send, rate_near, rate_far))
     received = exchange(send, "tissue")
     ends = exchange(ends, "vessel")
     near, far, sources = call(

time: 93.6 us -> 93.4 us (level)
  blocking collectives: 43.9 us -> 42.7 us
  starting transfers between devices: 23.3 us -> 24.3 us
    all_to_all x1, waiting for transfers between devices: 2.26 us -> 5.91 us  [exchange(): return lax.all_to_all(value, axis, 0, 0, tiled=True)]
    ppermute x6, waiting for transfers between devices: 6.36 us -> 2.73 us  [swap(): lax.ppermute(value, axis, [pair for i in starts for pair in ((i, i + 1),...]
    all_to_all x4, blocking collectives: 43.9 us -> 42.7 us  [exchange(): return lax.all_to_all(value, axis, 0, 0, tiled=True)]
    ppermute x6, starting transfers between devices: 15.7 us -> 16.7 us  [swap(): lax.ppermute(value, axis, [pair for i in starts for pair in ((i, i + 1),...]
  transfers between devices with their start and end apart: 7 -> 7, of which waited for: 3 -> 2; matrix products, arithmetic and copies ran while one was open for 0% -> 0% of each run, Pallas kernels for 3% -> 5%
where the time goes in v8:
time: 93.4 us; the launch traced here: 92.9 us
  blocking collectives  42.7 us (46%)
  starting transfers between devices  24.3 us (26%)
  Pallas kernels  16.5 us (18%)
  waiting for transfers between devices  8.64 us (9%)
    all_to_all x4, blocking collectives, exchange(): return lax.all_to_all(value, axis, 0, 0, tiled=True)  42.7 us
    ppermute x6, starting transfers between devices, swap(): lax.ppermute(value, axis, [pair for i in starts for pair in ((i, i + 1),...  16.7 us
    pallas_call x8, Pallas kernels, call(): pl.pallas_call(kernel, out_shape=[jax.ShapeDtypeStruct(out, F32) if isins...  16.5 us
    all_to_all x1, starting transfers between devices, exchange(): return lax.all_to_all(value, axis, 0, 0, tiled=True)  7.6 us
    all_to_all x1, waiting for transfers between devices, exchange(): return lax.all_to_all(value, axis, 0, 0, tiled=True)  5.91 us
    ppermute x6, waiting for transfers between devices, swap(): lax.ppermute(value, axis, [pair for i in starts for pair in ((i, i + 1),...  2.73 us
  transfers between devices with their start and end apart: 7, of which 2 were waited for; matrix products, arithmetic and copies ran while one was open for 0% of the time, Pallas kernels for 5%

profile of v8, /device:TPU:1, one launch (start us, length us, event | category | flops | bytes accessed | tf_op | source)
XLA Modules:
  0.0 92.9 jit_solution(10985960266867112255)
XLA Ops:
  0.6 1.9 %spread.1 = (f32[16,96,128]{2,1,0:T(8,128)}, f32[96,128]{1,0:T(8,128)S(1)}, f32[96,128]{1,0:T(8,128)S(1)}) custom-call(f32[96,128]{1,0:T(8,128)} %bitcast.2, f32[96,128]{1,0:T(8,128)} %bitcast.3), custom_call_target="tpu_custom_call" | custom-call | tf_op jit(solution)/shard_map/spread/pallas_call | solution.py:496
  2.5 7.6 %all-to-all-start = ((f32[16,96,128]{2,1,0:T(8,128)}), f32[16,96,128]{2,1,0:T(8,128)S(1)}, u32[]{:S(2)}, u32[]{:S(2)}) async-start(f32[16,96,128]{2,1,0:T(8,128)} %get-tuple-element.26), calls=%async_computation | async-start | bytes 1572864 | tf_op jit(solution)/shard_map/all_to_all | solution.py:520
  10.1 0.7 collective-permute-start.1
  10.8 3.9 %collective-permute-start = (f32[96,128]{1,0:T(8,128)S(1)}, f32[96,128]{1,0:T(8,128)S(1)}, u32[]{:S(2)}, u32[]{:S(2)}) collective-permute-start(f32[96,128]{1,0:T(8,128)S(1)} %get-tuple-element.30.rate_ref), channel_id=1, source_target_pairs={{0,1},{1,0},{2,3},{3,2},{4,5},{5,4},{6,7},{7,6},{8,9},{9,8},{10,11... | collective-permute-start | bytes 147464 | tf_op jit(solution)/shard_map/ppermute | solution.py:524
  14.6 2.7 %prepare.1 = (f32[5,16,8,128]{3,2,1,0:T(8,128)S(1)}, bf16[4,16,128,128]{3,2,1,0:T(8,128)(2,1)S(1)}) custom-call(s32[4,16,128]{2,1,0:T(8,128)} %refs_0_.1, f32[4,16,128]{2,1,0:T(8,128)} %refs_1_.1, s32[4,16,128]{2,1,0:T(8,128)} %refs_2_.1, f32[4,256]{1,0:T(4,128)} %refs_3_.1, s32[4,16]{1,0:T(4,128)} %refs_4_.1, f32[3]{0:T(128)} %refs_5_.1, f32[3,4]{1,0:T(4,128)} %refs_6_.1), custom_call_target="tpu_custom_call" | custom-call | tf_op jit(solution)/shard_map/prepare/pallas_call | solution.py:496
  17.4 5.9 %all-to-all-done.region_ref = f32[16,96,128]{2,1,0:T(8,128)S(1)} async-done(((f32[16,96,128]{2,1,0:T(8,128)}), f32[16,96,128]{2,1,0:T(8,128)S(1)}, u32[]{:S(2)}, u32[]{:S(2)}) %all-to-all-start) | async-done | bytes 786464 | tf_op jit(solution)/shard_map/all_to_all | solution.py:520
  23.3 2.1 %first_solve.1 = (f32[16,48,128]{2,1,0:T(8,128)S(1)}, f32[8,8,128]{2,1,0:T(8,128)S(1)}, f32[2,96,128]{2,1,0:T(8,128)S(1)}) custom-call(f32[16,96,128]{2,1,0:T(8,128)S(1)} %all-to-all-done.region_ref, f32[5,16,8,128]{3,2,1,0:T(8,128)S(1)} %get-tuple-element.27.slots, bf16[4,16,128,128]{3,2,1,0:T(8,128)(2,1)S(1)} %get-tuple-element.28.hots), custom_call_target="tpu_custom_call" | custom-call | tf_op jit(solution)/shard_map/first_solve/pallas_call | solution.py:496
  25.4 0.0 copy-start
  25.4 0.0 collective-permute-done.1.rate_far_ref
  25.4 0.0 collective-permute-done.rate_near_ref
  25.5 11.8 %all_to_all.25.recv_ref = f32[16,48,128]{2,1,0:T(8,128)S(1)} all-to-all(f32[16,48,128]{2,1,0:T(8,128)S(1)} %get-tuple-element.31), channel_id=1, replica_groups=mesh['vessel'=8,'tissue'=16] {'tissue'}, dimensions={0} | all-to-all | bytes 786432 | tf_op jit(solution)/shard_map/all_to_all | solution.py:520
  37.3 2.6 %first_scatter.1 = (f32[3,10,24,128]{3,2,1,0:T(8,128)S(1)}, f32[3,10,24,128]{3,2,1,0:T(8,128)S(1)}, f32[3,96,128]{2,1,0:T(8,128)S(1)}) custom-call(f32[16,48,128]{2,1,0:T(8,128)S(1)} %all_to_all.25.recv_ref, f32[96,128]{1,0:T(8,128)S(1)} %get-tuple-element.32.tissue_ref, f32[2,96,128]{2,1,0:T(8,128)S(1)} %get-tuple-element.33.around_ref, ...), custom_call_target="tpu_custom_call" | custom-call | tf_op jit(solution)/shard_map/first_scatter/pallas_call | solution.py:496
  39.9 6.8 %collective-permute-start.2 = (f32[3,10,24,128]{3,2,1,0:T(8,128)S(1)}, f32[3,10,24,128]{3,2,1,0:T(8,128)S(1)}, u32[]{:S(2)}, u32[]{:S(2)}) collective-permute-start(f32[3,10,24,128]{3,2,1,0:T(8,128)S(1)} %get-tuple-element.36), channel_id=1, source_target_pairs={{16,32},{32,16},{48,64},{64,48},{80,96},{96,80},{17,33},{33,17},{4... | collective-permute-start | bytes 1105928 | tf_op jit(solution)/shard_map/ppermute | solution.py:524
  46.7 0.1 collective-permute-start.3
  46.8 9.9 %all_to_all.26.ends_ref = f32[8,8,128]{2,1,0:T(8,128)S(1)} all-to-all(f32[8,8,128]{2,1,0:T(8,128)S(1)} %get-tuple-element.39), channel_id=1, replica_groups=mesh['vessel'=8,'tissue'=16] {'vessel'}, dimensions={0} | all-to-all | bytes 65536 | tf_op jit(solution)/shard_map/all_to_all | solution.py:520
  56.7 0.0 collective-permute-done.2.far
  56.7 0.0 collective-permute-done.3.near
  56.7 1.5 %first_sweeps.1 = (f32[96,128]{1,0:T(8,128)S(1)}, f32[96,128]{1,0:T(8,128)S(1)}, f32[3,12,16,128]{3,2,1,0:T(8,128)S(1)}, f32[12,16,128]{2,1,0:T(8,128)S(1)}, f32[16,16,128]{2,1,0:T(8,128)S(1)}) custom-call(f32[3,10,24,128]{3,2,1,0:T(8,128)S(1)} %collective-permute-done.2.far, f32[3,10,24,128]{3,2,1,0:T(8,128)S(1)} %collective-permute-done.3.near, ...), custom_call_target="tpu_custom_call" | custom-call | tf_op jit(solution)/shard_map/first_sweeps/pallas_call | solution.py:496
  58.2 9.5 %all_to_all.27.values_ref = f32[16,16,128]{2,1,0:T(8,128)S(1)} all-to-all(f32[16,16,128]{2,1,0:T(8,128)S(1)} %get-tuple-element.40), channel_id=1, replica_groups=mesh['vessel'=8,'tissue'=16] {'tissue'}, dimensions={0} | all-to-all | bytes 262144 | tf_op jit(solution)/shard_map/all_to_all | solution.py:520
  67.8 0.0 copy-done
  67.8 2.4 %second_solve.1 = (f32[16,48,128]{2,1,0:T(8,128)S(1)}, f32[3,4,256]{2,1,0:T(4,128)}) custom-call(s32[4]{0:T(128)S(1)} %copy-done, f32[16,16,128]{2,1,0:T(8,128)S(1)} %all_to_all.27.values_ref, f32[5,16,8,128]{3,2,1,0:T(8,128)S(1)} %get-tuple-element.27.slots, bf16[4,16,128,128]{3,2,1,0:T(8,128)(2,1)S(1)} %get-tuple-element.28.hots), custom_call_target="tpu_custom_call" | custom-call | tf_op jit(solution)/shard_map/second_solve/pallas_call | solution.py:496
  70.2 11.4 %all_to_all.28.recv_ref = f32[16,48,128]{2,1,0:T(8,128)S(1)} all-to-all(f32[16,48,128]{2,1,0:T(8,128)S(1)} %get-tuple-element.41), channel_id=1, replica_groups=mesh['vessel'=8,'tissue'=16] {'tissue'}, dimensions={0} | all-to-all | bytes 786432 | tf_op jit(solution)/shard_map/all_to_all | solution.py:520
  81.6 2.2 %second_scatter.1 = (f32[3,12,8,128]{3,2,1,0:T(8,128)S(1)}, f32[3,12,8,128]{3,2,1,0:T(8,128)S(1)}, f32[2,96,128]{2,1,0:T(8,128)S(1)}) custom-call(f32[16,48,128]{2,1,0:T(8,128)S(1)} %all_to_all.28.recv_ref, f32[96,128]{1,0:T(8,128)S(1)} %get-tuple-element.42.tissue_ref, f32[96,128]{1,0:T(8,128)S(1)} %get-tuple-element.43.side_ref), custom_call_target="tpu_custom_call" | custom-call | tf_op jit(solution)/shard_map/second_scatter/pallas_call | solution.py:496
  83.9 5.2 %collective-permute-start.4 = (f32[3,12,8,128]{3,2,1,0:T(8,128)S(1)}, f32[3,12,8,128]{3,2,1,0:T(8,128)S(1)}, u32[]{:S(2)}, u32[]{:S(2)}) collective-permute-start(f32[3,12,8,128]{3,2,1,0:T(8,128)S(1)} %get-tuple-element.44), channel_id=1, source_target_pairs={{16,32},{32,16},{48,64},{64,48},{80,96},{96,80},{17,33},{33,17},{4... | collective-permute-start | bytes 442376 | tf_op jit(solution)/shard_map/ppermute | solution.py:524
  89.0 0.1 collective-permute-start.5
  89.1 2.7 %collective-permute-done.4.far = f32[3,12,8,128]{3,2,1,0:T(8,128)S(1)} collective-permute-done((f32[3,12,8,128]{3,2,1,0:T(8,128)S(1)}, f32[3,12,8,128]{3,2,1,0:T(8,128)S(1)}, u32[]{:S(2)}, u32[]{:S(2)}) %collective-permute-start.4) | collective-permute-done | bytes 147488 | tf_op jit(solution)/shard_map/ppermute | solution.py:524
  91.8 0.0 collective-permute-done.5.near
  91.8 1.1 %second_sweeps.1 = f32[3,4,8,128]{3,2,1,0:T(8,128)} custom-call(f32[3,12,8,128]{3,2,1,0:T(8,128)S(1)} %collective-permute-done.4.far, f32[3,12,8,128]{3,2,1,0:T(8,128)S(1)} %collective-permute-done.5.near, f32[96,128]{1,0:T(8,128)S(1)} %get-tuple-element.42.tissue_ref, f32[96,128]{1,0:T(8,128)S(1)} %get-tuple-element.43.side_ref, ...), custom_call_target="tpu_custom_call" | custom-call | tf_op jit(solution)/shard_map/second_sweeps/pallas_call | solution.py:496
Async XLA Ops:
  2.5 20.8 %all-to-all-start = ((f32[16,96,128]{2,1,0:T(8,128)}), f32[16,96,128]{2,1,0:T(8,128)S(1)}, u32[]{:S(2)}, u32[]{:S(2)}) async-start(f32[16,96,128]{2,1,0:T(8,128)} %get-tuple-element.26), calls=%async_computation | async-start | bytes 1572864 | tf_op jit(solution)/shard_map/all_to_all | solution.py:520
  10.1 15.3 %collective-permute-start.1 = (f32[96,128]{1,0:T(8,128)S(1)}, f32[96,128]{1,0:T(8,128)S(1)}, u32[]{:S(2)}, u32[]{:S(2)}) collective-permute-start(f32[96,128]{1,0:T(8,128)S(1)} %get-tuple-element.30.rate_ref), channel_id=1, source_target_pairs={{1,2},{2,1},{3,4},{4,3},{5,6},{6,5},{7,8},{8,7},{9,10},{10,9},{11,... | collective-permute-start | bytes 147464 | tf_op jit(solution)/shard_map/ppermute | solution.py:524
  10.8 14.7 %collective-permute-start = (f32[96,128]{1,0:T(8,128)S(1)}, f32[96,128]{1,0:T(8,128)S(1)}, u32[]{:S(2)}, u32[]{:S(2)}) collective-permute-start(f32[96,128]{1,0:T(8,128)S(1)} %get-tuple-element.30.rate_ref), channel_id=1, source_target_pairs={{0,1},{1,0},{2,3},{3,2},{4,5},{5,4},{6,7},{7,6},{8,9},{9,8},{10,11... | collective-permute-start | bytes 147464 | tf_op jit(solution)/shard_map/ppermute | solution.py:524
  25.4 42.4 %copy-start = (s32[4]{0:T(128)S(1)}, s32[4]{0:T(128)}, u32[]{:S(2)}) copy-start(s32[4]{0:T(128)} %upstream_ref.1) | copy-start | bytes 52
  39.9 16.8 %collective-permute-start.2 = (f32[3,10,24,128]{3,2,1,0:T(8,128)S(1)}, f32[3,10,24,128]{3,2,1,0:T(8,128)S(1)}, u32[]{:S(2)}, u32[]{:S(2)}) collective-permute-start(f32[3,10,24,128]{3,2,1,0:T(8,128)S(1)} %get-tuple-element.36), channel_id=1, source_target_pairs={{16,32},{32,16},{48,64},{64,48},{80,96},{96,80},{17,33},{33,17},{4... | collective-permute-start | bytes 1105928 | tf_op jit(solution)/shard_map/ppermute | solution.py:524
  46.7 10.0 %collective-permute-start.3 = (f32[3,10,24,128]{3,2,1,0:T(8,128)S(1)}, f32[3,10,24,128]{3,2,1,0:T(8,128)S(1)}, u32[]{:S(2)}, u32[]{:S(2)}) collective-permute-start(f32[3,10,24,128]{3,2,1,0:T(8,128)S(1)} %get-tuple-element.37), channel_id=1, source_target_pairs={{0,16},{16,0},{32,48},{48,32},{64,80},{80,64},{96,112},{112,96},{1... | collective-permute-start | bytes 1105928 | tf_op jit(solution)/shard_map/ppermute | solution.py:524
  83.9 8.0 %collective-permute-start.4 = (f32[3,12,8,128]{3,2,1,0:T(8,128)S(1)}, f32[3,12,8,128]{3,2,1,0:T(8,128)S(1)}, u32[]{:S(2)}, u32[]{:S(2)}) collective-permute-start(f32[3,12,8,128]{3,2,1,0:T(8,128)S(1)} %get-tuple-element.44), channel_id=1, source_target_pairs={{16,32},{32,16},{48,64},{64,48},{80,96},{96,80},{17,33},{33,17},{4... | collective-permute-start | bytes 442376 | tf_op jit(solution)/shard_map/ppermute | solution.py:524
  89.0 2.8 %collective-permute-start.5 = (f32[3,12,8,128]{3,2,1,0:T(8,128)S(1)}, f32[3,12,8,128]{3,2,1,0:T(8,128)S(1)}, u32[]{:S(2)}, u32[]{:S(2)}) collective-permute-start(f32[3,12,8,128]{3,2,1,0:T(8,128)S(1)} %get-tuple-element.45), channel_id=1, source_target_pairs={{0,16},{16,0},{32,48},{48,32},{64,80},{80,64},{96,112},{112,96},{1... | collective-permute-start | bytes 442376 | tf_op jit(solution)/shard_map/ppermute | solution.py:524

commit v9 on v8

--- a/solution.py
+++ b/solution.py
@@ -177,7 +177,7 @@
             slots[0, t, WEIGHTS + block : WEIGHTS + block + 1] = jnp.where(segment >= 128, -weight, weight)
         return carry
 
-    lax.fori_loop(0, BRICKS, brick, 0, unroll=4)
+    lax.fori_loop(0, BRICKS, brick, 0, unroll=BRICKS)
     row = rows_of((8, SEG))
     scale = jnp.broadcast_to(column_of(perm_ref, lambda block, k: k), (16, SEG))
     write_table(slots, SCALE, scale)
@@ -260,7 +260,7 @@
     vessel = solve_blocks(read_table(slots, INLET), values, slots, hots, send_ref, False)
     spot = lanes_of((16, 128)) == rows_of((16, 128))
     ends = jnp.sum(jnp.where(spot, vessel[:, SEG - 1 : SEG], 0.0), axis=0, keepdims=True)
-    ends_ref[...] = jnp.broadcast_to(ends[None], (PARTS, 8, 128))
+    ends_ref[...] = jnp.broadcast_to(ends[None], (PARTS, 1, 128))
     t = lax.axis_index("tissue")
     around_ref[0] = jnp.where(t < BRICKS - 1, region_ref[jnp.minimum(t + 1, BRICKS - 1)], 0.0)
     around_ref[1] = jnp.where(t > 0, region_ref[jnp.maximum(t - 1, 0)], 0.0)
@@ -451,7 +451,7 @@
     brick_split = split_brick(brick)
     ends = ends_ref[0, 0:1]
     for part in range(1, PARTS):
-        ends = ends + pltpu.roll(ends_ref[part], 16 * part, 1)[0:1]
+        ends = ends + pltpu.roll(ends_ref[part], 16 * part, 1)
 
     def receiver(s, carry):
         cells = [recv_ref[s, 4 * b + 3 : 4 * b + 4, :].astype(jnp.int32) for b in range(4)]
@@ -569,7 +569,7 @@
     send, ends, around = call(
         first_solve_kernel,
         "first_solve",
-        [(BRICKS, 48, 128), (PARTS, 8, 128), (2, 96, 128)],
+        [(BRICKS, 48, 128), (PARTS, 1, 128), (2, 96, 128)],
         [region, *prepared],
         values_scratch,
     )

time: 93.4 us -> 93.3 us (level)
  no operation moved by 1% of the time
where the time goes in v9:
time: 93.3 us; the launch traced here: 92.8 us
  blocking collectives  42.6 us (46%)
  starting transfers between devices  24.3 us (26%)
  Pallas kernels  16.2 us (17%)
  waiting for transfers between devices  8.97 us (10%)
    all_to_all x4, blocking collectives, exchange(): return lax.all_to_all(value, axis, 0, 0, tiled=True)  42.6 us
    ppermute x6, starting transfers between devices, swap(): lax.ppermute(value, axis, [pair for i in starts for pair in ((i, i + 1),...  16.7 us
    pallas_call x8, Pallas kernels, call(): pl.pallas_call(kernel, out_shape=[jax.ShapeDtypeStruct(out, F32) if isins...  16.2 us
    all_to_all x1, starting transfers between devices, exchange(): return lax.all_to_all(value, axis, 0, 0, tiled=True)  7.6 us
    all_to_all x1, waiting for transfers between devices, exchange(): return lax.all_to_all(value, axis, 0, 0, tiled=True)  6.24 us
    ppermute x6, waiting for transfers between devices, swap(): lax.ppermute(value, axis, [pair for i in starts for pair in ((i, i + 1),...  2.73 us
  transfers between devices with their start and end apart: 7, of which 2 were waited for; matrix products, arithmetic and copies ran while one was open for 0% of the time, Pallas kernels for 5%

profile of v9, /device:TPU:1, one launch (start us, length us, event | category | flops | bytes accessed | tf_op | source)
XLA Modules:
  0.0 92.8 jit_solution(6302096059240808121)
XLA Ops:
  0.6 1.9 %spread.1 = (f32[16,96,128]{2,1,0:T(8,128)}, f32[96,128]{1,0:T(8,128)S(1)}, f32[96,128]{1,0:T(8,128)S(1)}) custom-call(f32[96,128]{1,0:T(8,128)} %bitcast.2, f32[96,128]{1,0:T(8,128)} %bitcast.3), custom_call_target="tpu_custom_call" | custom-call | tf_op jit(solution)/shard_map/spread/pallas_call | solution.py:496
  2.5 7.6 %all-to-all-start = ((f32[16,96,128]{2,1,0:T(8,128)}), f32[16,96,128]{2,1,0:T(8,128)S(1)}, u32[]{:S(2)}, u32[]{:S(2)}) async-start(f32[16,96,128]{2,1,0:T(8,128)} %get-tuple-element.26), calls=%async_computation | async-start | bytes 1572864 | tf_op jit(solution)/shard_map/all_to_all | solution.py:520
  10.1 0.7 collective-permute-start.1
  10.8 3.9 %collective-permute-start = (f32[96,128]{1,0:T(8,128)S(1)}, f32[96,128]{1,0:T(8,128)S(1)}, u32[]{:S(2)}, u32[]{:S(2)}) collective-permute-start(f32[96,128]{1,0:T(8,128)S(1)} %get-tuple-element.30.rate_ref), channel_id=1, source_target_pairs={{0,1},{1,0},{2,3},{3,2},{4,5},{5,4},{6,7},{7,6},{8,9},{9,8},{10,11... | collective-permute-start | bytes 147464 | tf_op jit(solution)/shard_map/ppermute | solution.py:524
  14.6 2.4 %prepare.1 = (f32[5,16,8,128]{3,2,1,0:T(8,128)S(1)}, bf16[4,16,128,128]{3,2,1,0:T(8,128)(2,1)S(1)}) custom-call(s32[4,16,128]{2,1,0:T(8,128)} %refs_0_.1, f32[4,16,128]{2,1,0:T(8,128)} %refs_1_.1, s32[4,16,128]{2,1,0:T(8,128)} %refs_2_.1, f32[4,256]{1,0:T(4,128)} %refs_3_.1, s32[4,16]{1,0:T(4,128)} %refs_4_.1, f32[3]{0:T(128)} %refs_5_.1, f32[3,4]{1,0:T(4,128)} %refs_6_.1), custom_call_target="tpu_custom_call" | custom-call | tf_op jit(solution)/shard_map/prepare/pallas_call | solution.py:496
  17.0 6.2 %all-to-all-done.region_ref = f32[16,96,128]{2,1,0:T(8,128)S(1)} async-done(((f32[16,96,128]{2,1,0:T(8,128)}), f32[16,96,128]{2,1,0:T(8,128)S(1)}, u32[]{:S(2)}, u32[]{:S(2)}) %all-to-all-start) | async-done | bytes 786464 | tf_op jit(solution)/shard_map/all_to_all | solution.py:520
  23.3 2.1 %first_solve.1 = (f32[16,48,128]{2,1,0:T(8,128)S(1)}, f32[8,1,128]{2,1,0:T(1,128)S(1)}, f32[2,96,128]{2,1,0:T(8,128)S(1)}) custom-call(f32[16,96,128]{2,1,0:T(8,128)S(1)} %all-to-all-done.region_ref, f32[5,16,8,128]{3,2,1,0:T(8,128)S(1)} %get-tuple-element.27.slots, bf16[4,16,128,128]{3,2,1,0:T(8,128)(2,1)S(1)} %get-tuple-element.28.hots), custom_call_target="tpu_custom_call" | custom-call | tf_op jit(solution)/shard_map/first_solve/pallas_call | solution.py:496
  25.4 0.0 copy-start
  25.4 0.0 collective-permute-done.1.rate_far_ref
  25.4 0.0 collective-permute-done.rate_near_ref
  25.5 11.8 %all_to_all.25.recv_ref = f32[16,48,128]{2,1,0:T(8,128)S(1)} all-to-all(f32[16,48,128]{2,1,0:T(8,128)S(1)} %get-tuple-element.31), channel_id=1, replica_groups=mesh['vessel'=8,'tissue'=16] {'tissue'}, dimensions={0} | all-to-all | bytes 786432 | tf_op jit(solution)/shard_map/all_to_all | solution.py:520
  37.3 2.6 %first_scatter.1 = (f32[3,10,24,128]{3,2,1,0:T(8,128)S(1)}, f32[3,10,24,128]{3,2,1,0:T(8,128)S(1)}, f32[3,96,128]{2,1,0:T(8,128)S(1)}) custom-call(f32[16,48,128]{2,1,0:T(8,128)S(1)} %all_to_all.25.recv_ref, f32[96,128]{1,0:T(8,128)S(1)} %get-tuple-element.32.tissue_ref, f32[2,96,128]{2,1,0:T(8,128)S(1)} %get-tuple-element.33.around_ref, ...), custom_call_target="tpu_custom_call" | custom-call | tf_op jit(solution)/shard_map/first_scatter/pallas_call | solution.py:496
  39.9 6.8 %collective-permute-start.2 = (f32[3,10,24,128]{3,2,1,0:T(8,128)S(1)}, f32[3,10,24,128]{3,2,1,0:T(8,128)S(1)}, u32[]{:S(2)}, u32[]{:S(2)}) collective-permute-start(f32[3,10,24,128]{3,2,1,0:T(8,128)S(1)} %get-tuple-element.36), channel_id=1, source_target_pairs={{16,32},{32,16},{48,64},{64,48},{80,96},{96,80},{17,33},{33,17},{4... | collective-permute-start | bytes 1105928 | tf_op jit(solution)/shard_map/ppermute | solution.py:524
  46.7 0.1 collective-permute-start.3
  46.8 9.7 %all_to_all.26.ends_ref = f32[8,1,128]{2,1,0:T(1,128)S(1)} all-to-all(f32[8,1,128]{2,1,0:T(1,128)S(1)} %get-tuple-element.39), channel_id=1, replica_groups=mesh['vessel'=8,'tissue'=16] {'vessel'}, dimensions={0} | all-to-all | bytes 8192 | tf_op jit(solution)/shard_map/all_to_all | solution.py:520
  56.5 0.0 collective-permute-done.2.far
  56.6 0.0 collective-permute-done.3.near
  56.6 1.6 %first_sweeps.1 = (f32[96,128]{1,0:T(8,128)S(1)}, f32[96,128]{1,0:T(8,128)S(1)}, f32[3,12,16,128]{3,2,1,0:T(8,128)S(1)}, f32[12,16,128]{2,1,0:T(8,128)S(1)}, f32[16,16,128]{2,1,0:T(8,128)S(1)}) custom-call(f32[3,10,24,128]{3,2,1,0:T(8,128)S(1)} %collective-permute-done.2.far, f32[3,10,24,128]{3,2,1,0:T(8,128)S(1)} %collective-permute-done.3.near, ...), custom_call_target="tpu_custom_call" | custom-call | tf_op jit(solution)/shard_map/first_sweeps/pallas_call | solution.py:496
  58.1 9.5 %all_to_all.27.values_ref = f32[16,16,128]{2,1,0:T(8,128)S(1)} all-to-all(f32[16,16,128]{2,1,0:T(8,128)S(1)} %get-tuple-element.40), channel_id=1, replica_groups=mesh['vessel'=8,'tissue'=16] {'tissue'}, dimensions={0} | all-to-all | bytes 262144 | tf_op jit(solution)/shard_map/all_to_all | solution.py:520
  67.6 0.0 copy-done
  67.6 2.4 %second_solve.1 = (f32[16,48,128]{2,1,0:T(8,128)S(1)}, f32[3,4,256]{2,1,0:T(4,128)}) custom-call(s32[4]{0:T(128)S(1)} %copy-done, f32[16,16,128]{2,1,0:T(8,128)S(1)} %all_to_all.27.values_ref, f32[5,16,8,128]{3,2,1,0:T(8,128)S(1)} %get-tuple-element.27.slots, bf16[4,16,128,128]{3,2,1,0:T(8,128)(2,1)S(1)} %get-tuple-element.28.hots), custom_call_target="tpu_custom_call" | custom-call | tf_op jit(solution)/shard_map/second_solve/pallas_call | solution.py:496
  70.0 11.5 %all_to_all.28.recv_ref = f32[16,48,128]{2,1,0:T(8,128)S(1)} all-to-all(f32[16,48,128]{2,1,0:T(8,128)S(1)} %get-tuple-element.41), channel_id=1, replica_groups=mesh['vessel'=8,'tissue'=16] {'tissue'}, dimensions={0} | all-to-all | bytes 786432 | tf_op jit(solution)/shard_map/all_to_all | solution.py:520
  81.5 2.2 %second_scatter.1 = (f32[3,12,8,128]{3,2,1,0:T(8,128)S(1)}, f32[3,12,8,128]{3,2,1,0:T(8,128)S(1)}, f32[2,96,128]{2,1,0:T(8,128)S(1)}) custom-call(f32[16,48,128]{2,1,0:T(8,128)S(1)} %all_to_all.28.recv_ref, f32[96,128]{1,0:T(8,128)S(1)} %get-tuple-element.42.tissue_ref, f32[96,128]{1,0:T(8,128)S(1)} %get-tuple-element.43.side_ref), custom_call_target="tpu_custom_call" | custom-call | tf_op jit(solution)/shard_map/second_scatter/pallas_call | solution.py:496
  83.7 5.1 %collective-permute-start.4 = (f32[3,12,8,128]{3,2,1,0:T(8,128)S(1)}, f32[3,12,8,128]{3,2,1,0:T(8,128)S(1)}, u32[]{:S(2)}, u32[]{:S(2)}) collective-permute-start(f32[3,12,8,128]{3,2,1,0:T(8,128)S(1)} %get-tuple-element.44), channel_id=1, source_target_pairs={{16,32},{32,16},{48,64},{64,48},{80,96},{96,80},{17,33},{33,17},{4... | collective-permute-start | bytes 442376 | tf_op jit(solution)/shard_map/ppermute | solution.py:524
  88.9 0.1 collective-permute-start.5
  89.0 2.7 %collective-permute-done.4.far = f32[3,12,8,128]{3,2,1,0:T(8,128)S(1)} collective-permute-done((f32[3,12,8,128]{3,2,1,0:T(8,128)S(1)}, f32[3,12,8,128]{3,2,1,0:T(8,128)S(1)}, u32[]{:S(2)}, u32[]{:S(2)}) %collective-permute-start.4) | collective-permute-done | bytes 147488 | tf_op jit(solution)/shard_map/ppermute | solution.py:524
  91.7 0.0 collective-permute-done.5.near
  91.7 1.1 %second_sweeps.1 = f32[3,4,8,128]{3,2,1,0:T(8,128)} custom-call(f32[3,12,8,128]{3,2,1,0:T(8,128)S(1)} %collective-permute-done.4.far, f32[3,12,8,128]{3,2,1,0:T(8,128)S(1)} %collective-permute-done.5.near, f32[96,128]{1,0:T(8,128)S(1)} %get-tuple-element.42.tissue_ref, f32[96,128]{1,0:T(8,128)S(1)} %get-tuple-element.43.side_ref, ...), custom_call_target="tpu_custom_call" | custom-call | tf_op jit(solution)/shard_map/second_sweeps/pallas_call | solution.py:496
Async XLA Ops:
  2.5 20.8 %all-to-all-start = ((f32[16,96,128]{2,1,0:T(8,128)}), f32[16,96,128]{2,1,0:T(8,128)S(1)}, u32[]{:S(2)}, u32[]{:S(2)}) async-start(f32[16,96,128]{2,1,0:T(8,128)} %get-tuple-element.26), calls=%async_computation | async-start | bytes 1572864 | tf_op jit(solution)/shard_map/all_to_all | solution.py:520
  10.1 15.3 %collective-permute-start.1 = (f32[96,128]{1,0:T(8,128)S(1)}, f32[96,128]{1,0:T(8,128)S(1)}, u32[]{:S(2)}, u32[]{:S(2)}) collective-permute-start(f32[96,128]{1,0:T(8,128)S(1)} %get-tuple-element.30.rate_ref), channel_id=1, source_target_pairs={{1,2},{2,1},{3,4},{4,3},{5,6},{6,5},{7,8},{8,7},{9,10},{10,9},{11,... | collective-permute-start | bytes 147464 | tf_op jit(solution)/shard_map/ppermute | solution.py:524
  10.8 14.7 %collective-permute-start = (f32[96,128]{1,0:T(8,128)S(1)}, f32[96,128]{1,0:T(8,128)S(1)}, u32[]{:S(2)}, u32[]{:S(2)}) collective-permute-start(f32[96,128]{1,0:T(8,128)S(1)} %get-tuple-element.30.rate_ref), channel_id=1, source_target_pairs={{0,1},{1,0},{2,3},{3,2},{4,5},{5,4},{6,7},{7,6},{8,9},{9,8},{10,11... | collective-permute-start | bytes 147464 | tf_op jit(solution)/shard_map/ppermute | solution.py:524
  25.4 42.2 %copy-start = (s32[4]{0:T(128)S(1)}, s32[4]{0:T(128)}, u32[]{:S(2)}) copy-start(s32[4]{0:T(128)} %upstream_ref.1) | copy-start | bytes 52
  39.9 16.6 %collective-permute-start.2 = (f32[3,10,24,128]{3,2,1,0:T(8,128)S(1)}, f32[3,10,24,128]{3,2,1,0:T(8,128)S(1)}, u32[]{:S(2)}, u32[]{:S(2)}) collective-permute-start(f32[3,10,24,128]{3,2,1,0:T(8,128)S(1)} %get-tuple-element.36), channel_id=1, source_target_pairs={{16,32},{32,16},{48,64},{64,48},{80,96},{96,80},{17,33},{33,17},{4... | collective-permute-start | bytes 1105928 | tf_op jit(solution)/shard_map/ppermute | solution.py:524
  46.7 9.8 %collective-permute-start.3 = (f32[3,10,24,128]{3,2,1,0:T(8,128)S(1)}, f32[3,10,24,128]{3,2,1,0:T(8,128)S(1)}, u32[]{:S(2)}, u32[]{:S(2)}) collective-permute-start(f32[3,10,24,128]{3,2,1,0:T(8,128)S(1)} %get-tuple-element.37), channel_id=1, source_target_pairs={{0,16},{16,0},{32,48},{48,32},{64,80},{80,64},{96,112},{112,96},{1... | collective-permute-start | bytes 1105928 | tf_op jit(solution)/shard_map/ppermute | solution.py:524
  83.7 8.0 %collective-permute-start.4 = (f32[3,12,8,128]{3,2,1,0:T(8,128)S(1)}, f32[3,12,8,128]{3,2,1,0:T(8,128)S(1)}, u32[]{:S(2)}, u32[]{:S(2)}) collective-permute-start(f32[3,12,8,128]{3,2,1,0:T(8,128)S(1)} %get-tuple-element.44), channel_id=1, source_target_pairs={{16,32},{32,16},{48,64},{64,48},{80,96},{96,80},{17,33},{33,17},{4... | collective-permute-start | bytes 442376 | tf_op jit(solution)/shard_map/ppermute | solution.py:524
  88.9 2.8 %collective-permute-start.5 = (f32[3,12,8,128]{3,2,1,0:T(8,128)S(1)}, f32[3,12,8,128]{3,2,1,0:T(8,128)S(1)}, u32[]{:S(2)}, u32[]{:S(2)}) collective-permute-start(f32[3,12,8,128]{3,2,1,0:T(8,128)S(1)} %get-tuple-element.45), channel_id=1, source_target_pairs={{0,16},{16,0},{32,48},{48,32},{64,80},{80,64},{96,112},{112,96},{1... | collective-permute-start | bytes 442376 | tf_op jit(solution)/shard_map/ppermute | solution.py:524
